TPU v7x, 32 devices: a whole 2x2x4 slice. The times are simulated.
32 devices in a mesh: seq: 2 (over y), fsdp: 16 (over z, x, core).
Axes of the slice: x: 2, y: 2, z: 4, core: 2. Of those that a mesh axis runs over, the one named last changes fastest.
Arguments:
- block_input: bfloat16 [16, 1024, 768], P('fsdp', 'seq'), may hold values from -6 to 6
- lead_gain: bfloat16 [768], P('fsdp'), may hold values from 0.099609375 to 1.8984375
- joint_weight: bfloat16 [768, 2304], P('fsdp'), may hold values from -0.3125 to 0.3125
- output_weight: bfloat16 [768, 768], P('fsdp'), may hold values from -0.875 to 0.875
- tail_gain: bfloat16 [768], P('fsdp'), may hold values from 0.099609375 to 1.8984375
- up_weight: bfloat16 [768, 3072], P('fsdp'), may hold values from -0.21875 to 0.21875
- down_weight: bfloat16 [3072, 768], P('fsdp'), may hold values from -0.109375 to 0.109375
- cotangent: bfloat16 [16, 1024, 768], P('fsdp', 'seq'), may hold values from -6 to 6
Outputs:
- block_output: bfloat16 [16, 1024, 768], P('fsdp', 'seq')
- input_grad: float32 [16, 1024, 768], P('fsdp', 'seq')
- lead_grad: float32 [768], P('fsdp')
- joint_grad: float32 [768, 2304], P('fsdp')
- output_grad: float32 [768, 768], P('fsdp')
- tail_grad: float32 [768], P('fsdp')
- up_grad: float32 [768, 3072], P('fsdp')
- down_grad: float32 [3072, 768], P('fsdp')
All inputs are finite; a program needn't handle non-finite values.
Results may differ from a plain program's by a relative error of at most 0.014.
The roundings to bfloat16 on the way count: a program that leaves them out, or rounds other values in their place, can miss the bound.
Values may be sent and summed in bfloat16 or wider, within the bound.
No kernel may reach another device: no remote copies, remote signals or barrier semaphores. Data moves between devices by JAX's collectives and lax.ppermute only.
A program may use at most 192 MiB of HBM per device.

v0:
```python
import functools

import jax
import jax.numpy as jnp
from jax import lax
from jax.experimental import pallas as pl
from jax.experimental.pallas import tpu as pltpu
from jax.sharding import PartitionSpec as P

HD = 64
EPS = 1e-05
PAIR = 2 * HD
BAND = 256
LOG2E = 1.4426950408889634
LIMIT = 56 << 20
F32 = jnp.float32
BF16 = jnp.bfloat16

VMEM = pl.BlockSpec(memory_space=pltpu.VMEM)
SMEM = pl.BlockSpec(memory_space=pltpu.SMEM)
ANY = pl.BlockSpec(memory_space=pl.ANY)


def dot(left, right):
    return jnp.dot(left, right, preferred_element_type=F32)


def dot_t(left, right):
    return lax.dot_general(left, right, (((1,), (1,)), ((), ())), preferred_element_type=F32)


def shaped(*dims, dtype=BF16):
    return jax.ShapeDtypeStruct(dims, dtype)


def cost(microseconds):
    return pl.CostEstimate(flops=int(microseconds * 1e7), transcendentals=0, bytes_accessed=int(microseconds * 3e4))


def waiting(kernel, fixed, after):
    def run(*refs):
        kernel(*refs[:fixed], *refs[fixed + after :])

    return run


def whole(*dims):
    return pl.BlockSpec(dims, lambda *_: (0,) * len(dims))


def column(rows, columns, pick=lambda step: step):
    return pl.BlockSpec((rows, columns), lambda *steps: (0, pick(*steps)))


def call(kernel, name, outs, meta, inputs, scratch=(), took=4, after=(), grid=(), specs=None, out_specs=None):
    return pl.pallas_call(
        waiting(kernel, 1 + len(inputs), len(after)),
        name=name,
        grid=grid,
        out_shape=outs,
        in_specs=[SMEM] + list(specs or [VMEM] * len(inputs)) + [ANY] * len(after),
        out_specs=list(out_specs or [VMEM] * len(outs)),
        scratch_shapes=list(scratch),
        compiler_params=pltpu.CompilerParams(vmem_limit_bytes=LIMIT),
        cost_estimate=cost(took),
    )(meta, *inputs, *after)


def standardize(values):
    center = values - jnp.mean(values, axis=-1, keepdims=True)
    spread = jnp.mean(center * center, axis=-1, keepdims=True)
    rstd = lax.rsqrt(spread + EPS)
    return center * rstd, rstd


def norm_back(z, rstd, g):
    return (g - jnp.mean(g, axis=-1, keepdims=True) - z * jnp.mean(g * z, axis=-1, keepdims=True)) * rstd


def half_at(index, size):
    return pl.ds(pl.multiple_of(index * size, size), size)


def rows_in_order(meta, source, target):
    size = source.shape[0] // 16
    for spot in range(16):
        rows = pl.ds(pl.multiple_of(meta[1 + spot] * size, size), size)
        target[spot * size : (spot + 1) * size, :] = source[rows, :]


def placed(meta, near, far, target):
    size = target.shape[0] // 16
    for spot in range(16):
        source = (near, far)[spot // 8]
        rows = pl.ds(pl.multiple_of(meta[17 + spot] * size, size), size)
        target[rows, :] = source[spot % 8 * size : (spot % 8 + 1) * size, :]


def first_norm(meta, own, other, z):
    half = own.shape[0]
    for source, place in ((own, meta[0]), (other, 1 - meta[0])):
        z[half_at(place, half), :] = standardize(source[...].astype(F32))[0]


def first_scale(meta, z, near, far, zb, gains, columns):
    placed(meta, near, far, columns)
    gains[...] = columns[...].T[:16, :]
    zb[...] = (z[...] * gains[0:1, :].astype(F32)).astype(BF16)


def turn(meta, zb, zt, turned):
    turned[...] = zb[...].T
    rows_in_order(meta, turned, zt)


def mix(meta, mine, other, mixed, mt, turned):
    width = mine.shape[1]
    for side, source in ((meta[0], mine), (1 - meta[0], other)):
        mixed[:, half_at(side, width)] = source[...]
    turned[...] = mixed[...].T
    rows_in_order(meta, turned, mt)


def attend(meta, zb, near, far, qkv, o_own, o_other, lse, weight, km, vt, s_sc, ot, o_all):
    length = zb.shape[0]
    half = length // 2
    placed(meta, near, far, weight)
    qkv[...] = dot(zb[...], weight[...]).astype(BF16)
    lane = lax.broadcasted_iota(jnp.int32, (1, PAIR), 1)
    keys = qkv[:, PAIR : 2 * PAIR]
    zero = jnp.zeros_like(keys)
    km[0] = jnp.where(lane < HD, keys, zero)
    km[1] = jnp.where(lane < HD, zero, keys)
    vt[...] = qkv[:, 2 * PAIR :].T
    lse[0] = jnp.zeros(lse.shape[1:], F32)
    allowed = lax.broadcasted_iota(jnp.int32, (BAND, BAND), 0) <= lax.broadcasted_iota(jnp.int32, (BAND, BAND), 1)

    def q_step(q_band, _):
        spots = half_at(q_band, BAND)
        queries = qkv[spots, :PAIR]

        def score(k_band, tops, diagonal):
            rows = half_at(k_band, BAND)
            peaks = []
            for head in range(2):
                s = dot_t(km[head, rows, :], queries) * (HD ** -0.5 * LOG2E)
                if diagonal:
                    s = jnp.where(allowed, s, 0.0)
                s_sc[head, rows, :] = s
                peaks.append(jnp.maximum(tops[head], jnp.max(jnp.abs(s), axis=0, keepdims=True)))
            return tuple(peaks)

        def weigh(k_band, carry, tops, diagonal):
            rows = half_at(k_band, BAND)
            results = []
            for head, (total, out) in enumerate(carry):
                s = s_sc[head, rows, :]
                grow = jnp.exp2(s - tops[head])
                shrink = jnp.exp2(-s - tops[head])
                both = grow + shrink
                if diagonal:
                    both = jnp.where(allowed, both, 0.0)
                part = dot(vt[head * HD : (head + 1) * HD, rows], (grow - shrink).astype(BF16))
                results.append((total + jnp.sum(both, axis=0, keepdims=True), out + part))
            return tuple(results)

        none = jnp.zeros((1, BAND), F32)
        tops = score(q_band, (none, none), True)
        tops = lax.fori_loop(0, q_band, lambda k_band, tops: score(k_band, tops, False), tops)
        start = (none, jnp.zeros((HD, BAND), F32))
        carry = weigh(q_band, (start, start), tops, True)
        carry = lax.fori_loop(0, q_band, lambda k_band, carry: weigh(k_band, carry, tops, False), carry)
        for head, (total, out) in enumerate(carry):
            ot[head * HD : (head + 1) * HD, :] = out / total
            lse[0, head : head + 1, spots] = tops[head] + jnp.log2(0.5 * total)
        o_all[spots, :] = ot[...].T.astype(BF16)
        return 0

    lax.fori_loop(0, length // BAND, q_step, 0)
    o_own[...] = o_all[half_at(meta[0], half), :]
    o_other[...] = o_all[half_at(1 - meta[0], half), :]


def attend_back(pair, meta, qkv, o_own, o_other, d_own, d_other, lse, zt, weight, *refs):
    last = pair == 2
    count = (0, 0, 6)[pair]
    extra, refs = refs[:count], refs[count:]
    keep, send, *outs = refs[: 3 + last]
    km, vm, kt, do, inner, dk, dv, dqt, dqkv, s_sc, w_sc, p_sc, ds_sc = refs[3 + last :]
    length = qkv.shape[0]
    half = length // 2
    lane = lax.broadcasted_iota(jnp.int32, (1, PAIR), 1)
    low = lane < HD
    keys = qkv[:, PAIR : 2 * PAIR]
    values = qkv[:, 2 * PAIR :]
    zero = jnp.zeros_like(keys)
    km[0] = jnp.where(low, keys, zero)
    km[1] = jnp.where(low, zero, keys)
    vm[0] = jnp.where(low, values, zero)
    vm[1] = jnp.where(low, zero, values)
    kt[...] = keys.T
    pick = (
        lax.broadcasted_iota(jnp.int32, (8, PAIR), 1) // HD == lax.broadcasted_iota(jnp.int32, (8, PAIR), 0)
    ).astype(F32)
    for o_part, d_part, place in ((o_own, d_own, meta[0]), (o_other, d_other, 1 - meta[0])):
        do[half_at(place, half), :] = d_part[...]
        product = o_part[...].astype(F32) * d_part[...].astype(F32)
        inner[:, half_at(place, half)] = lax.dot_general(
            pick, product, (((1,), (1,)), ((), ())), preferred_element_type=F32, precision=lax.Precision.HIGHEST
        )
    allowed = lax.broadcasted_iota(jnp.int32, (BAND, BAND), 0) <= lax.broadcasted_iota(jnp.int32, (BAND, BAND), 1)
    for q_band in range(length // BAND):
        spots = slice(q_band * BAND, (q_band + 1) * BAND)
        end = (q_band + 1) * BAND
        queries = qkv[spots, :PAIR]
        upstream = do[spots, :]
        small = jnp.zeros_like(queries)
        for head in range(2):
            mine = slice(head * HD, (head + 1) * HD)
            q_mine = jnp.where(low, queries, small) if head == 0 else jnp.where(low, small, queries)
            d_mine = jnp.where(low, upstream, small) if head == 0 else jnp.where(low, small, upstream)
            base = lse[0, head : head + 1, spots] + 1.0
            mean = inner[head : head + 1, spots]
            s_sc[head, :end, :] = dot_t(km[head, :end, :], queries)
            w_sc[head, :end, :] = dot_t(vm[head, :end, :], upstream)
            for k_band in range(q_band + 1):
                rows = slice(k_band * BAND, (k_band + 1) * BAND)
                s = s_sc[head, rows, :] * (HD ** -0.5 * LOG2E)
                dw = w_sc[head, rows, :]
                if k_band == q_band:
                    s = jnp.where(allowed, s, 0.0)
                    dw = jnp.where(allowed, dw, 0.0)
                grow = jnp.exp2(s - base)
                shrink = jnp.exp2(-s - base)
                p = grow - shrink
                p_sc[head, rows, :] = p.astype(BF16)
                ds_sc[head, rows, :] = ((grow + shrink) * dw - p * mean).astype(BF16)
            dv_part = dot(p_sc[head, :end, :], d_mine)
            dk_part = dot(ds_sc[head, :end, :], q_mine)
            dqt[mine, :] = dot(kt[mine, :end], ds_sc[head, :end, :])
            old = q_band * BAND if head == 0 else end
            if old:
                dv[:old, :] += dv_part[:old]
                dk[:old, :] += dk_part[:old]
            if head == 0:
                dv[old:end, :] = dv_part[old:]
                dk[old:end, :] = dk_part[old:]
        dqkv[spots, :PAIR] = (dqt[...].T * HD ** -0.5).astype(BF16)
    dqkv[:, PAIR : 2 * PAIR] = (dk[...] * HD ** -0.5).astype(BF16)
    dqkv[:, 2 * PAIR :] = dv[...].astype(BF16)
    middle = keep.shape[0]
    start = keep.shape[1] - 3 * PAIR
    send[:, start:] = dot(zt[middle:, :], dqkv[...]).astype(BF16)
    keep[:, start:] = dot(zt[:middle, :], dqkv[...]).astype(BF16)
    if last:
        for spot in range(2):
            columns = slice(spot * 3 * PAIR, (spot + 1) * 3 * PAIR)
            keep[:, columns] = extra[3 * spot][...]
            send[:, columns] = extra[3 * spot + 1][...]
        for side, target in zip((1 - meta[0], meta[0]), outs):
            rows = half_at(side, half)
            part = dot_t(dqkv[rows, :], weight[:, 6 * PAIR :])
            for spot in range(2):
                columns = slice(spot * 3 * PAIR, (spot + 1) * 3 * PAIR)
                part += dot_t(extra[3 * spot + 2][rows, :], weight[:, columns])
            target[...] = part.astype(target.dtype)
    else:
        outs[0][...] = dqkv[...]


def added(step, total, first, part):
    @pl.when(step == 0)
    def _():
        total[...] = part if first is None else first[...] + part

    @pl.when(step > 0)
    def _():
        total[...] += part


def feed(
    meta, own, mixed, gains, weight, up, down, upstream,
    out, first, up_keep, up_send, down_keep, down_send, dresid, db, away, mine_out,
    resid, zb, zt_natural, zt, total, g_total, active, dpre, turned, picked,
):
    step = pl.program_id(0)
    gain = gains[1:2, :].astype(F32)

    @pl.when(step == 0)
    def _():
        summed = own[...].astype(F32) + dot(mixed[...], weight[...])
        resid[...] = summed
        z = (standardize(summed)[0] * gain).astype(BF16)
        zb[...] = z
        zt_natural[...] = z.T
        rows_in_order(meta, zt_natural, zt)

    width = active.shape[1]
    root = 0.7978845608028654
    for part in range(3):
        mine = slice(part * width // 3, (part + 1) * width // 3)
        v = dot(zb[...], up[:, mine])
        slope_in = dot_t(upstream[...], down[mine, :])
        square = v * v
        t = jnp.tanh(root * v * (1.0 + 0.044715 * square))
        cdf = 0.5 * (1.0 + t)
        active[:, mine] = (v * cdf).astype(BF16)
        slope = cdf + v * (0.5 * root) * (1.0 - t * t) * (1.0 + 0.134145 * square)
        dpre[:, mine] = (slope_in * slope).astype(BF16)
        turned[mine, :] = active[:, mine].T
    added(step, total, resid, dot(active[...], down[...]))
    added(step, g_total, None, dot_t(dpre[...], up[...]))

    @pl.when(step < 2)
    def _():
        first[:, :width] = dot(zt_natural[...], dpre[...]).astype(BF16)
        first[:, width:] = dot(turned[...], upstream[...]).astype(BF16)

    @pl.when(step >= 2)
    def _():
        rows_in_order(meta, turned, picked)
        size = width // 2
        for spot, (up_part, down_part) in enumerate(((up_keep, down_keep), (up_send, down_send))):
            mine = slice(spot * size, (spot + 1) * size)
            up_part[...] = dot(zt[mine, :], dpre[...]).astype(BF16)
            down_part[...] = dot(picked[mine, :], upstream[...]).astype(BF16)

    @pl.when(step == pl.num_programs(0) - 1)
    def _():
        z, rstd = standardize(resid[...])
        grad = upstream[...].astype(F32) + norm_back(z, rstd, g_total[...] * gain)
        low = grad.astype(BF16)
        for side, target in ((1 - meta[0], away), (meta[0], mine_out)):
            target[...] = dot_t(low, weight[half_at(side, 3 * PAIR), :]).astype(BF16)
        dresid[...] = grad
        db[...] = low
        out[...] = total[...].astype(out.dtype)


def output_back(meta, mt, db, keep, send):
    middle = keep.shape[0]
    send[...] = dot(mt[middle:, :], db[...]).astype(BF16)
    keep[...] = dot(mt[:middle, :], db[...]).astype(BF16)


def input_back(meta, own, mine, other, dresid, gains, out):
    z, rstd = standardize(own[...].astype(F32))
    g = (mine[...] + other[...].astype(F32)) * gains[0:1, :].astype(F32)
    out[...] = dresid[...] + norm_back(z, rstd, g)


def row_sums(values):
    ones = jnp.ones((8, values.shape[1]), F32)
    sums = lax.dot_general(
        ones, values, (((1,), (1,)), ((), ())), preferred_element_type=F32, precision=lax.Precision.HIGHEST
    )
    return sums[0:1, :]


def joint_out(meta, own, other, weight, gain, grad, gain_grad):
    for side, source in ((meta[0], own), (1 - meta[0], other)):
        for pair in range(3):
            for kind in range(3):
                columns = pl.ds(pl.multiple_of((kind * 6 + side * 3 + pair) * PAIR, PAIR), PAIR)
                at = (pair * 3 + kind) * PAIR
                grad[:, columns] = source[:, at : at + PAIR].astype(F32)
    gain_grad[...] = row_sums(grad[...] * weight[...].astype(F32)) / gain[...].astype(F32)


def feed_out(split, meta, first, first_too, last, last_too, weight, gain, up, down, output, gain_grad):
    rows, dim = output.shape
    output[...] = last[:, -dim:].astype(F32) + last_too[:, -dim:].astype(F32)
    for k in range(4):
        parts = []
        for kind in range(2):
            if k < 2 or not split:
                one, two = (first, first_too) if k < 2 else (last, last_too)
                at = ((2 * k + kind) if k < 2 else (2 * kind + k - 2)) * dim
                parts.append(one[:, at : at + dim].astype(F32) + two[:, at : at + dim].astype(F32))
            else:
                at = kind * dim
                parts.append(jnp.where(meta[0] == k - 2, last[:, at : at + dim], last_too[:, at : at + dim]).astype(F32))
        for owner in range(dim // rows):
            up[:, (4 * owner + k) * rows : (4 * owner + k + 1) * rows] = parts[0][:, owner * rows : (owner + 1) * rows]
        down[k * rows : (k + 1) * rows, :] = parts[1]
    gain_grad[...] = row_sums(up[...] * weight[...].astype(F32)) / gain[...].astype(F32)


SWAP = [(0, 1), (1, 0)]


def flipped(array, parts, bit):
    return lax.ppermute(array, "fsdp", [(spot, spot ^ bit) for spot in range(parts)])


def exchanged(blocks, parts):
    groups = [list(range(side, parts, 4)) for side in range(4)]
    return lax.all_to_all(blocks, "fsdp", 0, 0, axis_index_groups=groups, tiled=True)


def rounded_sum(terms):
    total = terms[0].astype(F32)
    for term in terms[1:]:
        total = total + term.astype(F32)
    return total.astype(BF16)


def pinned(array, mark):
    return lax.optimization_barrier((array, mark))[0]


class Reduction:
    def __init__(self, terms, parts, place):
        self.terms, self.parts, self.place = terms, parts, place

    def go(self, step):
        if step == "seq":
            width = self.terms[0].shape[3] // 2
            away = rounded_sum(
                [lax.dynamic_slice_in_dim(term, (1 - self.place) * width, width, 3) for term in self.terms]
            )
            self.terms = [lax.dynamic_slice_in_dim(term, self.place * width, width, 3) for term in self.terms]
            self.came = lax.ppermute(away, "seq", SWAP)
        else:
            away = rounded_sum([term[:, 1:] for term in self.terms])
            self.terms = [term[:, :1] for term in self.terms]
            self.came = flipped(away, self.parts, 2)
        return away

    def take(self, mark):
        self.terms.append(pinned(self.came, mark))


def body(block_input, lead_gain, joint_weight, output_weight, tail_gain, up_weight, down_weight, cotangent):
    rows, triple = joint_weight.shape
    dim = block_input.shape[2]
    wide = up_weight.shape[1]
    half = block_input.shape[1]
    length = 2 * half
    parts = dim // rows
    group = triple // 6
    chunk = dim // 2
    place = lax.axis_index("seq")
    me = lax.axis_index("fsdp")
    direct = parts == 16
    base = me if direct else jnp.zeros_like(me)
    spots = jnp.arange(16, dtype=jnp.int32)
    few = jnp.arange(8, dtype=jnp.int32)
    eight = (few % 2) * 8 + (few // 2 % 2) * 4 + few // 4 * 2
    meta = jnp.concatenate(
        [
            place[None],
            spots % 8 // 2 * 4 + ((base % 4) ^ (spots % 2 * 2 + spots // 8)),
            base ^ jnp.concatenate([eight, eight ^ 1]) if direct else spots,
        ]
    ).astype(jnp.int32)

    joint_own = lax.dynamic_index_in_dim(joint_weight.reshape(rows, 3, 2, group), place, 2, keepdims=False)
    joint_own = joint_own.reshape(rows, 3, 3, PAIR).transpose(0, 2, 1, 3).reshape(rows, 3 * group)
    up_turned = up_weight.reshape(rows, parts, 4, rows).transpose(2, 0, 1, 3).reshape(4, rows, dim)
    down_turned = down_weight.reshape(4, rows, dim)
    hidden = [part[k] for k in range(4) for part in (up_turned, down_turned)]

    own = block_input[0]
    upstream = cotangent[0]
    rest = lax.all_gather(jnp.concatenate([output_weight, *hidden], axis=1), "fsdp", axis=0, tiled=True)
    other = lax.ppermute(own, "seq", SWAP)
    both_gains = jnp.pad(jnp.stack([lead_gain, tail_gain], axis=1), ((0, 0), (0, PAIR - 2)))
    first = jnp.concatenate([joint_own, both_gains], axis=1)
    if direct:
        for bit in (8, 4, 2):
            if bit == 2:
                first, other = lax.optimization_barrier((first, other))
            first = jnp.concatenate([first, flipped(first, parts, bit)], axis=0)
        firsts = (first, flipped(first, parts, 1))
    else:
        first = lax.all_gather(first, "fsdp", axis=0, tiled=True)
        firsts = (first[:chunk], first[chunk:])

    (z_one,) = call(first_norm, "first_norm", (shaped(length, dim, dtype=F32),), meta, (own, other), took=3)
    zb, gains = call(
        first_scale,
        "first_scale",
        (shaped(length, dim), shaped(16, dim)),
        meta,
        (z_one, *firsts),
        [pltpu.VMEM((dim, PAIR), BF16)],
        took=2,
        grid=(1,),
        specs=[VMEM] + [column(chunk, PAIR, lambda step: 9)] * 2,
    )
    triples = column(length, 3 * PAIR)
    pair_tokens = column(half, PAIR)
    lse_spec = pl.BlockSpec((1, 8, length), lambda step: (step, 0, 0))
    qkv, o_own, o_other, lse, weight = call(
        attend,
        "attend",
        (
            shaped(length, 9 * PAIR),
            shaped(half, group),
            shaped(half, group),
            shaped(3, 8, length, dtype=F32),
            shaped(dim, 9 * PAIR),
        ),
        meta,
        (zb, *firsts),
        [
            pltpu.VMEM((2, length, PAIR), BF16),
            pltpu.VMEM((PAIR, length), BF16),
            pltpu.VMEM((2, length, BAND), F32),
            pltpu.VMEM((PAIR, BAND), F32),
            pltpu.VMEM((length, PAIR), BF16),
        ],
        took=22,
        grid=(3,),
        specs=[whole(length, dim)] + [column(chunk, 3 * PAIR)] * 2,
        out_specs=[triples, pair_tokens, pair_tokens, lse_spec, column(dim, 3 * PAIR)],
    )
    o_came = lax.ppermute(o_other, "seq", SWAP)
    store = [pltpu.VMEM((dim, length), BF16)]
    (zt,) = call(turn, "turn", (shaped(dim, length),), meta, (zb,), store, took=2, after=[lse])
    mixed, mixed_t = call(
        mix,
        "mix",
        (shaped(half, dim), shaped(dim, half)),
        meta,
        (o_own, o_came),
        [pltpu.VMEM((dim, half), BF16)],
        took=2,
        after=[zt],
    )
    rest_block = column(dim, dim, lambda step: 0)
    total_f32 = shaped(half, dim, dtype=F32)
    tokens = whole(half, dim)

    later = column(chunk, dim, lambda k: jnp.maximum(k - 2, 0))
    out, grad_first, up_keep, up_send, down_keep, down_send, dresid, db, dm_away, dm_mine = call(
        feed,
        "feed",
        (shaped(half, dim), shaped(dim, 4 * dim))
        + (shaped(chunk, 2 * dim),) * 4
        + (total_f32, shaped(half, dim), shaped(half, group), shaped(half, group)),
        meta,
        (own, mixed, gains, rest, rest, rest, upstream),
        [
            pltpu.VMEM((half, dim), F32),
            pltpu.VMEM((half, dim), BF16),
            pltpu.VMEM((dim, half), BF16),
            pltpu.VMEM((dim, half), BF16),
            pltpu.VMEM((half, dim), F32),
            pltpu.VMEM((half, dim), F32),
            pltpu.VMEM((half, dim), BF16),
            pltpu.VMEM((half, dim), BF16),
            pltpu.VMEM((dim, half), BF16),
            pltpu.VMEM((dim, half), BF16),
        ],
        took=36,
        grid=(4,),
        specs=[
            tokens,
            tokens,
            whole(16, dim),
            rest_block,
            column(dim, dim, lambda k: 1 + 2 * k),
            column(dim, dim, lambda k: 2 + 2 * k),
            tokens,
        ],
        out_specs=[tokens, column(dim, 2 * dim, lambda k: jnp.minimum(k, 1))]
        + [later] * 4
        + [tokens, tokens, whole(half, group), whole(half, group)],
    )

    if direct:
        first_sum = lax.psum_scatter(grad_first, "fsdp", scatter_dimension=0, tiled=True)
        up_came = flipped(up_send, parts, 1)
        down_came = flipped(down_send, parts, 1)

    def blocks_of(part):
        return part.reshape(4, 2, rows, -1)

    dm_came = lax.ppermute(dm_away, "seq", SWAP)
    mixed_keep, mixed_send = call(output_back, "output_back", (shaped(chunk, dim),) * 2, meta, (mixed_t, db))
    dm_came = pinned(dm_came, mixed_keep)
    marks = [[mixed_keep], [], []]
    if direct:
        mixed_came = flipped(mixed_send, parts, 1)
        up_red = Reduction([blocks_of(part) for part in (up_keep, pinned(up_came, db))], parts, place)
        marks[0].append(up_red.go(2))
        down_red = Reduction([blocks_of(part) for part in (down_keep, pinned(down_came, dm_came))], parts, place)
        marks[0].append(down_red.go("seq"))
        mixed_red = Reduction([blocks_of(part) for part in (mixed_keep, pinned(mixed_came, dm_came))], parts, place)
        marks[0].append(mixed_red.go(2))
        marks[0].append(up_red.came)

    def attend_back_call(pair, outs, out_specs, extra, after):
        width = (9 if pair == 2 else 3) * PAIR
        pick = lambda step: pair
        return call(
            functools.partial(attend_back, pair),
            "attend_back",
            (shaped(chunk, width), shaped(chunk, width)) + outs,
            meta,
            (qkv, o_own, o_other, dm_mine, dm_came, lse, zt, weight, *extra),
            [
                pltpu.VMEM((2, length, PAIR), BF16),
                pltpu.VMEM((2, length, PAIR), BF16),
                pltpu.VMEM((PAIR, length), BF16),
                pltpu.VMEM((length, PAIR), BF16),
                pltpu.VMEM((8, length), F32),
                pltpu.VMEM((length, PAIR), F32),
                pltpu.VMEM((length, PAIR), F32),
                pltpu.VMEM((PAIR, BAND), F32),
                pltpu.VMEM((length, 3 * PAIR), BF16),
                pltpu.VMEM((2, length, BAND), F32),
                pltpu.VMEM((2, length, BAND), F32),
                pltpu.VMEM((2, length, BAND), BF16),
                pltpu.VMEM((2, length, BAND), BF16),
            ],
            took=10,
            after=after,
            grid=(1,),
            specs=[column(length, 3 * PAIR, pick)]
            + [column(half, PAIR, pick)] * 4
            + [
                pl.BlockSpec((1, 8, length), lambda step: (pair, 0, 0)),
                whole(dim, length),
                whole(dim, 9 * PAIR) if pair == 2 else column(dim, 3 * PAIR, pick),
            ]
            + [whole(*part.shape) for part in extra],
            out_specs=[whole(chunk, width)] * 2 + out_specs,
        )

    one = (shaped(length, 3 * PAIR),)
    keep_0, send_0, token_0 = attend_back_call(0, one, [whole(length, 3 * PAIR)], (), marks[0])
    if direct:
        up_red.take(token_0)
        down_red.take(token_0)
        marks[1] = [up_red.go("seq"), down_red.go(2)]
    keep_1, send_1, token_1 = attend_back_call(1, one, [whole(length, 3 * PAIR)], (), marks[1] + [token_0])
    if direct:
        last_sum = []
        for red in (up_red, down_red, mixed_red):
            red.take(token_1)
            last_sum.append(rounded_sum(red.terms))
        last_sum = jnp.concatenate(last_sum, axis=-1).reshape(4, rows, -1)
        deep = me // 4
        last_parts = [lax.dynamic_index_in_dim(last_sum, deep, 0, keepdims=False)]
        for far in (1, 2, 3):
            away = lax.dynamic_index_in_dim(last_sum, deep ^ far, 0, keepdims=False)
            marks[2].append(away)
            last_parts.append(flipped(away, parts, 4 * far))
    joint_keep, joint_send, sent, own_part = attend_back_call(
        2,
        (shaped(half, dim), total_f32),
        [tokens] * 2,
        (keep_0, send_0, token_0, keep_1, send_1, token_1),
        marks[2],
    )
    other_part = lax.ppermute(sent, "seq", SWAP)
    marks = []
    marks = []
    if direct:
        joint_came = flipped(joint_send, parts, 1)
        joint_red = Reduction([blocks_of(part) for part in (joint_keep, joint_came)], parts, place)
        joint_red.go(2)
        joint_red.take(joint_keep)
        joint_sum = rounded_sum(joint_red.terms).reshape(4, rows, -1)
        marks = [first_sum, joint_sum]
        joint_sum = exchanged(joint_sum, parts)
    (input_grad,) = call(
        input_back, "input_back", (total_f32,), meta, (own, own_part, other_part, dresid, gains), after=marks
    )

    if direct:
        last_sum = rounded_sum(last_parts)
        joint_sum = jnp.sum(pinned(joint_sum, input_grad).astype(F32), axis=0).astype(BF16)
    else:

        def scattered(keep, send):
            blocks = jnp.stack([keep, send]).reshape(2, 4, 2, dim // 16, -1).transpose(1, 2, 0, 3, 4).reshape(dim, -1)
            return lax.psum_scatter(blocks, "fsdp", scatter_dimension=0, tiled=True)

        first_sum = lax.psum_scatter(grad_first, "fsdp", scatter_dimension=0, tiled=True)
        last_sum = ((up_keep, up_send), (down_keep, down_send), (mixed_keep, mixed_send))
        last_sum = jnp.concatenate([scattered(*pair) for pair in last_sum], axis=1)
        joint_sum = scattered(joint_keep, joint_send)
    first_sum, last_sum, joint_sum = ((part, lax.ppermute(part, "seq", SWAP)) for part in (first_sum, last_sum, joint_sum))
    up_grad, down_grad, output_grad, tail_grad = call(
        functools.partial(feed_out, direct),
        "feed_out",
        (
            shaped(rows, wide, dtype=F32),
            shaped(4 * rows, dim, dtype=F32),
            shaped(rows, dim, dtype=F32),
            shaped(1, rows, dtype=F32),
        ),
        meta,
        (*first_sum, *last_sum, up_weight, tail_gain[None, :]),
    )
    joint_grad, lead_grad = call(
        joint_out,
        "joint_out",
        (shaped(rows, triple, dtype=F32), shaped(1, rows, dtype=F32)),
        meta,
        (*joint_sum, joint_weight, lead_gain[None, :]),
        took=2,
        after=[up_grad],
    )
    return (
        out[None],
        input_grad[None],
        lead_grad[0],
        joint_grad,
        output_grad,
        tail_grad[0],
        up_grad,
        down_grad,
    )


def solution(mesh):
    split = P("fsdp", "seq", None)
    placed = (split, P("fsdp"), P("fsdp", None), P("fsdp", None), P("fsdp"), P("fsdp", None), P("fsdp", None), split)
    return jax.shard_map(
        body,
        mesh=mesh,
        in_specs=placed,
        out_specs=(split, split, P("fsdp"), P("fsdp", None), P("fsdp", None), P("fsdp"), P("fsdp", None), P("fsdp", None)),
        check_vma=False,
    )
```

profile of v0, /device:TPU:0, one launch (start us, length us, event | category | flops | bytes accessed | tf_op | source)
XLA Modules:
  0.0 261.7 jit_solution(12437489037019216449)
XLA Ops:
  7.2 1.7 reshape.88
  12.5 4.1 %collective-permute-start = (bf16[48,1280]{1,0:T(8,128)(2,1)S(1)}, bf16[48,1280]{1,0:T(8,128)(2,1)S(1)}, u32[]{:S(2)}, u32[]{:S(2)}) collective-permute-start(bf16[48,1280]{1,0:T(8,128)(2,1)S(1)} %pad_maximum_fusion.3), channel_id=1, source_target_pairs={{0,8},{1,9},{2,10},{3,11},{4,12},{5,13},{6,14},{7,15},{8,0},{9,1},... | collective-permute-start | bytes 368648 | tf_op jit(solution)/shard_map/ppermute | solution.py:393
  16.6 1.5 collective-permute-start.2
  18.1 4.4 %collective-permute-done = bf16[48,1280]{1,0:T(8,128)(2,1)S(1)} collective-permute-done((bf16[48,1280]{1,0:T(8,128)(2,1)S(1)}, bf16[48,1280]{1,0:T(8,128)(2,1)S(1)}, u32[]{:S(2)}, u32[]{:S(2)}) %collective-permute-start) | collective-permute-done | bytes 122912 | tf_op jit(solution)/shard_map/ppermute | solution.py:393
  23.3 17.1 %collective-permute-done.1 = bf16[96,1280]{1,0:T(8,128)(2,1)S(1)} collective-permute-done((bf16[96,1280]{1,0:T(8,128)(2,1)S(1)}, bf16[96,1280]{1,0:T(8,128)(2,1)S(1)}, u32[]{:S(2)}, u32[]{:S(2)}) %collective-permute-start.1) | collective-permute-done | bytes 245792 | tf_op jit(solution)/shard_map/ppermute | solution.py:393
  40.5 1.3 collective-permute-start.3
  41.8 7.6 %collective-permute-done.3 = bf16[192,1280]{1,0:T(8,128)(2,1)S(1)} collective-permute-done((bf16[192,1280]{1,0:T(8,128)(2,1)S(1)}, bf16[192,1280]{1,0:T(8,128)(2,1)S(1)}, u32[]{:S(2)}, u32[]{:S(2)}) %collective-permute-start.3) | collective-permute-done | bytes 491552 | tf_op jit(solution)/shard_map/ppermute | solution.py:393
  50.3 4.0 %first_norm.1.refs_1_ = f32[1024,768]{1,0:T(8,128)} custom-call(s32[33]{0:T(128)} %pad_add_fusion.refs_0_, bf16[512,768]{1,0:T(8,128)(2,1)} %bitcast.62, bf16[512,768]{1,0:T(8,128)(2,1)} %copy-done.22), custom_call_target="tpu_custom_call" | custom-call | flops 30000000 | bytes 90000 | tf_op jit(solution)/shard_map/first_norm/pallas_call | solution.py:56
  55.3 3.6 %first_scale.1 = (bf16[1024,768]{1,0:T(8,128)(2,1)}, bf16[16,768]{1,0:T(8,128)(2,1)}) custom-call(s32[33]{0:T(128)} %pad_add_fusion.refs_0_, f32[1024,768]{1,0:T(8,128)} %first_norm.1.refs_1_, bf16[384,1280]{1,0:T(8,128)(2,1)} %copy-done.1, bf16[384,1280]{1,0:T(8,128)(2,1)} %copy-done.2), custom_call_target="tpu_custom_call" | custom-call | flops 20000000 | bytes 60000 | tf_op jit(solution)/shard_map/first_scale/pallas_call | solution.py:56
  58.9 24.2 %attend.1 = (bf16[1024,1152]{1,0:T(8,128)(2,1)}, bf16[512,384]{1,0:T(8,128)(2,1)}, bf16[512,384]{1,0:T(8,128)(2,1)}, f32[3,8,1024]{2,1,0:T(8,128)}, bf16[768,1152]{1,0:T(8,128)(2,1)}) custom-call(s32[33]{0:T(128)} %pad_add_fusion.refs_0_, bf16[1024,768]{1,0:T(8,128)(2,1)} %get-tuple-element.60.refs_1_, bf16[384,1280]{1,0:T(8,128)(2,1)} %copy-done.1, ...), custom_call_target="tpu_custom_call" | custom-call | flops 220000000 | bytes 660000 | tf_op jit(solution)/shard_map/attend/pallas_call | solution.py:56
  83.1 1.7 collective-permute-start.5
  84.8 3.2 %turn.1.refs_3_.refs_7_ = bf16[768,1024]{1,0:T(8,128)(2,1)} custom-call(s32[33]{0:T(128)} %pad_add_fusion.refs_0_, bf16[1024,768]{1,0:T(8,128)(2,1)} %get-tuple-element.60.refs_1_, f32[3,8,1024]{2,1,0:T(8,128)} %get-tuple-element.63.refs_2_.refs_6_), custom_call_target="tpu_custom_call" | custom-call | flops 20000000 | bytes 60000 | tf_op jit(solution)/shard_map/turn/pallas_call | solution.py:56
  88.0 6.7 %collective-permute-done.5.refs_2_ = bf16[512,384]{1,0:T(8,128)(2,1)S(1)} collective-permute-done((bf16[512,384]{1,0:T(8,128)(2,1)}, bf16[512,384]{1,0:T(8,128)(2,1)S(1)}, u32[]{:S(2)}, u32[]{:S(2)}) %collective-permute-start.5) | collective-permute-done | bytes 393248 | tf_op jit(solution)/shard_map/ppermute | solution.py:519
  95.5 2.4 mix.1
  97.9 10.5 %all-gather.2.cloned.1.call-done.refs_4_.refs_5_.refs_6_ = bf16[768,6912]{1,0:T(8,128)(2,1)} async-done(((bf16[48,6912]{1,0:T(8,128)(2,1)}), bf16[768,6912]{1,0:T(8,128)(2,1)}) %all-gather.2.cloned.1.call-update) | async-done | bytes 10616848 | tf_op jit(solution)/shard_map/all_gather | solution.py:466
  108.4 30.8 %feed.1 = (bf16[512,768]{1,0:T(8,128)(2,1)}, bf16[768,3072]{1,0:T(8,128)(2,1)}, bf16[384,1536]{1,0:T(8,128)(2,1)}, bf16[384,1536]{1,0:T(8,128)(2,1)}, bf16[384,1...) custom-call(s32[33]{0:T(128)} %pad_add_fusion.refs_0_, ...), custom_call_target="tpu_custom_call" | custom-call | flops 360000000 | bytes 1080000 | tf_op jit(solution)/shard_map/feed/pallas_call | solution.py:56
  139.2 1.2 copy-done.33
  141.1 3.0 %output_back.1 = (bf16[384,768]{1,0:T(8,128)(2,1)}, bf16[384,768]{1,0:T(8,128)(2,1)}) custom-call(s32[33]{0:T(128)} %pad_add_fusion.refs_0_, bf16[768,512]{1,0:T(8,128)(2,1)} %get-tuple-element.70.refs_1_, bf16[512,768]{1,0:T(8,128)(2,1)} %get-tuple-element.71.refs_2_), custom_call_target="tpu_custom_call" | custom-call | flops 40000000 | bytes 120000 | tf_op jit(solution)/shard_map/output_back/pallas_call | solution.py:56
  144.3 1.5 collective-permute-start.6
  147.4 8.4 %collective-permute-done.6.refs_5_ = bf16[512,384]{1,0:T(8,128)(2,1)S(1)} collective-permute-done((bf16[512,384]{1,0:T(8,128)(2,1)}, bf16[512,384]{1,0:T(8,128)(2,1)S(1)}, u32[]{:S(2)}, u32[]{:S(2)}) %collective-permute-start.6) | collective-permute-done | bytes 393248 | tf_op jit(solution)/shard_map/ppermute | solution.py:581
  155.8 1.6 add_convert_fusion.refs_11_
  157.4 1.5 collective-permute-start.11
  159.0 1.2 slice.120
  162.8 8.3 %attend_back.3 = (bf16[384,384]{1,0:T(8,128)(2,1)}, bf16[384,384]{1,0:T(8,128)(2,1)}, bf16[1024,384]{1,0:T(8,128)(2,1)}) custom-call(s32[33]{0:T(128)} %pad_add_fusion.refs_0_, bf16[1024,1152]{1,0:T(8,128)(2,1)} %get-tuple-element.67.refs_1_, bf16[512,384]{1,0:T(8,128)(2,1)} %get-tuple-element.61.refs_1_.refs_2_, ...), custom_call_target="tpu_custom_call" | custom-call | flops 100000000 | bytes 300000 | tf_op jit(solution)/shard_map/attend_back/pallas_call | solution.py:56
  171.2 1.1 add_convert_fusion.8.refs_9_
  172.3 1.5 collective-permute-start.12
  173.7 1.3 add_convert_fusion.7.refs_10_
  175.7 8.6 %attend_back.4 = (bf16[384,384]{1,0:T(8,128)(2,1)}, bf16[384,384]{1,0:T(8,128)(2,1)}, bf16[1024,384]{1,0:T(8,128)(2,1)}) custom-call(s32[33]{0:T(128)} %pad_add_fusion.refs_0_, bf16[1024,1152]{1,0:T(8,128)(2,1)} %get-tuple-element.67.refs_1_, bf16[512,384]{1,0:T(8,128)(2,1)} %get-tuple-element.61.refs_1_.refs_2_, ...), custom_call_target="tpu_custom_call" | custom-call | flops 100000000 | bytes 300000 | tf_op jit(solution)/shard_map/attend_back/pallas_call | solution.py:56
  184.4 1.2 add_convert_fusion.4
  185.6 2.8 %collective-permute-done.13 = bf16[4,1,48,768]{3,2,1,0:T(8,128)(2,1)S(1)} collective-permute-done((bf16[4,1,48,768]{3,2,1,0:T(8,128)(2,1)S(1)}, bf16[4,1,48,768]{3,2,1,0:T(8,128)(2,1)S(1)}, u32[]{:S(2)}, u32[]{:S(2)}) %collective-permute-start.13) | collective-permute-done | bytes 294944 | tf_op jit(solution)/shard_map/ppermute | solution.py:393
  188.6 1.3 add_convert_fusion.5
  190.9 14.4 %attend_back.5 = (bf16[384,1152]{1,0:T(8,128)(2,1)}, bf16[384,1152]{1,0:T(8,128)(2,1)}, bf16[512,768]{1,0:T(8,128)(2,1)}, f32[512,768]{1,0:T(8,128)}) custom-call(s32[33]{0:T(128)} %pad_add_fusion.refs_0_, bf16[1024,1152]{1,0:T(8,128)(2,1)} %get-tuple-element.67.refs_1_, bf16[512,384]{1,0:T(8,128)(2,1)} %get-tuple-element.61.refs_1_.refs_2_, ...), custom_call_target="tpu_custom_call" | custom-call | flops 100000000 | bytes 300000 | tf_op jit(solution)/shard_map/attend_back/pallas_call | solution.py:56
  205.4 2.6 %collective-permute-done.16 = bf16[384,1152]{1,0:T(8,128)(2,1)S(1)} collective-permute-done((bf16[384,1152]{1,0:T(8,128)(2,1)}, bf16[384,1152]{1,0:T(8,128)(2,1)S(1)}, u32[]{:S(2)}, u32[]{:S(2)}) %collective-permute-start.16) | collective-permute-done | bytes 884768 | tf_op jit(solution)/shard_map/ppermute | solution.py:393
  208.0 1.1 add_convert_fusion.3
  209.8 1.3 collective-permute-start.20
  211.1 2.5 collective-permute-start.21
  214.2 1.4 collective-permute-start.15
  215.5 5.9 %collective-permute-done.17 = bf16[4,1,48,1152]{3,2,0,1:T(8,128)(2,1)S(1)} collective-permute-done((bf16[4,1,48,1152]{3,2,0,1:T(8,128)(2,1)S(1)}, bf16[4,1,48,1152]{3,2,0,1:T(8,128)(2,1)S(1)}, u32[]{:S(2)}, u32[]{:S(2)}) %collective-permute-start.17) | collective-permute-done | bytes 442400 | tf_op jit(solution)/shard_map/ppermute | solution.py:393
  221.4 2.0 fusion.refs_7_
  223.4 4.5 %all-to-all-start = ((bf16[4,48,1152]{2,1,0:T(8,128)(2,1)}), bf16[4,48,1152]{2,1,0:T(8,128)(2,1)S(1)}, u32[]{:S(2)}, u32[]{:S(2)}) async-start(bf16[4,48,1152]{2,1,0:T(8,128)(2,1)} %fusion.refs_7_), calls=%async_computation.1 | async-start | bytes 884736 | tf_op jit(solution)/shard_map/all_to_all | solution.py:398
  228.9 5.5 %collective-permute-done.21 = bf16[48,2304]{1,0:T(8,128)(2,1)} collective-permute-done((bf16[48,2304]{1,0:T(8,128)(2,1)S(1)}, bf16[48,2304]{1,0:T(8,128)(2,1)}, u32[]{:S(2)}, u32[]{:S(2)}) %collective-permute-start.21) | collective-permute-done | bytes 221216 | tf_op jit(solution)/shard_map/ppermute | solution.py:393
  234.5 1.2 fusion.3.refs_3_
  235.6 1.9 collective-permute-start.23
  237.6 4.5 %input_back.1 = f32[512,768]{1,0:T(8,128)} custom-call(s32[33]{0:T(128)} %pad_add_fusion.refs_0_, bf16[512,768]{1,0:T(8,128)(2,1)} %bitcast.64, f32[512,768]{1,0:T(8,128)} %get-tuple-element.94.refs_2_, bf16[512,768]{1,0:T(8,128)(2,1)} %collective-permute-done.15.refs_3_, f32[512,768]{1,0:T(8,128)} %get-tuple-element.96.refs_4_, ...), custom_call_target="tpu_custom_call" | custom-call | flops 40000000 | bytes 120000 | tf_op jit(solution)/shard_map/input_back/pallas_call | solution.py:56
  242.1 4.3 %all-to-all-done = bf16[4,48,1152]{2,1,0:T(8,128)(2,1)S(1)} async-done(((bf16[4,48,1152]{2,1,0:T(8,128)(2,1)}), bf16[4,48,1152]{2,1,0:T(8,128)(2,1)S(1)}, u32[]{:S(2)}, u32[]{:S(2)}) %all-to-all-start) | async-done | bytes 442400 | tf_op jit(solution)/shard_map/all_to_all | solution.py:398
  246.5 1.5 collective-permute-start.18
  248.8 2.9 %feed_out.1 = (f32[48,3072]{1,0:T(8,128)}, f32[192,768]{1,0:T(8,128)}, f32[48,768]{1,0:T(8,128)}, f32[1,48]{1,0:T(1,128)}) custom-call(s32[33]{0:T(128)} %pad_add_fusion.refs_0_, bf16[48,3072]{1,0:T(8,128)(2,1)} %reduce-scatter.2.cloned.1.call-done.refs_6_.refs_1_, bf16[48,3072]{1,0:T(8,128)(2,1)} %copy-done.26, bf16[48,2304]{1,0:T(8,128)(2,1)} %copy-done.20, ...), custom_call_target="tpu_custom_call" | custom-call | flops 40000000 | bytes 120000 | tf_op jit(solution)/shard_map/feed_out/pallas_call | solution.py:56
  252.4 2.1 joint_out.1
  (139 shorter events, 17.6 us)
Async XLA Ops:
  7.2 101.2 %all-gather.2.cloned.1.call-start = ((), (), s32[]{:S(2)}) async-start(), calls=%async_computation.2 | async-start | bytes 11280384 | tf_op jit(solution)/shard_map/all_gather | solution.py:466
  9.1 1.1 copy-start.25
  10.2 1.5 copy-start.19
  11.6 4.9 %copy-start = (bf16[1,512,768]{2,1,0:T(8,128)(2,1)S(1)}, bf16[1,512,768]{2,1,0:T(8,128)(2,1)}, u32[]{:S(2)}) copy-start(bf16[1,512,768]{2,1,0:T(8,128)(2,1)} %param.8) | copy-start | bytes 2359300
  11.6 216.2 %reduce-scatter.2.cloned.1.call-start = ((), (), s32[]{:S(2)}) async-start(), calls=%async_computation.3 | async-start | bytes 5013504 | tf_op jit(solution)/shard_map/reduce_scatter | solution.py:574
  12.5 10.1 %collective-permute-start = (bf16[48,1280]{1,0:T(8,128)(2,1)S(1)}, bf16[48,1280]{1,0:T(8,128)(2,1)S(1)}, u32[]{:S(2)}, u32[]{:S(2)}) collective-permute-start(bf16[48,1280]{1,0:T(8,128)(2,1)S(1)} %pad_maximum_fusion.3), channel_id=1, source_target_pairs={{0,8},{1,9},{2,10},{3,11},{4,12},{5,13},{6,14},{7,15},{8,0},{9,1},... | collective-permute-start | bytes 368648 | tf_op jit(solution)/shard_map/ppermute | solution.py:393
  16.6 23.9 %collective-permute-start.2 = (bf16[512,768]{1,0:T(8,128)(2,1)S(1)}, bf16[512,768]{1,0:T(8,128)(2,1)S(1)}, u32[]{:S(2)}, u32[]{:S(2)}) collective-permute-start(bf16[512,768]{1,0:T(8,128)(2,1)S(1)} %bitcast.65), channel_id=1, source_target_pairs={{0,16},{16,0},{1,17},{17,1},{2,18},{18,2},{3,19},{19,3},{4,20},{20... | collective-permute-start | bytes 2359304 | tf_op jit(solution)/shard_map/ppermute | solution.py:467
  22.5 17.9 %collective-permute-start.1 = (bf16[96,1280]{1,0:T(8,128)(2,1)S(1)}, bf16[96,1280]{1,0:T(8,128)(2,1)S(1)}, u32[]{:S(2)}, u32[]{:S(2)}) collective-permute-start(bf16[96,1280]{1,0:T(8,128)(2,1)S(1)} %pad_maximum_fusion.2), channel_id=1, source_target_pairs={{0,4},{1,5},{2,6},{3,7},{4,0},{5,1},{6,2},{7,3},{8,12},{9,13},{10,... | collective-permute-start | bytes 737288 | tf_op jit(solution)/shard_map/ppermute | solution.py:393
  40.5 9.8 %copy-start.22 = (bf16[512,768]{1,0:T(8,128)(2,1)}, bf16[512,768]{1,0:T(8,128)(2,1)S(1)}, u32[]{:S(2)}) copy-start(bf16[512,768]{1,0:T(8,128)(2,1)S(1)} %collective-permute-done.2.refs_2_) | copy-start | bytes 2359300
  40.5 8.9 %collective-permute-start.3 = (bf16[192,1280]{1,0:T(8,128)(2,1)S(1)}, bf16[192,1280]{1,0:T(8,128)(2,1)S(1)}, u32[]{:S(2)}, u32[]{:S(2)}) collective-permute-start(bf16[192,1280]{1,0:T(8,128)(2,1)S(1)} %pad_maximum_fusion.1), channel_id=1, source_target_pairs={{0,2},{1,3},{2,0},{3,1},{4,6},{5,7},{6,4},{7,5},{8,10},{9,11},{10,... | collective-permute-start | bytes 1474568 | tf_op jit(solution)/shard_map/ppermute | solution.py:393
  49.4 4.9 %copy-start.1 = (bf16[384,1280]{1,0:T(8,128)(2,1)}, bf16[384,1280]{1,0:T(8,128)(2,1)S(1)}, u32[]{:S(2)}) copy-start(bf16[384,1280]{1,0:T(8,128)(2,1)S(1)} %constant_dynamic-update-slice_fusion.refs_2_) | copy-start | bytes 2949124
  49.5 4.9 %collective-permute-start.4 = (bf16[384,1280]{1,0:T(8,128)(2,1)S(1)}, bf16[384,1280]{1,0:T(8,128)(2,1)S(1)}, u32[]{:S(2)}, u32[]{:S(2)}) collective-permute-start(bf16[384,1280]{1,0:T(8,128)(2,1)S(1)} %constant_dynamic-update-slice_fusion.refs_2_), channel_id=1, source_target_pairs={{0,1},{1,0},{2,3},{3,2},{4,5},{5,4},{6,7},{7,6},{8,9},{9,8},{10,11... | collective-permute-start | bytes 2949128 | tf_op jit(solution)/shard_map/ppermute | solution.py:393
  83.1 11.7 %collective-permute-start.5 = (bf16[512,384]{1,0:T(8,128)(2,1)}, bf16[512,384]{1,0:T(8,128)(2,1)S(1)}, u32[]{:S(2)}, u32[]{:S(2)}) collective-permute-start(bf16[512,384]{1,0:T(8,128)(2,1)} %get-tuple-element.62.refs_3_), channel_id=1, source_target_pairs={{0,16},{16,0},{1,17},{17,1},{2,18},{18,2},{3,19},{19,3},{4,20},{20... | collective-permute-start | bytes 1179656 | tf_op jit(solution)/shard_map/ppermute | solution.py:519
  139.2 1.3 copy-start.33
  139.2 1.6 copy-start.32
  139.2 6.6 %copy-start.13 = (bf16[384,1536]{1,0:T(8,128)(2,1)S(1)}, bf16[384,1536]{1,0:T(8,128)(2,1)}, u32[]{:S(2)}) copy-start(bf16[384,1536]{1,0:T(8,128)(2,1)} %get-tuple-element.75) | copy-start | bytes 3538948
  140.5 5.3 %collective-permute-start.7 = (bf16[384,1536]{1,0:T(8,128)(2,1)S(1)}, bf16[384,1536]{1,0:T(8,128)(2,1)S(1)}, u32[]{:S(2)}, u32[]{:S(2)}) collective-permute-start(bf16[384,1536]{1,0:T(8,128)(2,1)S(1)} %copy-done.33), channel_id=1, source_target_pairs={{0,1},{1,0},{2,3},{3,2},{4,5},{5,4},{6,7},{7,6},{8,9},{9,8},{10,11... | collective-permute-start | bytes 3538952 | tf_op jit(solution)/shard_map/ppermute | solution.py:393
  140.8 15.0 %collective-permute-start.8 = (bf16[384,1536]{1,0:T(8,128)(2,1)S(1)}, bf16[384,1536]{1,0:T(8,128)(2,1)}, u32[]{:S(2)}, u32[]{:S(2)}) collective-permute-start(bf16[384,1536]{1,0:T(8,128)(2,1)S(1)} %copy-done.32), channel_id=1, source_target_pairs={{0,1},{1,0},{2,3},{3,2},{4,5},{5,4},{6,7},{7,6},{8,9},{9,8},{10,11... | collective-permute-start | bytes 3538952 | tf_op jit(solution)/shard_map/ppermute | solution.py:393
  144.0 16.2 %collective-permute-start.9 = (bf16[384,768]{1,0:T(8,128)(2,1)}, bf16[384,768]{1,0:T(8,128)(2,1)}, u32[]{:S(2)}, u32[]{:S(2)}) collective-permute-start(bf16[384,768]{1,0:T(8,128)(2,1)} %get-tuple-element.81), channel_id=1, source_target_pairs={{0,1},{1,0},{2,3},{3,2},{4,5},{5,4},{6,7},{7,6},{8,9},{9,8},{10,11... | collective-permute-start | bytes 1769480 | tf_op jit(solution)/shard_map/ppermute | solution.py:393
  144.3 11.5 %collective-permute-start.6 = (bf16[512,384]{1,0:T(8,128)(2,1)}, bf16[512,384]{1,0:T(8,128)(2,1)S(1)}, u32[]{:S(2)}, u32[]{:S(2)}) collective-permute-start(bf16[512,384]{1,0:T(8,128)(2,1)} %get-tuple-element.69), channel_id=1, source_target_pairs={{0,16},{16,0},{1,17},{17,1},{2,18},{18,2},{3,19},{19,3},{4,20},{20... | collective-permute-start | bytes 1179656 | tf_op jit(solution)/shard_map/ppermute | solution.py:581
  146.8 13.4 %copy-start.4 = (bf16[4,1,48,1536]{3,2,1,0:T(8,128)(2,1)}, bf16[4,1,48,1536]{3,2,1,0:T(8,128)(2,1)S(1)}, u32[]{:S(2)}) copy-start(bf16[4,1,48,1536]{3,2,1,0:T(8,128)(2,1)S(1)} %add_convert_fusion.1.refs_10_) | copy-start | bytes 1769476
  146.8 15.2 %collective-permute-start.10 = (bf16[4,1,48,1536]{3,2,1,0:T(8,128)(2,1)S(1)}, bf16[4,1,48,1536]{3,2,1,0:T(8,128)(2,1)S(1)}, u32[]{:S(2)}, u32[]{:S(2)}) collective-permute-start(bf16[4,1,48,1536]{3,2,1,0:T(8,128)(2,1)S(1)} %add_convert_fusion.1.refs_10_), channel_id=1, source_target_pairs={{0,2},{1,3},{2,0},{3,1},{4,6},{5,7},{6,4},{7,5},{8,10},{9,11},{10,... | collective-permute-start | bytes 1769480 | tf_op jit(solution)/shard_map/ppermute | solution.py:393
  155.8 4.4 %copy-start.3 = (bf16[512,384]{1,0:T(8,128)(2,1)}, bf16[512,384]{1,0:T(8,128)(2,1)S(1)}, u32[]{:S(2)}) copy-start(bf16[512,384]{1,0:T(8,128)(2,1)S(1)} %collective-permute-done.6.refs_5_) | copy-start | bytes 1179652
  155.8 4.4 %copy-start.5 = (bf16[384,768]{1,0:T(8,128)(2,1)S(1)}, bf16[384,768]{1,0:T(8,128)(2,1)}, u32[]{:S(2)}) copy-start(bf16[384,768]{1,0:T(8,128)(2,1)} %get-tuple-element.72.refs_9_) | copy-start | bytes 1769476
  157.4 4.6 %copy-start.9 = (bf16[4,2,48,768]{3,2,1,0:T(8,128)(2,1)}, bf16[4,2,48,768]{3,2,1,0:T(8,128)(2,1)S(1)}, u32[]{:S(2)}) copy-start(bf16[4,2,48,768]{3,2,1,0:T(8,128)(2,1)S(1)} %add_convert_fusion.refs_11_) | copy-start | bytes 1769476
  157.4 14.8 %collective-permute-start.11 = (bf16[4,2,48,768]{3,2,1,0:T(8,128)(2,1)S(1)}, bf16[4,2,48,768]{3,2,1,0:T(8,128)(2,1)}, u32[]{:S(2)}, u32[]{:S(2)}) collective-permute-start(bf16[4,2,48,768]{3,2,1,0:T(8,128)(2,1)S(1)} %add_convert_fusion.refs_11_), channel_id=1, source_target_pairs={{0,16},{16,0},{1,17},{17,1},{2,18},{18,2},{3,19},{19,3},{4,20},{20... | collective-permute-start | bytes 1769480 | tf_op jit(solution)/shard_map/ppermute | solution.py:423
  159.0 3.0 %copy-start.15 = (bf16[384,1536]{1,0:T(8,128)(2,1)S(1)}, bf16[384,1536]{1,0:T(8,128)(2,1)}, u32[]{:S(2)}) copy-start(bf16[384,1536]{1,0:T(8,128)(2,1)} %copy-done.14) | copy-start | bytes 3538948
  161.3 23.1 %collective-permute-start.14 = (bf16[4,1,48,768]{3,2,1,0:T(8,128)(2,1)S(1)}, bf16[4,1,48,768]{3,2,1,0:T(8,128)(2,1)}, u32[]{:S(2)}, u32[]{:S(2)}) collective-permute-start(bf16[4,1,48,768]{3,2,1,0:T(8,128)(2,1)S(1)} %add_convert_fusion.9.refs_12_), channel_id=1, source_target_pairs={{0,2},{1,3},{2,0},{3,1},{4,6},{5,7},{6,4},{7,5},{8,10},{9,11},{10,... | collective-permute-start | bytes 884744 | tf_op jit(solution)/shard_map/ppermute | solution.py:393
  172.2 3.4 %copy-start.11 = (bf16[4,1,48,768]{3,2,1,0:T(8,128)(2,1)}, bf16[4,1,48,768]{3,2,1,0:T(8,128)(2,1)S(1)}, u32[]{:S(2)}) copy-start(bf16[4,1,48,768]{3,2,1,0:T(8,128)(2,1)S(1)} %add_convert_fusion.8.refs_9_) | copy-start | bytes 884740
  172.3 13.3 %collective-permute-start.12 = (bf16[4,1,48,768]{3,2,1,0:T(8,128)(2,1)S(1)}, bf16[4,1,48,768]{3,2,1,0:T(8,128)(2,1)S(1)}, u32[]{:S(2)}, u32[]{:S(2)}) collective-permute-start(bf16[4,1,48,768]{3,2,1,0:T(8,128)(2,1)S(1)} %add_convert_fusion.8.refs_9_), channel_id=1, source_target_pairs={{0,16},{16,0},{1,17},{17,1},{2,18},{18,2},{3,19},{19,3},{4,20},{20... | collective-permute-start | bytes 884744 | tf_op jit(solution)/shard_map/ppermute | solution.py:423
  175.0 13.4 %collective-permute-start.13 = (bf16[4,1,48,768]{3,2,1,0:T(8,128)(2,1)S(1)}, bf16[4,1,48,768]{3,2,1,0:T(8,128)(2,1)S(1)}, u32[]{:S(2)}, u32[]{:S(2)}) collective-permute-start(bf16[4,1,48,768]{3,2,1,0:T(8,128)(2,1)S(1)} %add_convert_fusion.7.refs_10_), channel_id=1, source_target_pairs={{0,2},{1,3},{2,0},{3,1},{4,6},{5,7},{6,4},{7,5},{8,10},{9,11},{10,... | collective-permute-start | bytes 884744 | tf_op jit(solution)/shard_map/ppermute | solution.py:393
  175.7 8.6 %copy-start.6 = (bf16[384,768]{1,0:T(8,128)(2,1)S(1)}, bf16[384,768]{1,0:T(8,128)(2,1)}, u32[]{:S(2)}) copy-start(bf16[384,768]{1,0:T(8,128)(2,1)} %get-tuple-element.72.refs_9_) | copy-start | bytes 1769476
  184.3 4.1 %copy-start.8 = (bf16[4,1,48,1536]{3,2,1,0:T(8,128)(2,1)S(1)}, bf16[4,1,48,1536]{3,2,1,0:T(8,128)(2,1)}, u32[]{:S(2)}) copy-start(bf16[4,1,48,1536]{3,2,1,0:T(8,128)(2,1)} %copy-done.7) | copy-start | bytes 1769476
  205.3 4.5 %copy-start.18 = (bf16[48,2304]{1,0:T(8,128)(2,1)S(1)}, bf16[48,2304]{1,0:T(8,128)(2,1)}, u32[]{:S(2)}) copy-start(bf16[48,2304]{1,0:T(8,128)(2,1)} %get-tuple-element.110.refs_15_) | copy-start | bytes 663556
  205.3 5.8 %copy-start.17 = (bf16[48,2304]{1,0:T(8,128)(2,1)S(1)}, bf16[48,2304]{1,0:T(8,128)(2,1)}, u32[]{:S(2)}) copy-start(bf16[48,2304]{1,0:T(8,128)(2,1)} %get-tuple-element.109.refs_16_) | copy-start | bytes 663556
  205.3 8.3 %copy-start.16 = (bf16[48,2304]{1,0:T(8,128)(2,1)S(1)}, bf16[48,2304]{1,0:T(8,128)(2,1)}, u32[]{:S(2)}) copy-start(bf16[48,2304]{1,0:T(8,128)(2,1)} %get-tuple-element.108.refs_17_) | copy-start | bytes 663556
  205.3 2.7 %collective-permute-start.16 = (bf16[384,1152]{1,0:T(8,128)(2,1)}, bf16[384,1152]{1,0:T(8,128)(2,1)S(1)}, u32[]{:S(2)}, u32[]{:S(2)}) collective-permute-start(bf16[384,1152]{1,0:T(8,128)(2,1)} %get-tuple-element.99), channel_id=1, source_target_pairs={{0,1},{1,0},{2,3},{3,2},{4,5},{5,4},{6,7},{7,6},{8,9},{9,8},{10,11... | collective-permute-start | bytes 2654216 | tf_op jit(solution)/shard_map/ppermute | solution.py:393
  209.2 12.3 %collective-permute-start.17 = (bf16[4,1,48,1152]{3,2,0,1:T(8,128)(2,1)S(1)}, bf16[4,1,48,1152]{3,2,0,1:T(8,128)(2,1)S(1)}, u32[]{:S(2)}, u32[]{:S(2)}) collective-permute-start(bf16[4,1,48,1152]{3,2,0,1:T(8,128)(2,1)S(1)} %add_convert_fusion.3), channel_id=1, source_target_pairs={{0,2},{1,3},{2,0},{3,1},{4,6},{5,7},{6,4},{7,5},{8,10},{9,11},{10,... | collective-permute-start | bytes 1327112 | tf_op jit(solution)/shard_map/ppermute | solution.py:393
  209.8 19.1 %collective-permute-start.20 = (bf16[48,2304]{1,0:T(8,128)(2,1)S(1)}, bf16[48,2304]{1,0:T(8,128)(2,1)S(1)}, u32[]{:S(2)}, u32[]{:S(2)}) collective-permute-start(bf16[48,2304]{1,0:T(8,128)(2,1)S(1)} %copy-done.18), channel_id=1, source_target_pairs={{0,4},{1,5},{2,6},{3,7},{4,0},{5,1},{6,2},{7,3},{8,12},{9,13},{10,... | collective-permute-start | bytes 663560 | tf_op jit(solution)/shard_map/ppermute | solution.py:393
  211.1 23.3 %collective-permute-start.21 = (bf16[48,2304]{1,0:T(8,128)(2,1)S(1)}, bf16[48,2304]{1,0:T(8,128)(2,1)}, u32[]{:S(2)}, u32[]{:S(2)}) collective-permute-start(bf16[48,2304]{1,0:T(8,128)(2,1)S(1)} %copy-done.17), channel_id=1, source_target_pairs={{0,8},{1,9},{2,10},{3,11},{4,12},{5,13},{6,14},{7,15},{8,0},{9,1},... | collective-permute-start | bytes 663560 | tf_op jit(solution)/shard_map/ppermute | solution.py:393
  213.6 20.9 %collective-permute-start.22 = (bf16[48,2304]{1,0:T(8,128)(2,1)S(1)}, bf16[48,2304]{1,0:T(8,128)(2,1)}, u32[]{:S(2)}, u32[]{:S(2)}) collective-permute-start(bf16[48,2304]{1,0:T(8,128)(2,1)S(1)} %copy-done.16), channel_id=1, source_target_pairs={{0,12},{1,13},{2,14},{3,15},{4,8},{5,9},{6,10},{7,11},{8,4},{9,5},... | collective-permute-start | bytes 663560 | tf_op jit(solution)/shard_map/ppermute | solution.py:393
  214.2 23.4 %collective-permute-start.15 = (bf16[512,768]{1,0:T(8,128)(2,1)}, bf16[512,768]{1,0:T(8,128)(2,1)}, u32[]{:S(2)}, u32[]{:S(2)}) collective-permute-start(bf16[512,768]{1,0:T(8,128)(2,1)} %get-tuple-element.95), channel_id=1, source_target_pairs={{0,16},{16,0},{1,17},{17,1},{2,18},{18,2},{3,19},{19,3},{4,20},{20... | collective-permute-start | bytes 2359304 | tf_op jit(solution)/shard_map/ppermute | solution.py:659
  223.4 23.0 %all-to-all-start = ((bf16[4,48,1152]{2,1,0:T(8,128)(2,1)}), bf16[4,48,1152]{2,1,0:T(8,128)(2,1)S(1)}, u32[]{:S(2)}, u32[]{:S(2)}) async-start(bf16[4,48,1152]{2,1,0:T(8,128)(2,1)} %fusion.refs_7_), calls=%async_computation.1 | async-start | bytes 884736 | tf_op jit(solution)/shard_map/all_to_all | solution.py:398
  227.9 20.2 %collective-permute-start.19 = (bf16[48,3072]{1,0:T(8,128)(2,1)}, bf16[48,3072]{1,0:T(8,128)(2,1)S(1)}, u32[]{:S(2)}, u32[]{:S(2)}) collective-permute-start(bf16[48,3072]{1,0:T(8,128)(2,1)} %reduce-scatter.2.cloned.1.call-done.refs_6_.refs_1_), channel_id=1, source_target_pairs={{0,16},{16,0},{1,17},{17,1},{2,18},{18,2},{3,19},{19,3},{4,20},{20... | collective-permute-start | bytes 884744 | tf_op jit(solution)/shard_map/ppermute | solution.py:687
  235.6 6.5 %copy-start.20 = (bf16[48,2304]{1,0:T(8,128)(2,1)}, bf16[48,2304]{1,0:T(8,128)(2,1)S(1)}, u32[]{:S(2)}) copy-start(bf16[48,2304]{1,0:T(8,128)(2,1)S(1)} %fusion.3.refs_3_) | copy-start | bytes 663556
  235.6 12.4 %collective-permute-start.23 = (bf16[48,2304]{1,0:T(8,128)(2,1)S(1)}, bf16[48,2304]{1,0:T(8,128)(2,1)S(1)}, u32[]{:S(2)}, u32[]{:S(2)}) collective-permute-start(bf16[48,2304]{1,0:T(8,128)(2,1)S(1)} %fusion.3.refs_3_), channel_id=1, source_target_pairs={{0,16},{16,0},{1,17},{17,1},{2,18},{18,2},{3,19},{19,3},{4,20},{20... | collective-permute-start | bytes 663560 | tf_op jit(solution)/shard_map/ppermute | solution.py:687
  246.5 5.2 %copy-start.23 = (bf16[48,1152]{1,0:T(8,128)(2,1)}, bf16[48,1152]{1,0:T(8,128)(2,1)S(1)}, u32[]{:S(2)}) copy-start(bf16[48,1152]{1,0:T(8,128)(2,1)S(1)} %reduce_sum.12.refs_1_) | copy-start | bytes 331780
  246.5 5.2 %collective-permute-start.18 = (bf16[48,1152]{1,0:T(8,128)(2,1)S(1)}, bf16[48,1152]{1,0:T(8,128)(2,1)S(1)}, u32[]{:S(2)}, u32[]{:S(2)}) collective-permute-start(bf16[48,1152]{1,0:T(8,128)(2,1)S(1)} %reduce_sum.12.refs_1_), channel_id=1, source_target_pairs={{0,16},{16,0},{1,17},{17,1},{2,18},{18,2},{3,19},{19,3},{4,20},{20... | collective-permute-start | bytes 331784 | tf_op jit(solution)/shard_map/ppermute | solution.py:687
  (13 other events, 10.3 us)
Sparse Core Ops, SparseCore 0:
  11.7 96.6 all-gather.1
  139.3 86.1 reduce-scatter.1
where the time goes:
time: 267 us; the launch traced here: 262 us
  Pallas kernels  112 us (42%)
  waiting for transfers between devices  76.1 us (29%)
  starting transfers between devices  32.1 us (12%)
  between operations  15.1 us (6%)
  local copies, waits for them, and re-layouts  13.4 us (5%)
  other arithmetic  13.1 us (5%)
    pallas_call x13, Pallas kernels, call(): pl.pallas_call(waiting(kernel, 1 + len(inputs), len(after)), name=name, g...  112 us
    ppermute x15, waiting for transfers between devices, flipped(): lax.ppermute(array, 'fsdp', [(spot, spot ^ bit) for spot in range(parts)])  46.1 us
    ppermute x15, starting transfers between devices, flipped(): lax.ppermute(array, 'fsdp', [(spot, spot ^ bit) for spot in range(parts)])  13.9 us
    all_gather x1, waiting for transfers between devices, body(): lax.all_gather(jnp.concatenate([output_weight, *hidden], axis=1), 'fsdp',...  10.5 us
    convert_element_type x10, other arithmetic, rounded_sum(): return total.astype(BF16)  10.2 us
    ppermute x1, waiting for transfers between devices, body(): dm_came = lax.ppermute(dm_away, 'seq', SWAP)  8.42 us
    unnamed x78, local copies, waits for them, and re-layouts  7.74 us
    ppermute x1, waiting for transfers between devices, body(): o_came = lax.ppermute(o_other, 'seq', SWAP)  6.74 us
  transfers between devices with their start and end apart: 27, of which 11 were waited for; matrix products, arithmetic and copies ran while one was open for 6% of the time, Pallas kernels for 30%

commit v1 on v0

--- a/solution.py
+++ b/solution.py
@@ -183,10 +183,10 @@
 
 def attend_back(pair, meta, qkv, o_own, o_other, d_own, d_other, lse, zt, weight, *refs):
     last = pair == 2
-    count = (0, 0, 6)[pair]
+    count = (0, 0, 4)[pair]
     extra, refs = refs[:count], refs[count:]
-    keep, send, *outs = refs[: 3 + last]
-    km, vm, kt, do, inner, dk, dv, dqt, dqkv, s_sc, w_sc, p_sc, ds_sc = refs[3 + last :]
+    keep, send, *outs = refs[:3]
+    km, vm, kt, do, inner, dk, dv, dqt, dqkv, s_sc, w_sc, p_sc, ds_sc = refs[3:]
     length = qkv.shape[0]
     half = length // 2
     lane = lax.broadcasted_iota(jnp.int32, (1, PAIR), 1)
@@ -255,17 +255,20 @@
     if last:
         for spot in range(2):
             columns = slice(spot * 3 * PAIR, (spot + 1) * 3 * PAIR)
-            keep[:, columns] = extra[3 * spot][...]
-            send[:, columns] = extra[3 * spot + 1][...]
-        for side, target in zip((1 - meta[0], meta[0]), outs):
-            rows = half_at(side, half)
-            part = dot_t(dqkv[rows, :], weight[:, 6 * PAIR :])
-            for spot in range(2):
-                columns = slice(spot * 3 * PAIR, (spot + 1) * 3 * PAIR)
-                part += dot_t(extra[3 * spot + 2][rows, :], weight[:, columns])
-            target[...] = part.astype(target.dtype)
-    else:
-        outs[0][...] = dqkv[...]
+            keep[:, columns] = extra[2 * spot][...]
+            send[:, columns] = extra[2 * spot + 1][...]
+    outs[0][...] = dqkv[...]
+
+
+def token_back(meta, t0, t1, t2, weight, away, mine_out):
+    half = away.shape[0]
+    for side, target in ((1 - meta[0], away), (meta[0], mine_out)):
+        part = None
+        for spot, token in enumerate((t0, t1, t2)):
+            columns = slice(spot * 3 * PAIR, (spot + 1) * 3 * PAIR)
+            new = dot_t(token[half_at(side, half), :], weight[:, columns])
+            part = new if part is None else part + new
+        target[...] = part.astype(target.dtype)
 
 
 def added(step, total, first, part):
@@ -280,8 +283,7 @@
 
 def feed(
     meta, own, mixed, gains, weight, up, down, upstream,
-    out, first, up_keep, up_send, down_keep, down_send, dresid, db, away, mine_out,
-    resid, zb, zt_natural, zt, total, g_total, active, dpre, turned, picked,
+    active, dpre, zt_natural, zt, resid, dresid, db, away, mine_out, zb, g_total,
 ):
     step = pl.program_id(0)
     gain = gains[1:2, :].astype(F32)
@@ -307,23 +309,7 @@
         active[:, mine] = (v * cdf).astype(BF16)
         slope = cdf + v * (0.5 * root) * (1.0 - t * t) * (1.0 + 0.134145 * square)
         dpre[:, mine] = (slope_in * slope).astype(BF16)
-        turned[mine, :] = active[:, mine].T
-    added(step, total, resid, dot(active[...], down[...]))
     added(step, g_total, None, dot_t(dpre[...], up[...]))
-
-    @pl.when(step < 2)
-    def _():
-        first[:, :width] = dot(zt_natural[...], dpre[...]).astype(BF16)
-        first[:, width:] = dot(turned[...], upstream[...]).astype(BF16)
-
-    @pl.when(step >= 2)
-    def _():
-        rows_in_order(meta, turned, picked)
-        size = width // 2
-        for spot, (up_part, down_part) in enumerate(((up_keep, down_keep), (up_send, down_send))):
-            mine = slice(spot * size, (spot + 1) * size)
-            up_part[...] = dot(zt[mine, :], dpre[...]).astype(BF16)
-            down_part[...] = dot(picked[mine, :], upstream[...]).astype(BF16)
 
     @pl.when(step == pl.num_programs(0) - 1)
     def _():
@@ -334,13 +320,44 @@
             target[...] = dot_t(low, weight[half_at(side, 3 * PAIR), :]).astype(BF16)
         dresid[...] = grad
         db[...] = low
+
+
+def hidden_back(
+    meta, zt_natural, zt, active, dpre, upstream, mt, db,
+    first, up_keep, up_send, down_keep, down_send, mixed_keep, mixed_send, turned, picked,
+):
+    step = pl.program_id(0)
+    width = active.shape[1]
+    turned[...] = active[...].T
+
+    @pl.when(step < 2)
+    def _():
+        first[:, :width] = dot(zt_natural[...], dpre[...]).astype(BF16)
+        first[:, width:] = dot(turned[...], upstream[...]).astype(BF16)
+
+    @pl.when(step >= 2)
+    def _():
+        rows_in_order(meta, turned, picked)
+        size = width // 2
+        for spot, (up_part, down_part) in enumerate(((up_keep, down_keep), (up_send, down_send))):
+            mine = slice(spot * size, (spot + 1) * size)
+            up_part[...] = dot(zt[mine, :], dpre[...]).astype(BF16)
+            down_part[...] = dot(picked[mine, :], upstream[...]).astype(BF16)
+
+    @pl.when(step == pl.num_programs(0) - 1)
+    def _():
+        size = width // 2
+        mixed_send[...] = dot(mt[size:, :], db[...]).astype(BF16)
+        mixed_keep[...] = dot(mt[:size, :], db[...]).astype(BF16)
+
+
+def forward_out(meta, before, active, down, out, total):
+    step = pl.program_id(0)
+    added(step, total, before, dot(active[...], down[...]))
+
+    @pl.when(step == pl.num_programs(0) - 1)
+    def _():
         out[...] = total[...].astype(out.dtype)
-
-
-def output_back(meta, mt, db, keep, send):
-    middle = keep.shape[0]
-    send[...] = dot(mt[middle:, :], db[...]).astype(BF16)
-    keep[...] = dot(mt[:middle, :], db[...]).astype(BF16)
 
 
 def input_back(meta, own, mine, other, dresid, gains, out):
@@ -369,7 +386,12 @@
 
 def feed_out(split, meta, first, first_too, last, last_too, weight, gain, up, down, output, gain_grad):
     rows, dim = output.shape
-    output[...] = last[:, -dim:].astype(F32) + last_too[:, -dim:].astype(F32)
+    if split:
+        width = dim // 2
+        for side, source in ((meta[0], last), (1 - meta[0], last_too)):
+            output[:, half_at(side, width)] = source[:, 2 * dim :].astype(F32)
+    else:
+        output[...] = last[:, -dim:].astype(F32) + last_too[:, -dim:].astype(F32)
     for k in range(4):
         parts = []
         for kind in range(2):
@@ -534,27 +556,17 @@
     tokens = whole(half, dim)
 
     later = column(chunk, dim, lambda k: jnp.maximum(k - 2, 0))
-    out, grad_first, up_keep, up_send, down_keep, down_send, dresid, db, dm_away, dm_mine = call(
+    turned = whole(dim, half)
+    active, dpre, zt_natural, zt_two, resid, dresid, db, dm_away, dm_mine = call(
         feed,
         "feed",
-        (shaped(half, dim), shaped(dim, 4 * dim))
-        + (shaped(chunk, 2 * dim),) * 4
-        + (total_f32, shaped(half, dim), shaped(half, group), shaped(half, group)),
+        (shaped(half, wide),) * 2
+        + (shaped(dim, half),) * 2
+        + (total_f32, total_f32, shaped(half, dim), shaped(half, group), shaped(half, group)),
         meta,
         (own, mixed, gains, rest, rest, rest, upstream),
-        [
-            pltpu.VMEM((half, dim), F32),
-            pltpu.VMEM((half, dim), BF16),
-            pltpu.VMEM((dim, half), BF16),
-            pltpu.VMEM((dim, half), BF16),
-            pltpu.VMEM((half, dim), F32),
-            pltpu.VMEM((half, dim), F32),
-            pltpu.VMEM((half, dim), BF16),
-            pltpu.VMEM((half, dim), BF16),
-            pltpu.VMEM((dim, half), BF16),
-            pltpu.VMEM((dim, half), BF16),
-        ],
-        took=36,
+        [pltpu.VMEM((half, dim), BF16), pltpu.VMEM((half, dim), F32)],
+        took=20,
         grid=(4,),
         specs=[
             tokens,
@@ -565,33 +577,32 @@
             column(dim, dim, lambda k: 2 + 2 * k),
             tokens,
         ],
-        out_specs=[tokens, column(dim, 2 * dim, lambda k: jnp.minimum(k, 1))]
-        + [later] * 4
-        + [tokens, tokens, whole(half, group), whole(half, group)],
-    )
-
-    if direct:
-        first_sum = lax.psum_scatter(grad_first, "fsdp", scatter_dimension=0, tiled=True)
-        up_came = flipped(up_send, parts, 1)
-        down_came = flipped(down_send, parts, 1)
+        out_specs=[column(half, dim)] * 2 + [turned] * 2 + [tokens] * 3 + [whole(half, group)] * 2,
+    )
+    dm_came = lax.ppermute(dm_away, "seq", SWAP)
+    grad_first, up_keep, up_send, down_keep, down_send, mixed_keep, mixed_send = call(
+        hidden_back,
+        "hidden_back",
+        (shaped(dim, 4 * dim),) + (shaped(chunk, 2 * dim),) * 4 + (shaped(chunk, dim),) * 2,
+        meta,
+        (zt_natural, zt_two, active, dpre, upstream, mixed_t, db),
+        [pltpu.VMEM((dim, half), BF16), pltpu.VMEM((dim, half), BF16)],
+        took=12,
+        grid=(4,),
+        specs=[turned, turned, column(half, dim), column(half, dim), tokens, turned, tokens],
+        out_specs=[column(dim, 2 * dim, lambda k: jnp.minimum(k, 1))] + [later] * 4 + [whole(chunk, dim)] * 2,
+    )
+    dm_came = pinned(dm_came, up_keep)
 
     def blocks_of(part):
         return part.reshape(4, 2, rows, -1)
 
-    dm_came = lax.ppermute(dm_away, "seq", SWAP)
-    mixed_keep, mixed_send = call(output_back, "output_back", (shaped(chunk, dim),) * 2, meta, (mixed_t, db))
-    dm_came = pinned(dm_came, mixed_keep)
-    marks = [[mixed_keep], [], []]
+    marks = [[], [], []]
     if direct:
-        mixed_came = flipped(mixed_send, parts, 1)
-        up_red = Reduction([blocks_of(part) for part in (up_keep, pinned(up_came, db))], parts, place)
-        marks[0].append(up_red.go(2))
-        down_red = Reduction([blocks_of(part) for part in (down_keep, pinned(down_came, dm_came))], parts, place)
-        marks[0].append(down_red.go("seq"))
-        mixed_red = Reduction([blocks_of(part) for part in (mixed_keep, pinned(mixed_came, dm_came))], parts, place)
-        marks[0].append(mixed_red.go(2))
-        marks[0].append(up_red.came)
-
+        first_sum = lax.psum_scatter(pinned(grad_first, dm_came), "fsdp", scatter_dimension=0, tiled=True)
+        up_came, down_came, mixed_came = (
+            flipped(pinned(part, dm_came), parts, 1) for part in (up_send, down_send, mixed_send)
+        )
     def attend_back_call(pair, outs, out_specs, extra, after):
         width = (9 if pair == 2 else 3) * PAIR
         pick = lambda step: pair
@@ -624,7 +635,7 @@
             + [
                 pl.BlockSpec((1, 8, length), lambda step: (pair, 0, 0)),
                 whole(dim, length),
-                whole(dim, 9 * PAIR) if pair == 2 else column(dim, 3 * PAIR, pick),
+                column(dim, 3 * PAIR, pick),
             ]
             + [whole(*part.shape) for part in extra],
             out_specs=[whole(chunk, width)] * 2 + out_specs,
@@ -633,47 +644,83 @@
     one = (shaped(length, 3 * PAIR),)
     keep_0, send_0, token_0 = attend_back_call(0, one, [whole(length, 3 * PAIR)], (), marks[0])
     if direct:
-        up_red.take(token_0)
-        down_red.take(token_0)
-        marks[1] = [up_red.go("seq"), down_red.go(2)]
+        pairs = ((up_keep, up_came), (down_keep, down_came), (mixed_keep, mixed_came))
+        up_red, down_red, mixed_red = (
+            Reduction([blocks_of(part) for part in (keep, pinned(came, token_0))], parts, place) for keep, came in pairs
+        )
+        marks[1] += [up_red.go(2), down_red.go("seq"), mixed_red.go("seq")]
     keep_1, send_1, token_1 = attend_back_call(1, one, [whole(length, 3 * PAIR)], (), marks[1] + [token_0])
+    marks[2].append(token_1)
+    joint_keep, joint_send, token_2 = attend_back_call(
+        2, one, [whole(length, 3 * PAIR)], (keep_0, send_0, keep_1, send_1), marks[2]
+    )
+    if direct:
+        reds = (up_red, down_red, mixed_red)
+        joint_send, *cames = lax.optimization_barrier((joint_send, *(red.came for red in reds)))
+        for red, came in zip(reds, cames):
+            red.terms.append(came)
+    marks = []
+    marks = []
+    if direct:
+        joint_came = flipped(joint_send, parts, 1)
+        joint_red = Reduction([blocks_of(part) for part in (joint_keep, joint_came)], parts, place)
+        marks = [up_red.go("seq"), down_red.go(2), mixed_red.go(2), joint_red.go(2)]
+    sent, own_part = call(
+        token_back,
+        "token_back",
+        (shaped(half, dim), total_f32),
+        meta,
+        (token_0, token_1, token_2, weight),
+        took=5,
+        after=marks,
+    )
+    other_part = lax.ppermute(sent, "seq", SWAP)
+
+    def forward_call(late, before, after):
+        at = 2 * late
+        return call(
+            forward_out,
+            "forward_out",
+            (shaped(half, dim) if late else total_f32,),
+            meta,
+            (before, active, rest),
+            [pltpu.VMEM((half, dim), F32)],
+            took=3,
+            after=after,
+            grid=(2,),
+            specs=[tokens, column(half, dim, lambda k: at + k), column(dim, dim, lambda k: 2 + 2 * (at + k))],
+            out_specs=[tokens],
+        )
+
+    marks = [own_part]
+    if direct:
+        joint_red.take(own_part)
+        joint_sum = rounded_sum(joint_red.terms).reshape(4, rows, -1)
+        marks.append(joint_sum)
+    (out,) = forward_call(0, resid, marks)
+    marks = []
     if direct:
         last_sum = []
         for red in (up_red, down_red, mixed_red):
-            red.take(token_1)
+            red.take(out)
             last_sum.append(rounded_sum(red.terms))
         last_sum = jnp.concatenate(last_sum, axis=-1).reshape(4, rows, -1)
         deep = me // 4
         last_parts = [lax.dynamic_index_in_dim(last_sum, deep, 0, keepdims=False)]
         for far in (1, 2, 3):
             away = lax.dynamic_index_in_dim(last_sum, deep ^ far, 0, keepdims=False)
-            marks[2].append(away)
             last_parts.append(flipped(away, parts, 4 * far))
-    joint_keep, joint_send, sent, own_part = attend_back_call(
-        2,
-        (shaped(half, dim), total_f32),
-        [tokens] * 2,
-        (keep_0, send_0, token_0, keep_1, send_1, token_1),
-        marks[2],
-    )
-    other_part = lax.ppermute(sent, "seq", SWAP)
-    marks = []
-    marks = []
-    if direct:
-        joint_came = flipped(joint_send, parts, 1)
-        joint_red = Reduction([blocks_of(part) for part in (joint_keep, joint_came)], parts, place)
-        joint_red.go(2)
-        joint_red.take(joint_keep)
-        joint_sum = rounded_sum(joint_red.terms).reshape(4, rows, -1)
-        marks = [first_sum, joint_sum]
+            marks.append(away)
         joint_sum = exchanged(joint_sum, parts)
+    (out,) = forward_call(1, out, marks)
+    marks = [out]
     (input_grad,) = call(
         input_back, "input_back", (total_f32,), meta, (own, own_part, other_part, dresid, gains), after=marks
     )
 
     if direct:
         last_sum = rounded_sum(last_parts)
-        joint_sum = jnp.sum(pinned(joint_sum, input_grad).astype(F32), axis=0).astype(BF16)
+        joint_sum = jnp.sum(pinned(joint_sum, out).astype(F32), axis=0).astype(BF16)
     else:
 
         def scattered(keep, send):
@@ -684,7 +731,16 @@
         last_sum = ((up_keep, up_send), (down_keep, down_send), (mixed_keep, mixed_send))
         last_sum = jnp.concatenate([scattered(*pair) for pair in last_sum], axis=1)
         joint_sum = scattered(joint_keep, joint_send)
+    first_sum = pinned(first_sum, input_grad)
     first_sum, last_sum, joint_sum = ((part, lax.ppermute(part, "seq", SWAP)) for part in (first_sum, last_sum, joint_sum))
+    joint_grad, lead_grad = call(
+        joint_out,
+        "joint_out",
+        (shaped(rows, triple, dtype=F32), shaped(1, rows, dtype=F32)),
+        meta,
+        (*joint_sum, joint_weight, lead_gain[None, :]),
+        took=2,
+    )
     up_grad, down_grad, output_grad, tail_grad = call(
         functools.partial(feed_out, direct),
         "feed_out",
@@ -696,15 +752,7 @@
         ),
         meta,
         (*first_sum, *last_sum, up_weight, tail_gain[None, :]),
-    )
-    joint_grad, lead_grad = call(
-        joint_out,
-        "joint_out",
-        (shaped(rows, triple, dtype=F32), shaped(1, rows, dtype=F32)),
-        meta,
-        (*joint_sum, joint_weight, lead_gain[None, :]),
-        took=2,
-        after=[up_grad],
+        after=[joint_grad],
     )
     return (
         out[None],

time: 267 us -> 264 us (0.989)
  waiting for transfers between devices: 76.1 us -> 63.8 us
  Pallas kernels: 112 us -> 122 us
    pallas_call x13 -> x16, Pallas kernels: 112 us -> 122 us  [call(): pl.pallas_call(waiting(kernel, 1 + len(inputs), len(after)), name=name, g...]
    ppermute x1, waiting for transfers between devices: 8.42 us -> 0.01 us  [body(): dm_came = lax.ppermute(dm_away, 'seq', SWAP)]
    ppermute x15, waiting for transfers between devices: 46.1 us -> 39.4 us  [flipped(): lax.ppermute(array, 'fsdp', [(spot, spot ^ bit) for spot in range(parts)])]
    ppermute x3, waiting for transfers between devices: 0.01 us -> 3.31 us  [body(): lax.ppermute(part, 'seq', SWAP)]
    unnamed x78 -> x82, local copies, waits for them, and re-layouts: 7.74 us -> 8.4 us
    convert_element_type x10 -> x11, other arithmetic: 10.2 us -> 10.3 us  [rounded_sum(): return total.astype(BF16)]
  transfers between devices with their start and end apart: 27 -> 28, of which waited for: 11 -> 10; matrix products, arithmetic and copies ran while one was open for 6% -> 5% of each run, Pallas kernels for 30% -> 39%
where the time goes in v1:
time: 264 us; the launch traced here: 260 us
  Pallas kernels  122 us (46%)
  waiting for transfers between devices  63.8 us (24%)
  starting transfers between devices  33.4 us (13%)
  between operations  15.2 us (6%)
  other arithmetic  13.3 us (5%)
  local copies, waits for them, and re-layouts  12.1 us (5%)
    pallas_call x16, Pallas kernels, call(): pl.pallas_call(waiting(kernel, 1 + len(inputs), len(after)), name=name, g...  122 us
    ppermute x15, waiting for transfers between devices, flipped(): lax.ppermute(array, 'fsdp', [(spot, spot ^ bit) for spot in range(parts)])  39.4 us
    ppermute x15, starting transfers between devices, flipped(): lax.ppermute(array, 'fsdp', [(spot, spot ^ bit) for spot in range(parts)])  15.8 us
    all_gather x1, waiting for transfers between devices, body(): lax.all_gather(jnp.concatenate([output_weight, *hidden], axis=1), 'fsdp',...  10.5 us
    convert_element_type x11, other arithmetic, rounded_sum(): return total.astype(BF16)  10.3 us
    unnamed x82, local copies, waits for them, and re-layouts  8.4 us
    ppermute x1, waiting for transfers between devices, body(): o_came = lax.ppermute(o_other, 'seq', SWAP)  6.69 us
  transfers between devices with their start and end apart: 28, of which 10 were waited for; matrix products, arithmetic and copies ran while one was open for 5% of the time, Pallas kernels for 39%

profile of v1, /device:TPU:0, one launch (start us, length us, event | category | flops | bytes accessed | tf_op | source)
XLA Modules:
  0.0 259.8 jit_solution(7397916323124707920)
XLA Ops:
  8.1 1.7 reshape.88
  12.9 4.1 %collective-permute-start = (bf16[48,1280]{1,0:T(8,128)(2,1)S(1)}, bf16[48,1280]{1,0:T(8,128)(2,1)S(1)}, u32[]{:S(2)}, u32[]{:S(2)}) collective-permute-start(bf16[48,1280]{1,0:T(8,128)(2,1)S(1)} %pad_maximum_fusion.3), channel_id=1, source_target_pairs={{0,8},{1,9},{2,10},{3,11},{4,12},{5,13},{6,14},{7,15},{8,0},{9,1},... | collective-permute-start | bytes 368648 | tf_op jit(solution)/shard_map/ppermute | solution.py:415
  17.0 1.5 collective-permute-start.2
  18.5 4.4 %collective-permute-done = bf16[48,1280]{1,0:T(8,128)(2,1)S(1)} collective-permute-done((bf16[48,1280]{1,0:T(8,128)(2,1)S(1)}, bf16[48,1280]{1,0:T(8,128)(2,1)S(1)}, u32[]{:S(2)}, u32[]{:S(2)}) %collective-permute-start) | collective-permute-done | bytes 122912 | tf_op jit(solution)/shard_map/ppermute | solution.py:415
  23.7 17.1 %collective-permute-done.1 = bf16[96,1280]{1,0:T(8,128)(2,1)S(1)} collective-permute-done((bf16[96,1280]{1,0:T(8,128)(2,1)S(1)}, bf16[96,1280]{1,0:T(8,128)(2,1)S(1)}, u32[]{:S(2)}, u32[]{:S(2)}) %collective-permute-start.1) | collective-permute-done | bytes 245792 | tf_op jit(solution)/shard_map/ppermute | solution.py:415
  40.9 1.3 collective-permute-start.3
  42.2 7.6 %collective-permute-done.3 = bf16[192,1280]{1,0:T(8,128)(2,1)S(1)} collective-permute-done((bf16[192,1280]{1,0:T(8,128)(2,1)S(1)}, bf16[192,1280]{1,0:T(8,128)(2,1)S(1)}, u32[]{:S(2)}, u32[]{:S(2)}) %collective-permute-start.3) | collective-permute-done | bytes 491552 | tf_op jit(solution)/shard_map/ppermute | solution.py:415
  50.7 4.0 %first_norm.1.refs_1_ = f32[1024,768]{1,0:T(8,128)} custom-call(s32[33]{0:T(128)} %pad_add_fusion.refs_0_, bf16[512,768]{1,0:T(8,128)(2,1)} %bitcast.63, bf16[512,768]{1,0:T(8,128)(2,1)} %copy-done.18), custom_call_target="tpu_custom_call" | custom-call | flops 30000000 | bytes 90000 | tf_op jit(solution)/shard_map/first_norm/pallas_call | solution.py:56
  55.7 3.6 %first_scale.1 = (bf16[1024,768]{1,0:T(8,128)(2,1)}, bf16[16,768]{1,0:T(8,128)(2,1)}) custom-call(s32[33]{0:T(128)} %pad_add_fusion.refs_0_, f32[1024,768]{1,0:T(8,128)} %first_norm.1.refs_1_, bf16[384,1280]{1,0:T(8,128)(2,1)} %copy-done.1, bf16[384,1280]{1,0:T(8,128)(2,1)} %copy-done.2), custom_call_target="tpu_custom_call" | custom-call | flops 20000000 | bytes 60000 | tf_op jit(solution)/shard_map/first_scale/pallas_call | solution.py:56
  59.3 24.2 %attend.1 = (bf16[1024,1152]{1,0:T(8,128)(2,1)}, bf16[512,384]{1,0:T(8,128)(2,1)}, bf16[512,384]{1,0:T(8,128)(2,1)}, f32[3,8,1024]{2,1,0:T(8,128)}, bf16[768,1152]{1,0:T(8,128)(2,1)}) custom-call(s32[33]{0:T(128)} %pad_add_fusion.refs_0_, bf16[1024,768]{1,0:T(8,128)(2,1)} %get-tuple-element.72.refs_1_, bf16[384,1280]{1,0:T(8,128)(2,1)} %copy-done.1, ...), custom_call_target="tpu_custom_call" | custom-call | flops 220000000 | bytes 660000 | tf_op jit(solution)/shard_map/attend/pallas_call | solution.py:56
  83.4 1.7 collective-permute-start.5
  85.2 3.3 %turn.1.refs_3_.refs_7_ = bf16[768,1024]{1,0:T(8,128)(2,1)} custom-call(s32[33]{0:T(128)} %pad_add_fusion.refs_0_, bf16[1024,768]{1,0:T(8,128)(2,1)} %get-tuple-element.72.refs_1_, f32[3,8,1024]{2,1,0:T(8,128)} %get-tuple-element.75.refs_2_.refs_6_), custom_call_target="tpu_custom_call" | custom-call | flops 20000000 | bytes 60000 | tf_op jit(solution)/shard_map/turn/pallas_call | solution.py:56
  88.4 6.7 %collective-permute-done.5.refs_2_ = bf16[512,384]{1,0:T(8,128)(2,1)S(1)} collective-permute-done((bf16[512,384]{1,0:T(8,128)(2,1)}, bf16[512,384]{1,0:T(8,128)(2,1)S(1)}, u32[]{:S(2)}, u32[]{:S(2)}) %collective-permute-start.5) | collective-permute-done | bytes 393248 | tf_op jit(solution)/shard_map/ppermute | solution.py:541
  95.8 2.4 mix.1
  98.3 10.5 %all-gather.2.cloned.1.call-done.refs_4_.refs_5_.refs_6_.refs_3_ = bf16[768,6912]{1,0:T(8,128)(2,1)} async-done(((bf16[48,6912]{1,0:T(8,128)(2,1)}), bf16[768,6912]{1,0:T(8,128)(2,1)}) %all-gather.2.cloned.1.call-update) | async-done | bytes 10616848 | tf_op jit(solution)/shard_map/all_gather | solution.py:488
  108.8 18.5 %feed.1 = (bf16[512,3072]{1,0:T(8,128)(2,1)}, bf16[512,3072]{1,0:T(8,128)(2,1)}, bf16[768,512]{1,0:T(8,128)(2,1)}, bf16[768,512]{1,0:T(8,128)(2,1)}, f32[512,768...) custom-call(s32[33]{0:T(128)} %pad_add_fusion.refs_0_, ...), custom_call_target="tpu_custom_call" | custom-call | flops 200000000 | bytes 600000 | tf_op jit(solution)/shard_map/feed/pallas_call | solution.py:56
  127.4 1.5 collective-permute-start.6
  128.9 13.5 %hidden_back.1 = (bf16[768,3072]{1,0:T(8,128)(2,1)}, bf16[384,1536]{1,0:T(8,128)(2,1)}, bf16[384,1536]{1,0:T(8,128)(2,1)}, bf16[384,1536]{1,0:T(8,128)(2,1)}, bf...) custom-call(s32[33]{0:T(128)} %pad_add_fusion.refs_0_, ...), custom_call_target="tpu_custom_call" | custom-call | flops 120000000 | bytes 360000 | tf_op jit(solution)/shard_map/hidden_back/pallas_call | solution.py:56
  143.7 8.6 %attend_back.3 = (bf16[384,384]{1,0:T(8,128)(2,1)}, bf16[384,384]{1,0:T(8,128)(2,1)}, bf16[1024,384]{1,0:T(8,128)(2,1)}) custom-call(s32[33]{0:T(128)} %pad_add_fusion.refs_0_, bf16[1024,1152]{1,0:T(8,128)(2,1)} %get-tuple-element.80.refs_1_, bf16[512,384]{1,0:T(8,128)(2,1)} %get-tuple-element.73.refs_1_.refs_2_, ...), custom_call_target="tpu_custom_call" | custom-call | flops 100000000 | bytes 300000 | tf_op jit(solution)/shard_map/attend_back/pallas_call | solution.py:56
  153.3 1.3 add_convert_fusion.refs_10_
  155.8 1.2 add_convert_fusion.8.refs_11_
  157.0 1.5 collective-permute-start.12
  158.5 8.6 %attend_back.4 = (bf16[384,384]{1,0:T(8,128)(2,1)}, bf16[384,384]{1,0:T(8,128)(2,1)}, bf16[1024,384]{1,0:T(8,128)(2,1)}) custom-call(s32[33]{0:T(128)} %pad_add_fusion.refs_0_, bf16[1024,1152]{1,0:T(8,128)(2,1)} %get-tuple-element.80.refs_1_, bf16[512,384]{1,0:T(8,128)(2,1)} %get-tuple-element.73.refs_1_.refs_2_, ...), custom_call_target="tpu_custom_call" | custom-call | flops 100000000 | bytes 300000 | tf_op jit(solution)/shard_map/attend_back/pallas_call | solution.py:56
  167.1 9.7 %attend_back.5 = (bf16[384,1152]{1,0:T(8,128)(2,1)}, bf16[384,1152]{1,0:T(8,128)(2,1)}, bf16[1024,384]{1,0:T(8,128)(2,1)}) custom-call(s32[33]{0:T(128)} %pad_add_fusion.refs_0_, bf16[1024,1152]{1,0:T(8,128)(2,1)} %get-tuple-element.80.refs_1_, bf16[512,384]{1,0:T(8,128)(2,1)} %get-tuple-element.73.refs_1_.refs_2_, ...), custom_call_target="tpu_custom_call" | custom-call | flops 100000000 | bytes 300000 | tf_op jit(solution)/shard_map/attend_back/pallas_call | solution.py:56
  177.6 2.6 %collective-permute-done.13 = bf16[384,1152]{1,0:T(8,128)(2,1)} collective-permute-done((bf16[384,1152]{1,0:T(8,128)(2,1)}, bf16[384,1152]{1,0:T(8,128)(2,1)}, u32[]{:S(2)}, u32[]{:S(2)}) %collective-permute-start.13) | collective-permute-done | bytes 884768 | tf_op jit(solution)/shard_map/ppermute | solution.py:415
  180.3 1.2 add_convert_fusion.3
  181.5 1.8 collective-permute-start.14
  184.8 1.1 add_convert_fusion.7.refs_5_
  187.7 1.7 collective-permute-start.16
  189.3 6.1 %token_back.1 = (bf16[512,768]{1,0:T(8,128)(2,1)}, f32[512,768]{1,0:T(8,128)}) custom-call(s32[33]{0:T(128)} %pad_add_fusion.refs_0_, bf16[1024,384]{1,0:T(8,128)(2,1)} %get-tuple-element.91.refs_12_.refs_1_, bf16[1024,384]{1,0:T(8,128)(2,1)} %get-tuple-element.103.refs_13_.refs_2_, bf16[1024,384]{1,0:T(8,128)(2,1)} %get-tuple-element.108.refs_3_, ...), custom_call_target="tpu_custom_call" | custom-call | flops 50000000 | bytes 150000 | tf_op jit(solution)/shard_map/token_back/pallas_call | solution.py:56
  195.4 1.4 collective-permute-start.18
  196.9 1.9 fusion.refs_5_
  198.8 5.2 %forward_out.2.refs_1_ = f32[512,768]{1,0:T(8,128)} custom-call(s32[33]{0:T(128)} %pad_add_fusion.refs_0_, f32[512,768]{1,0:T(8,128)} %get-tuple-element.78.refs_1_, bf16[512,3072]{1,0:T(8,128)(2,1)} %get-tuple-element.79.refs_3_.refs_2_, bf16[768,6912]{1,0:T(8,128)(2,1)} %all-gather.2.cloned.1.call-done.refs_4_.refs_5_.refs_6_.refs_3_, ...), custom_call_target="tpu_custom_call" | custom-call | flops 30000000 | bytes 90000 | tf_op jit(solution)/shard_map/forward_out/pallas_call | solution.py:56
  204.1 1.1 add_convert_fusion.5
  205.2 1.2 add_convert_fusion.4
  207.6 2.7 %collective-permute-start.23 = (bf16[48,1920]{1,0:T(8,128)(2,1)S(1)}, bf16[48,1920]{1,0:T(8,128)(2,1)S(1)}, u32[]{:S(2)}, u32[]{:S(2)}) collective-permute-start(bf16[48,1920]{1,0:T(8,128)(2,1)S(1)} %get-tuple-element.136.refs_6_), channel_id=1, source_target_pairs={{0,12},{1,13},{2,14},{3,15},{4,8},{5,9},{6,10},{7,11},{8,4},{9,5},... | collective-permute-start | bytes 552968 | tf_op jit(solution)/shard_map/ppermute | solution.py:415
  210.3 1.7 collective-permute-start.21
  212.0 4.2 %all-to-all-start = ((bf16[4,48,1152]{2,1,0:T(8,128)(2,1)}), bf16[4,48,1152]{2,1,0:T(8,128)(2,1)S(1)}, u32[]{:S(2)}, u32[]{:S(2)}) async-start(bf16[4,48,1152]{2,1,0:T(8,128)(2,1)} %fusion.refs_5_), calls=%async_computation | async-start | bytes 884736 | tf_op jit(solution)/shard_map/all_to_all | solution.py:420
  216.3 5.0 %forward_out.3.refs_6_ = bf16[512,768]{1,0:T(8,128)(2,1)} custom-call(s32[33]{0:T(128)} %pad_add_fusion.refs_0_, f32[512,768]{1,0:T(8,128)} %forward_out.2.refs_1_, bf16[512,3072]{1,0:T(8,128)(2,1)} %get-tuple-element.79.refs_3_.refs_2_, bf16[768,6912]{1,0:T(8,128)(2,1)} %all-gather.2.cloned.1.call-done.refs_4_.refs_5_.refs_6_.refs_3_, ...), custom_call_target="tpu_custom_call" | custom-call | flops 30000000 | bytes 90000 | tf_op jit(solution)/shard_map/forward_out/pallas_call | solution.py:56
  222.1 4.5 %input_back.1 = f32[512,768]{1,0:T(8,128)} custom-call(s32[33]{0:T(128)} %pad_add_fusion.refs_0_, bf16[512,768]{1,0:T(8,128)(2,1)} %bitcast.65, f32[512,768]{1,0:T(8,128)} %get-tuple-element.115.refs_4_.refs_2_, bf16[512,768]{1,0:T(8,128)(2,1)} %copy-done.19, f32[512,768]{1,0:T(8,128)} %get-tuple-element.121.refs_4_, ...), custom_call_target="tpu_custom_call" | custom-call | flops 40000000 | bytes 120000 | tf_op jit(solution)/shard_map/input_back/pallas_call | solution.py:56
  227.6 1.5 collective-permute-start.20
  229.1 7.6 %collective-permute-done.22 = bf16[48,1920]{1,0:T(8,128)(2,1)S(1)} collective-permute-done((bf16[48,1920]{1,0:T(8,128)(2,1)S(1)}, bf16[48,1920]{1,0:T(8,128)(2,1)S(1)}, u32[]{:S(2)}, u32[]{:S(2)}) %collective-permute-start.22) | collective-permute-done | bytes 184352 | tf_op jit(solution)/shard_map/ppermute | solution.py:415
  236.9 1.5 collective-permute-start.24
  238.4 2.8 %all-to-all-done = bf16[4,48,1152]{2,1,0:T(8,128)(2,1)S(1)} async-done(((bf16[4,48,1152]{2,1,0:T(8,128)(2,1)}), bf16[4,48,1152]{2,1,0:T(8,128)(2,1)S(1)}, u32[]{:S(2)}, u32[]{:S(2)}) %all-to-all-start) | async-done | bytes 442400 | tf_op jit(solution)/shard_map/all_to_all | solution.py:420
  241.3 1.5 collective-permute-start.19
  242.8 3.3 %collective-permute-done.19.refs_2_ = bf16[48,1152]{1,0:T(8,128)(2,1)S(1)} collective-permute-done((bf16[48,1152]{1,0:T(8,128)(2,1)S(1)}, bf16[48,1152]{1,0:T(8,128)(2,1)S(1)}, u32[]{:S(2)}, u32[]{:S(2)}) %collective-permute-start.19) | collective-permute-done | bytes 110624 | tf_op jit(solution)/shard_map/ppermute | solution.py:735
  246.7 2.1 joint_out.1
  249.6 2.8 %feed_out.1 = (f32[48,3072]{1,0:T(8,128)}, f32[192,768]{1,0:T(8,128)}, f32[48,768]{1,0:T(8,128)}, f32[1,48]{1,0:T(1,128)}) custom-call(s32[33]{0:T(128)} %pad_add_fusion.refs_0_, bf16[48,3072]{1,0:T(8,128)(2,1)} %reduce-scatter.2.cloned.1.call-done.refs_1_, bf16[48,3072]{1,0:T(8,128)(2,1)} %copy-done.31, bf16[48,1920]{1,0:T(8,128)(2,1)} %copy-done.23, ...), custom_call_target="tpu_custom_call" | custom-call | flops 40000000 | bytes 120000 | tf_op jit(solution)/shard_map/feed_out/pallas_call | solution.py:56
  (149 shorter events, 19.4 us)
Async XLA Ops:
  7.2 101.7 %all-gather.2.cloned.1.call-start = ((), (), s32[]{:S(2)}) async-start(), calls=%async_computation.2 | async-start | bytes 11280384 | tf_op jit(solution)/shard_map/all_gather | solution.py:488
  12.0 5.0 %copy-start = (bf16[1,512,768]{2,1,0:T(8,128)(2,1)S(1)}, bf16[1,512,768]{2,1,0:T(8,128)(2,1)}, u32[]{:S(2)}) copy-start(bf16[1,512,768]{2,1,0:T(8,128)(2,1)} %param.8) | copy-start | bytes 2359300
  12.0 215.6 %reduce-scatter.2.cloned.1.call-start = ((), (), s32[]{:S(2)}) async-start(), calls=%async_computation.3 | async-start | bytes 5013504 | tf_op jit(solution)/shard_map/reduce_scatter | solution.py:602
  12.9 10.1 %collective-permute-start = (bf16[48,1280]{1,0:T(8,128)(2,1)S(1)}, bf16[48,1280]{1,0:T(8,128)(2,1)S(1)}, u32[]{:S(2)}, u32[]{:S(2)}) collective-permute-start(bf16[48,1280]{1,0:T(8,128)(2,1)S(1)} %pad_maximum_fusion.3), channel_id=1, source_target_pairs={{0,8},{1,9},{2,10},{3,11},{4,12},{5,13},{6,14},{7,15},{8,0},{9,1},... | collective-permute-start | bytes 368648 | tf_op jit(solution)/shard_map/ppermute | solution.py:415
  17.0 23.9 %collective-permute-start.2 = (bf16[512,768]{1,0:T(8,128)(2,1)S(1)}, bf16[512,768]{1,0:T(8,128)(2,1)S(1)}, u32[]{:S(2)}, u32[]{:S(2)}) collective-permute-start(bf16[512,768]{1,0:T(8,128)(2,1)S(1)} %bitcast.66), channel_id=1, source_target_pairs={{0,16},{16,0},{1,17},{17,1},{2,18},{18,2},{3,19},{19,3},{4,20},{20... | collective-permute-start | bytes 2359304 | tf_op jit(solution)/shard_map/ppermute | solution.py:489
  23.0 17.9 %collective-permute-start.1 = (bf16[96,1280]{1,0:T(8,128)(2,1)S(1)}, bf16[96,1280]{1,0:T(8,128)(2,1)S(1)}, u32[]{:S(2)}, u32[]{:S(2)}) collective-permute-start(bf16[96,1280]{1,0:T(8,128)(2,1)S(1)} %pad_maximum_fusion.2), channel_id=1, source_target_pairs={{0,4},{1,5},{2,6},{3,7},{4,0},{5,1},{6,2},{7,3},{8,12},{9,13},{10,... | collective-permute-start | bytes 737288 | tf_op jit(solution)/shard_map/ppermute | solution.py:415
  40.9 9.8 %copy-start.18 = (bf16[512,768]{1,0:T(8,128)(2,1)}, bf16[512,768]{1,0:T(8,128)(2,1)S(1)}, u32[]{:S(2)}) copy-start(bf16[512,768]{1,0:T(8,128)(2,1)S(1)} %collective-permute-done.2.refs_2_) | copy-start | bytes 2359300
  40.9 8.9 %collective-permute-start.3 = (bf16[192,1280]{1,0:T(8,128)(2,1)S(1)}, bf16[192,1280]{1,0:T(8,128)(2,1)S(1)}, u32[]{:S(2)}, u32[]{:S(2)}) collective-permute-start(bf16[192,1280]{1,0:T(8,128)(2,1)S(1)} %pad_maximum_fusion.1), channel_id=1, source_target_pairs={{0,2},{1,3},{2,0},{3,1},{4,6},{5,7},{6,4},{7,5},{8,10},{9,11},{10,... | collective-permute-start | bytes 1474568 | tf_op jit(solution)/shard_map/ppermute | solution.py:415
  49.9 4.9 %copy-start.1 = (bf16[384,1280]{1,0:T(8,128)(2,1)}, bf16[384,1280]{1,0:T(8,128)(2,1)S(1)}, u32[]{:S(2)}) copy-start(bf16[384,1280]{1,0:T(8,128)(2,1)S(1)} %constant_dynamic-update-slice_fusion.refs_2_) | copy-start | bytes 2949124
  49.9 4.9 %collective-permute-start.4 = (bf16[384,1280]{1,0:T(8,128)(2,1)S(1)}, bf16[384,1280]{1,0:T(8,128)(2,1)S(1)}, u32[]{:S(2)}, u32[]{:S(2)}) collective-permute-start(bf16[384,1280]{1,0:T(8,128)(2,1)S(1)} %constant_dynamic-update-slice_fusion.refs_2_), channel_id=1, source_target_pairs={{0,1},{1,0},{2,3},{3,2},{4,5},{5,4},{6,7},{7,6},{8,9},{9,8},{10,11... | collective-permute-start | bytes 2949128 | tf_op jit(solution)/shard_map/ppermute | solution.py:415
  83.4 11.7 %collective-permute-start.5 = (bf16[512,384]{1,0:T(8,128)(2,1)}, bf16[512,384]{1,0:T(8,128)(2,1)S(1)}, u32[]{:S(2)}, u32[]{:S(2)}) collective-permute-start(bf16[512,384]{1,0:T(8,128)(2,1)} %get-tuple-element.74.refs_3_), channel_id=1, source_target_pairs={{0,16},{16,0},{1,17},{17,1},{2,18},{18,2},{3,19},{19,3},{4,20},{20... | collective-permute-start | bytes 1179656 | tf_op jit(solution)/shard_map/ppermute | solution.py:541
  127.4 15.0 %collective-permute-start.6 = (bf16[512,384]{1,0:T(8,128)(2,1)}, bf16[512,384]{1,0:T(8,128)(2,1)S(1)}, u32[]{:S(2)}, u32[]{:S(2)}) collective-permute-start(bf16[512,384]{1,0:T(8,128)(2,1)} %get-tuple-element.82), channel_id=1, source_target_pairs={{0,16},{16,0},{1,17},{17,1},{2,18},{18,2},{3,19},{19,3},{4,20},{20... | collective-permute-start | bytes 1179656 | tf_op jit(solution)/shard_map/ppermute | solution.py:582
  143.1 9.1 %collective-permute-start.8 = (bf16[384,1536]{1,0:T(8,128)(2,1)}, bf16[384,1536]{1,0:T(8,128)(2,1)S(1)}, u32[]{:S(2)}, u32[]{:S(2)}) collective-permute-start(bf16[384,1536]{1,0:T(8,128)(2,1)} %get-tuple-element.97), channel_id=1, source_target_pairs={{0,1},{1,0},{2,3},{3,2},{4,5},{5,4},{6,7},{7,6},{8,9},{9,8},{10,11... | collective-permute-start | bytes 3538952 | tf_op jit(solution)/shard_map/ppermute | solution.py:415
  143.1 9.1 %collective-permute-start.7 = (bf16[384,1536]{1,0:T(8,128)(2,1)}, bf16[384,1536]{1,0:T(8,128)(2,1)S(1)}, u32[]{:S(2)}, u32[]{:S(2)}) collective-permute-start(bf16[384,1536]{1,0:T(8,128)(2,1)} %get-tuple-element.93), channel_id=1, source_target_pairs={{0,1},{1,0},{2,3},{3,2},{4,5},{5,4},{6,7},{7,6},{8,9},{9,8},{10,11... | collective-permute-start | bytes 3538952 | tf_op jit(solution)/shard_map/ppermute | solution.py:415
  143.6 12.2 %collective-permute-start.9 = (bf16[384,768]{1,0:T(8,128)(2,1)}, bf16[384,768]{1,0:T(8,128)(2,1)}, u32[]{:S(2)}, u32[]{:S(2)}) collective-permute-start(bf16[384,768]{1,0:T(8,128)(2,1)} %get-tuple-element.101), channel_id=1, source_target_pairs={{0,1},{1,0},{2,3},{3,2},{4,5},{5,4},{6,7},{7,6},{8,9},{9,8},{10,11... | collective-permute-start | bytes 1769480 | tf_op jit(solution)/shard_map/ppermute | solution.py:415
  143.7 9.6 %copy-start.11 = (bf16[384,1536]{1,0:T(8,128)(2,1)S(1)}, bf16[384,1536]{1,0:T(8,128)(2,1)}, u32[]{:S(2)}) copy-start(bf16[384,1536]{1,0:T(8,128)(2,1)} %get-tuple-element.95) | copy-start | bytes 3538948
  152.2 2.7 %copy-start.10 = (bf16[384,1536]{1,0:T(8,128)(2,1)S(1)}, bf16[384,1536]{1,0:T(8,128)(2,1)}, u32[]{:S(2)}) copy-start(bf16[384,1536]{1,0:T(8,128)(2,1)} %get-tuple-element.88) | copy-start | bytes 3538948
  154.6 2.4 copy-start.5
  154.6 22.2 %collective-permute-start.11 = (bf16[4,2,48,768]{3,2,1,0:T(8,128)(2,1)S(1)}, bf16[4,2,48,768]{3,2,1,0:T(8,128)(2,1)}, u32[]{:S(2)}, u32[]{:S(2)}) collective-permute-start(bf16[4,2,48,768]{3,2,1,0:T(8,128)(2,1)S(1)} %add_convert_fusion.refs_10_), channel_id=1, source_target_pairs={{0,16},{16,0},{1,17},{17,1},{2,18},{18,2},{3,19},{19,3},{4,20},{20... | collective-permute-start | bytes 1769480 | tf_op jit(solution)/shard_map/ppermute | solution.py:445
  155.1 3.4 %copy-start.4 = (bf16[4,1,48,1536]{3,2,1,0:T(8,128)(2,1)}, bf16[4,1,48,1536]{3,2,1,0:T(8,128)(2,1)S(1)}, u32[]{:S(2)}) copy-start(bf16[4,1,48,1536]{3,2,1,0:T(8,128)(2,1)S(1)} %add_convert_fusion.1.refs_9_) | copy-start | bytes 1769476
  155.1 21.7 %collective-permute-start.10 = (bf16[4,1,48,1536]{3,2,1,0:T(8,128)(2,1)S(1)}, bf16[4,1,48,1536]{3,2,1,0:T(8,128)(2,1)}, u32[]{:S(2)}, u32[]{:S(2)}) collective-permute-start(bf16[4,1,48,1536]{3,2,1,0:T(8,128)(2,1)S(1)} %add_convert_fusion.1.refs_9_), channel_id=1, source_target_pairs={{0,2},{1,3},{2,0},{3,1},{4,6},{5,7},{6,4},{7,5},{8,10},{9,11},{10,... | collective-permute-start | bytes 1769480 | tf_op jit(solution)/shard_map/ppermute | solution.py:415
  157.0 19.8 %collective-permute-start.12 = (bf16[4,2,48,384]{3,2,1,0:T(8,128)(2,1)S(1)}, bf16[4,2,48,384]{3,2,1,0:T(8,128)(2,1)S(1)}, u32[]{:S(2)}, u32[]{:S(2)}) collective-permute-start(bf16[4,2,48,384]{3,2,1,0:T(8,128)(2,1)S(1)} %add_convert_fusion.8.refs_11_), channel_id=1, source_target_pairs={{0,16},{16,0},{1,17},{17,1},{2,18},{18,2},{3,19},{19,3},{4,20},{20... | collective-permute-start | bytes 884744 | tf_op jit(solution)/shard_map/ppermute | solution.py:445
  177.5 2.8 %collective-permute-start.13 = (bf16[384,1152]{1,0:T(8,128)(2,1)}, bf16[384,1152]{1,0:T(8,128)(2,1)}, u32[]{:S(2)}, u32[]{:S(2)}) collective-permute-start(bf16[384,1152]{1,0:T(8,128)(2,1)} %get-tuple-element.114), channel_id=1, source_target_pairs={{0,1},{1,0},{2,3},{3,2},{4,5},{5,4},{6,7},{7,6},{8,9},{9,8},{10,11... | collective-permute-start | bytes 2654216 | tf_op jit(solution)/shard_map/ppermute | solution.py:415
  177.5 2.8 %copy-start.15 = (bf16[384,1152]{1,0:T(8,128)(2,1)S(1)}, bf16[384,1152]{1,0:T(8,128)(2,1)}, u32[]{:S(2)}) copy-start(bf16[384,1152]{1,0:T(8,128)(2,1)} %get-tuple-element.113) | copy-start | bytes 2654212
  177.5 5.7 %copy-start.25 = (bf16[384,768]{1,0:T(8,128)(2,1)S(1)}, bf16[384,768]{1,0:T(8,128)(2,1)}, u32[]{:S(2)}) copy-start(bf16[384,768]{1,0:T(8,128)(2,1)} %get-tuple-element.99) | copy-start | bytes 1769476
  177.6 5.7 %copy-start.30 = (bf16[4,2,48,384]{3,2,1,0:T(8,128)(2,1)S(1)}, bf16[4,2,48,384]{3,2,1,0:T(8,128)(2,1)}, u32[]{:S(2)}) copy-start(bf16[4,2,48,384]{3,2,1,0:T(8,128)(2,1)} %copy-done.29) | copy-start | bytes 884740
  180.3 6.3 %copy-start.14 = (bf16[384,1536]{1,0:T(8,128)(2,1)S(1)}, bf16[384,1536]{1,0:T(8,128)(2,1)}, u32[]{:S(2)}) copy-start(bf16[384,1536]{1,0:T(8,128)(2,1)} %copy-done.13) | copy-start | bytes 3538948
  181.5 6.1 %copy-start.6 = (bf16[4,1,48,1152]{3,2,0,1:T(8,128)(2,1)}, bf16[4,1,48,1152]{3,2,0,1:T(8,128)(2,1)S(1)}, u32[]{:S(2)}) copy-start(bf16[4,1,48,1152]{3,2,0,1:T(8,128)(2,1)S(1)} %add_convert_fusion.3) | copy-start | bytes 1327108
  181.5 5.1 %copy-start.12 = (bf16[384,1536]{1,0:T(8,128)(2,1)S(1)}, bf16[384,1536]{1,0:T(8,128)(2,1)}, u32[]{:S(2)}) copy-start(bf16[384,1536]{1,0:T(8,128)(2,1)} %get-tuple-element.95) | copy-start | bytes 3538948
  181.5 15.3 %collective-permute-start.14 = (bf16[4,1,48,1152]{3,2,0,1:T(8,128)(2,1)S(1)}, bf16[4,1,48,1152]{3,2,0,1:T(8,128)(2,1)S(1)}, u32[]{:S(2)}, u32[]{:S(2)}) collective-permute-start(bf16[4,1,48,1152]{3,2,0,1:T(8,128)(2,1)S(1)} %add_convert_fusion.3), channel_id=1, source_target_pairs={{0,2},{1,3},{2,0},{3,1},{4,6},{5,7},{6,4},{7,5},{8,10},{9,11},{10,... | collective-permute-start | bytes 1327112 | tf_op jit(solution)/shard_map/ppermute | solution.py:415
  184.2 3.4 %copy-start.24 = (bf16[4,1,48,384]{3,2,1,0:T(8,128)(2,1)}, bf16[4,1,48,384]{3,2,1,0:T(8,128)(2,1)S(1)}, u32[]{:S(2)}) copy-start(bf16[4,1,48,384]{3,2,1,0:T(8,128)(2,1)S(1)} %add_convert_fusion.10.refs_7_) | copy-start | bytes 442372
  184.3 19.8 %collective-permute-start.17 = (bf16[4,1,48,384]{3,2,1,0:T(8,128)(2,1)S(1)}, bf16[4,1,48,384]{3,2,1,0:T(8,128)(2,1)S(1)}, u32[]{:S(2)}, u32[]{:S(2)}) collective-permute-start(bf16[4,1,48,384]{3,2,1,0:T(8,128)(2,1)S(1)} %add_convert_fusion.10.refs_7_), channel_id=1, source_target_pairs={{0,2},{1,3},{2,0},{3,1},{4,6},{5,7},{6,4},{7,5},{8,10},{9,11},{10,... | collective-permute-start | bytes 442376 | tf_op jit(solution)/shard_map/ppermute | solution.py:415
  185.8 3.5 %copy-start.8 = (bf16[4,1,48,768]{3,2,1,0:T(8,128)(2,1)}, bf16[4,1,48,768]{3,2,1,0:T(8,128)(2,1)S(1)}, u32[]{:S(2)}) copy-start(bf16[4,1,48,768]{3,2,1,0:T(8,128)(2,1)S(1)} %add_convert_fusion.7.refs_5_) | copy-start | bytes 884740
  185.9 18.2 %collective-permute-start.15 = (bf16[4,1,48,768]{3,2,1,0:T(8,128)(2,1)S(1)}, bf16[4,1,48,768]{3,2,1,0:T(8,128)(2,1)S(1)}, u32[]{:S(2)}, u32[]{:S(2)}) collective-permute-start(bf16[4,1,48,768]{3,2,1,0:T(8,128)(2,1)S(1)} %add_convert_fusion.7.refs_5_), channel_id=1, source_target_pairs={{0,16},{16,0},{1,17},{17,1},{2,18},{18,2},{3,19},{19,3},{4,20},{20... | collective-permute-start | bytes 884744 | tf_op jit(solution)/shard_map/ppermute | solution.py:445
  187.7 16.4 %collective-permute-start.16 = (bf16[4,1,48,768]{3,2,1,0:T(8,128)(2,1)S(1)}, bf16[4,1,48,768]{3,2,1,0:T(8,128)(2,1)}, u32[]{:S(2)}, u32[]{:S(2)}) collective-permute-start(bf16[4,1,48,768]{3,2,1,0:T(8,128)(2,1)S(1)} %add_convert_fusion.6.refs_6_), channel_id=1, source_target_pairs={{0,2},{1,3},{2,0},{3,1},{4,6},{5,7},{6,4},{7,5},{8,10},{9,11},{10,... | collective-permute-start | bytes 884744 | tf_op jit(solution)/shard_map/ppermute | solution.py:415
  195.4 25.8 %collective-permute-start.18 = (bf16[512,768]{1,0:T(8,128)(2,1)}, bf16[512,768]{1,0:T(8,128)(2,1)S(1)}, u32[]{:S(2)}, u32[]{:S(2)}) collective-permute-start(bf16[512,768]{1,0:T(8,128)(2,1)} %get-tuple-element.120), channel_id=1, source_target_pairs={{0,16},{16,0},{1,17},{17,1},{2,18},{18,2},{3,19},{19,3},{4,20},{20... | collective-permute-start | bytes 2359304 | tf_op jit(solution)/shard_map/ppermute | solution.py:677
  207.5 8.7 %copy-start.20 = (bf16[48,1920]{1,0:T(8,128)(2,1)}, bf16[48,1920]{1,0:T(8,128)(2,1)S(1)}, u32[]{:S(2)}) copy-start(bf16[48,1920]{1,0:T(8,128)(2,1)S(1)} %get-tuple-element.138.refs_4_) | copy-start | bytes 552964
  207.5 8.7 %copy-start.21 = (bf16[48,1920]{1,0:T(8,128)(2,1)}, bf16[48,1920]{1,0:T(8,128)(2,1)S(1)}, u32[]{:S(2)}) copy-start(bf16[48,1920]{1,0:T(8,128)(2,1)S(1)} %get-tuple-element.137.refs_5_) | copy-start | bytes 552964
  207.5 8.7 %copy-start.22 = (bf16[48,1920]{1,0:T(8,128)(2,1)}, bf16[48,1920]{1,0:T(8,128)(2,1)S(1)}, u32[]{:S(2)}) copy-start(bf16[48,1920]{1,0:T(8,128)(2,1)S(1)} %get-tuple-element.136.refs_6_) | copy-start | bytes 552964
  207.6 21.6 %collective-permute-start.23 = (bf16[48,1920]{1,0:T(8,128)(2,1)S(1)}, bf16[48,1920]{1,0:T(8,128)(2,1)S(1)}, u32[]{:S(2)}, u32[]{:S(2)}) collective-permute-start(bf16[48,1920]{1,0:T(8,128)(2,1)S(1)} %get-tuple-element.136.refs_6_), channel_id=1, source_target_pairs={{0,12},{1,13},{2,14},{3,15},{4,8},{5,9},{6,10},{7,11},{8,4},{9,5},... | collective-permute-start | bytes 552968 | tf_op jit(solution)/shard_map/ppermute | solution.py:415
  210.3 26.5 %collective-permute-start.22 = (bf16[48,1920]{1,0:T(8,128)(2,1)S(1)}, bf16[48,1920]{1,0:T(8,128)(2,1)S(1)}, u32[]{:S(2)}, u32[]{:S(2)}) collective-permute-start(bf16[48,1920]{1,0:T(8,128)(2,1)S(1)} %get-tuple-element.137.refs_5_), channel_id=1, source_target_pairs={{0,8},{1,9},{2,10},{3,11},{4,12},{5,13},{6,14},{7,15},{8,0},{9,1},... | collective-permute-start | bytes 552968 | tf_op jit(solution)/shard_map/ppermute | solution.py:415
  210.3 26.5 %collective-permute-start.21 = (bf16[48,1920]{1,0:T(8,128)(2,1)S(1)}, bf16[48,1920]{1,0:T(8,128)(2,1)S(1)}, u32[]{:S(2)}, u32[]{:S(2)}) collective-permute-start(bf16[48,1920]{1,0:T(8,128)(2,1)S(1)} %get-tuple-element.138.refs_4_), channel_id=1, source_target_pairs={{0,4},{1,5},{2,6},{3,7},{4,0},{5,1},{6,2},{7,3},{8,12},{9,13},{10,... | collective-permute-start | bytes 552968 | tf_op jit(solution)/shard_map/ppermute | solution.py:415
  212.0 29.2 %all-to-all-start = ((bf16[4,48,1152]{2,1,0:T(8,128)(2,1)}), bf16[4,48,1152]{2,1,0:T(8,128)(2,1)S(1)}, u32[]{:S(2)}, u32[]{:S(2)}) async-start(bf16[4,48,1152]{2,1,0:T(8,128)(2,1)} %fusion.refs_5_), calls=%async_computation | async-start | bytes 884736 | tf_op jit(solution)/shard_map/all_to_all | solution.py:420
  227.6 21.2 %collective-permute-start.20 = (bf16[48,3072]{1,0:T(8,128)(2,1)}, bf16[48,3072]{1,0:T(8,128)(2,1)S(1)}, u32[]{:S(2)}, u32[]{:S(2)}) collective-permute-start(bf16[48,3072]{1,0:T(8,128)(2,1)} %reduce-scatter.2.cloned.1.call-done.refs_1_), channel_id=1, source_target_pairs={{0,16},{16,0},{1,17},{17,1},{2,18},{18,2},{3,19},{19,3},{4,20},{20... | collective-permute-start | bytes 884744 | tf_op jit(solution)/shard_map/ppermute | solution.py:735
  236.8 12.0 %copy-start.23 = (bf16[48,1920]{1,0:T(8,128)(2,1)}, bf16[48,1920]{1,0:T(8,128)(2,1)S(1)}, u32[]{:S(2)}) copy-start(bf16[48,1920]{1,0:T(8,128)(2,1)S(1)} %fusion.3.refs_3_) | copy-start | bytes 552964
  236.9 12.0 %collective-permute-start.24 = (bf16[48,1920]{1,0:T(8,128)(2,1)S(1)}, bf16[48,1920]{1,0:T(8,128)(2,1)S(1)}, u32[]{:S(2)}, u32[]{:S(2)}) collective-permute-start(bf16[48,1920]{1,0:T(8,128)(2,1)S(1)} %fusion.3.refs_3_), channel_id=1, source_target_pairs={{0,16},{16,0},{1,17},{17,1},{2,18},{18,2},{3,19},{19,3},{4,20},{20... | collective-permute-start | bytes 552968 | tf_op jit(solution)/shard_map/ppermute | solution.py:735
  241.2 4.9 %copy-start.26 = (bf16[48,1152]{1,0:T(8,128)(2,1)}, bf16[48,1152]{1,0:T(8,128)(2,1)S(1)}, u32[]{:S(2)}) copy-start(bf16[48,1152]{1,0:T(8,128)(2,1)S(1)} %reduce_sum.12.refs_1_) | copy-start | bytes 331780
  241.3 4.8 %collective-permute-start.19 = (bf16[48,1152]{1,0:T(8,128)(2,1)S(1)}, bf16[48,1152]{1,0:T(8,128)(2,1)S(1)}, u32[]{:S(2)}, u32[]{:S(2)}) collective-permute-start(bf16[48,1152]{1,0:T(8,128)(2,1)S(1)} %reduce_sum.12.refs_1_), channel_id=1, source_target_pairs={{0,16},{16,0},{1,17},{17,1},{2,18},{18,2},{3,19},{19,3},{4,20},{20... | collective-permute-start | bytes 331784 | tf_op jit(solution)/shard_map/ppermute | solution.py:735
  (16 other events, 17.1 us)
Sparse Core Ops, SparseCore 0:
  12.1 96.6 all-gather.1
  142.5 85.0 reduce-scatter.1

commit v2 on v1

--- a/solution.py
+++ b/solution.py
@@ -283,7 +283,7 @@
 
 def feed(
     meta, own, mixed, gains, weight, up, down, upstream,
-    active, dpre, zt_natural, zt, resid, dresid, db, away, mine_out, zb, g_total,
+    active, dpre, first, zt, resid, dresid, db, away, mine_out, zb, zt_natural, g_total, turned,
 ):
     step = pl.program_id(0)
     gain = gains[1:2, :].astype(F32)
@@ -311,6 +311,12 @@
         dpre[:, mine] = (slope_in * slope).astype(BF16)
     added(step, g_total, None, dot_t(dpre[...], up[...]))
 
+    @pl.when(step < 2)
+    def _():
+        turned[...] = active[...].T
+        first[:, :width] = dot(zt_natural[...], dpre[...]).astype(BF16)
+        first[:, width:] = dot(turned[...], upstream[...]).astype(BF16)
+
     @pl.when(step == pl.num_programs(0) - 1)
     def _():
         z, rstd = standardize(resid[...])
@@ -323,30 +329,21 @@
 
 
 def hidden_back(
-    meta, zt_natural, zt, active, dpre, upstream, mt, db,
-    first, up_keep, up_send, down_keep, down_send, mixed_keep, mixed_send, turned, picked,
+    meta, zt, active, dpre, upstream, mt, db,
+    up_keep, up_send, down_keep, down_send, mixed_keep, mixed_send, turned, picked,
 ):
     step = pl.program_id(0)
     width = active.shape[1]
     turned[...] = active[...].T
-
-    @pl.when(step < 2)
-    def _():
-        first[:, :width] = dot(zt_natural[...], dpre[...]).astype(BF16)
-        first[:, width:] = dot(turned[...], upstream[...]).astype(BF16)
-
-    @pl.when(step >= 2)
-    def _():
-        rows_in_order(meta, turned, picked)
-        size = width // 2
-        for spot, (up_part, down_part) in enumerate(((up_keep, down_keep), (up_send, down_send))):
-            mine = slice(spot * size, (spot + 1) * size)
-            up_part[...] = dot(zt[mine, :], dpre[...]).astype(BF16)
-            down_part[...] = dot(picked[mine, :], upstream[...]).astype(BF16)
+    rows_in_order(meta, turned, picked)
+    size = width // 2
+    for spot, (up_part, down_part) in enumerate(((up_keep, down_keep), (up_send, down_send))):
+        mine = slice(spot * size, (spot + 1) * size)
+        up_part[...] = dot(zt[mine, :], dpre[...]).astype(BF16)
+        down_part[...] = dot(picked[mine, :], upstream[...]).astype(BF16)
 
     @pl.when(step == pl.num_programs(0) - 1)
     def _():
-        size = width // 2
         mixed_send[...] = dot(mt[size:, :], db[...]).astype(BF16)
         mixed_keep[...] = dot(mt[:size, :], db[...]).astype(BF16)
 
@@ -555,17 +552,21 @@
     total_f32 = shaped(half, dim, dtype=F32)
     tokens = whole(half, dim)
 
-    later = column(chunk, dim, lambda k: jnp.maximum(k - 2, 0))
     turned = whole(dim, half)
-    active, dpre, zt_natural, zt_two, resid, dresid, db, dm_away, dm_mine = call(
+    active, dpre, grad_first, zt_two, resid, dresid, db, dm_away, dm_mine = call(
         feed,
         "feed",
         (shaped(half, wide),) * 2
-        + (shaped(dim, half),) * 2
+        + (shaped(dim, 4 * dim), shaped(dim, half))
         + (total_f32, total_f32, shaped(half, dim), shaped(half, group), shaped(half, group)),
         meta,
         (own, mixed, gains, rest, rest, rest, upstream),
-        [pltpu.VMEM((half, dim), BF16), pltpu.VMEM((half, dim), F32)],
+        [
+            pltpu.VMEM((half, dim), BF16),
+            pltpu.VMEM((dim, half), BF16),
+            pltpu.VMEM((half, dim), F32),
+            pltpu.VMEM((dim, half), BF16),
+        ],
         took=20,
         grid=(4,),
         specs=[
@@ -577,20 +578,22 @@
             column(dim, dim, lambda k: 2 + 2 * k),
             tokens,
         ],
-        out_specs=[column(half, dim)] * 2 + [turned] * 2 + [tokens] * 3 + [whole(half, group)] * 2,
+        out_specs=[column(half, dim)] * 2
+        + [column(dim, 2 * dim, lambda k: jnp.minimum(k, 1)), turned]
+        + [tokens] * 3 + [whole(half, group)] * 2,
     )
     dm_came = lax.ppermute(dm_away, "seq", SWAP)
-    grad_first, up_keep, up_send, down_keep, down_send, mixed_keep, mixed_send = call(
+    up_keep, up_send, down_keep, down_send, mixed_keep, mixed_send = call(
         hidden_back,
         "hidden_back",
-        (shaped(dim, 4 * dim),) + (shaped(chunk, 2 * dim),) * 4 + (shaped(chunk, dim),) * 2,
+        (shaped(chunk, 2 * dim),) * 4 + (shaped(chunk, dim),) * 2,
         meta,
-        (zt_natural, zt_two, active, dpre, upstream, mixed_t, db),
+        (zt_two, active, dpre, upstream, mixed_t, db),
         [pltpu.VMEM((dim, half), BF16), pltpu.VMEM((dim, half), BF16)],
-        took=12,
-        grid=(4,),
-        specs=[turned, turned, column(half, dim), column(half, dim), tokens, turned, tokens],
-        out_specs=[column(dim, 2 * dim, lambda k: jnp.minimum(k, 1))] + [later] * 4 + [whole(chunk, dim)] * 2,
+        took=7,
+        grid=(2,),
+        specs=[turned] + [column(half, dim, lambda k: k + 2)] * 2 + [tokens, turned, tokens],
+        out_specs=[column(chunk, dim)] * 4 + [whole(chunk, dim)] * 2,
     )
     dm_came = pinned(dm_came, up_keep)
 
@@ -599,7 +602,7 @@
 
     marks = [[], [], []]
     if direct:
-        first_sum = lax.psum_scatter(pinned(grad_first, dm_came), "fsdp", scatter_dimension=0, tiled=True)
+        first_sum = lax.psum_scatter(grad_first, "fsdp", scatter_dimension=0, tiled=True)
         up_came, down_came, mixed_came = (
             flipped(pinned(part, dm_came), parts, 1) for part in (up_send, down_send, mixed_send)
         )

time: 264 us -> 261 us (0.989)
  waiting for transfers between devices: 63.8 us -> 69.8 us
  starting transfers between devices: 33.4 us -> 28.8 us
    ppermute x15, waiting for transfers between devices: 39.4 us -> 43.4 us  [flipped(): lax.ppermute(array, 'fsdp', [(spot, spot ^ bit) for spot in range(parts)])]
    ppermute x3, starting transfers between devices: 4.56 us -> 1.32 us  [body(): lax.ppermute(part, 'seq', SWAP)]
    unnamed x82 -> x80, local copies, waits for them, and re-layouts: 8.4 us -> 7.28 us
  transfers between devices with their start and end apart: 28 -> 28, of which waited for: 10 -> 12; matrix products, arithmetic and copies ran while one was open for 5% -> 5% of each run, Pallas kernels for 39% -> 37%
where the time goes in v2:
time: 261 us; the launch traced here: 256 us
  Pallas kernels  120 us (46%)
  waiting for transfers between devices  69.8 us (27%)
  starting transfers between devices  28.8 us (11%)
  between operations  15.3 us (6%)
  other arithmetic  11.3 us (4%)
  local copies, waits for them, and re-layouts  10.9 us (4%)
    pallas_call x16, Pallas kernels, call(): pl.pallas_call(waiting(kernel, 1 + len(inputs), len(after)), name=name, g...  120 us
    ppermute x15, waiting for transfers between devices, flipped(): lax.ppermute(array, 'fsdp', [(spot, spot ^ bit) for spot in range(parts)])  43.4 us
    ppermute x15, starting transfers between devices, flipped(): lax.ppermute(array, 'fsdp', [(spot, spot ^ bit) for spot in range(parts)])  14.9 us
    all_gather x1, waiting for transfers between devices, body(): lax.all_gather(jnp.concatenate([output_weight, *hidden], axis=1), 'fsdp',...  10.6 us
    convert_element_type x11, other arithmetic, rounded_sum(): return total.astype(BF16)  9.41 us
    unnamed x80, local copies, waits for them, and re-layouts  7.28 us
    ppermute x1, waiting for transfers between devices, body(): o_came = lax.ppermute(o_other, 'seq', SWAP)  6.7 us
  transfers between devices with their start and end apart: 28, of which 12 were waited for; matrix products, arithmetic and copies ran while one was open for 5% of the time, Pallas kernels for 37%

profile of v2, /device:TPU:0, one launch (start us, length us, event | category | flops | bytes accessed | tf_op | source)
XLA Modules:
  0.0 256.3 jit_solution(5784740468718380132)
XLA Ops:
  8.1 1.7 reshape.88
  12.9 4.1 %collective-permute-start = (bf16[48,1280]{1,0:T(8,128)(2,1)S(1)}, bf16[48,1280]{1,0:T(8,128)(2,1)S(1)}, u32[]{:S(2)}, u32[]{:S(2)}) collective-permute-start(bf16[48,1280]{1,0:T(8,128)(2,1)S(1)} %pad_maximum_fusion.3), channel_id=1, source_target_pairs={{0,8},{1,9},{2,10},{3,11},{4,12},{5,13},{6,14},{7,15},{8,0},{9,1},... | collective-permute-start | bytes 368648 | tf_op jit(solution)/shard_map/ppermute | solution.py:412
  17.0 1.5 collective-permute-start.2
  18.5 4.4 %collective-permute-done = bf16[48,1280]{1,0:T(8,128)(2,1)S(1)} collective-permute-done((bf16[48,1280]{1,0:T(8,128)(2,1)S(1)}, bf16[48,1280]{1,0:T(8,128)(2,1)S(1)}, u32[]{:S(2)}, u32[]{:S(2)}) %collective-permute-start) | collective-permute-done | bytes 122912 | tf_op jit(solution)/shard_map/ppermute | solution.py:412
  23.7 17.1 %collective-permute-done.1 = bf16[96,1280]{1,0:T(8,128)(2,1)S(1)} collective-permute-done((bf16[96,1280]{1,0:T(8,128)(2,1)S(1)}, bf16[96,1280]{1,0:T(8,128)(2,1)S(1)}, u32[]{:S(2)}, u32[]{:S(2)}) %collective-permute-start.1) | collective-permute-done | bytes 245792 | tf_op jit(solution)/shard_map/ppermute | solution.py:412
  40.9 1.3 collective-permute-start.3
  42.2 7.6 %collective-permute-done.3 = bf16[192,1280]{1,0:T(8,128)(2,1)S(1)} collective-permute-done((bf16[192,1280]{1,0:T(8,128)(2,1)S(1)}, bf16[192,1280]{1,0:T(8,128)(2,1)S(1)}, u32[]{:S(2)}, u32[]{:S(2)}) %collective-permute-start.3) | collective-permute-done | bytes 491552 | tf_op jit(solution)/shard_map/ppermute | solution.py:412
  50.7 4.0 %first_norm.1.refs_1_ = f32[1024,768]{1,0:T(8,128)} custom-call(s32[33]{0:T(128)} %pad_add_fusion.refs_0_, bf16[512,768]{1,0:T(8,128)(2,1)} %bitcast.63, bf16[512,768]{1,0:T(8,128)(2,1)} %copy-done.16), custom_call_target="tpu_custom_call" | custom-call | flops 30000000 | bytes 90000 | tf_op jit(solution)/shard_map/first_norm/pallas_call | solution.py:56
  55.7 3.6 %first_scale.1 = (bf16[1024,768]{1,0:T(8,128)(2,1)}, bf16[16,768]{1,0:T(8,128)(2,1)}) custom-call(s32[33]{0:T(128)} %pad_add_fusion.refs_0_, f32[1024,768]{1,0:T(8,128)} %first_norm.1.refs_1_, bf16[384,1280]{1,0:T(8,128)(2,1)} %copy-done.1, bf16[384,1280]{1,0:T(8,128)(2,1)} %copy-done.2), custom_call_target="tpu_custom_call" | custom-call | flops 20000000 | bytes 60000 | tf_op jit(solution)/shard_map/first_scale/pallas_call | solution.py:56
  59.3 24.2 %attend.1 = (bf16[1024,1152]{1,0:T(8,128)(2,1)}, bf16[512,384]{1,0:T(8,128)(2,1)}, bf16[512,384]{1,0:T(8,128)(2,1)}, f32[3,8,1024]{2,1,0:T(8,128)}, bf16[768,1152]{1,0:T(8,128)(2,1)}) custom-call(s32[33]{0:T(128)} %pad_add_fusion.refs_0_, bf16[1024,768]{1,0:T(8,128)(2,1)} %get-tuple-element.70.refs_1_, bf16[384,1280]{1,0:T(8,128)(2,1)} %copy-done.1, ...), custom_call_target="tpu_custom_call" | custom-call | flops 220000000 | bytes 660000 | tf_op jit(solution)/shard_map/attend/pallas_call | solution.py:56
  83.5 1.7 collective-permute-start.5
  85.2 3.3 %turn.1.refs_3_.refs_7_ = bf16[768,1024]{1,0:T(8,128)(2,1)} custom-call(s32[33]{0:T(128)} %pad_add_fusion.refs_0_, bf16[1024,768]{1,0:T(8,128)(2,1)} %get-tuple-element.70.refs_1_, f32[3,8,1024]{2,1,0:T(8,128)} %get-tuple-element.73.refs_2_.refs_6_), custom_call_target="tpu_custom_call" | custom-call | flops 20000000 | bytes 60000 | tf_op jit(solution)/shard_map/turn/pallas_call | solution.py:56
  88.4 6.7 %collective-permute-done.5.refs_2_ = bf16[512,384]{1,0:T(8,128)(2,1)S(1)} collective-permute-done((bf16[512,384]{1,0:T(8,128)(2,1)}, bf16[512,384]{1,0:T(8,128)(2,1)S(1)}, u32[]{:S(2)}, u32[]{:S(2)}) %collective-permute-start.5) | collective-permute-done | bytes 393248 | tf_op jit(solution)/shard_map/ppermute | solution.py:538
  95.9 2.4 mix.1
  98.3 10.6 %all-gather.2.cloned.1.call-done.refs_4_.refs_5_.refs_6_.refs_3_ = bf16[768,6912]{1,0:T(8,128)(2,1)} async-done(((bf16[48,6912]{1,0:T(8,128)(2,1)}), bf16[768,6912]{1,0:T(8,128)(2,1)}) %all-gather.2.cloned.1.call-update) | async-done | bytes 10616848 | tf_op jit(solution)/shard_map/all_gather | solution.py:485
  108.8 21.9 %feed.1 = (bf16[512,3072]{1,0:T(8,128)(2,1)}, bf16[512,3072]{1,0:T(8,128)(2,1)}, bf16[768,3072]{1,0:T(8,128)(2,1)}, bf16[768,512]{1,0:T(8,128)(2,1)}, f32[512,76...) custom-call(s32[33]{0:T(128)} %pad_add_fusion.refs_0_, ...), custom_call_target="tpu_custom_call" | custom-call | flops 200000000 | bytes 600000 | tf_op jit(solution)/shard_map/feed/pallas_call | solution.py:56
  130.8 1.0 copy-done.34
  131.7 1.5 collective-permute-start.6
  133.2 8.2 %hidden_back.1 = (bf16[384,1536]{1,0:T(8,128)(2,1)}, bf16[384,1536]{1,0:T(8,128)(2,1)}, bf16[384,1536]{1,0:T(8,128)(2,1)}, bf16[384,1536]{1,0:T(8,128)(2,1)}, bf...) custom-call(s32[33]{0:T(128)} %pad_add_fusion.refs_0_, bf16[768,512]{1,0:T(8,128)(2,1)} %get-tuple-element.81.refs_1_, ...), custom_call_target="tpu_custom_call" | custom-call | flops 70000000 | bytes 210000 | tf_op jit(solution)/shard_map/hidden_back/pallas_call | solution.py:56
  141.4 1.6 collective-permute-done.6.refs_5_
  143.8 8.6 %attend_back.3 = (bf16[384,384]{1,0:T(8,128)(2,1)}, bf16[384,384]{1,0:T(8,128)(2,1)}, bf16[1024,384]{1,0:T(8,128)(2,1)}) custom-call(s32[33]{0:T(128)} %pad_add_fusion.refs_0_, bf16[1024,1152]{1,0:T(8,128)(2,1)} %get-tuple-element.78.refs_1_, bf16[512,384]{1,0:T(8,128)(2,1)} %get-tuple-element.71.refs_1_.refs_2_, ...), custom_call_target="tpu_custom_call" | custom-call | flops 100000000 | bytes 300000 | tf_op jit(solution)/shard_map/attend_back/pallas_call | solution.py:56
  152.4 1.3 add_convert_fusion.refs_10_
  153.8 1.5 collective-permute-start.11
  156.1 1.1 add_convert_fusion.8.refs_11_
  157.9 8.3 %attend_back.4 = (bf16[384,384]{1,0:T(8,128)(2,1)}, bf16[384,384]{1,0:T(8,128)(2,1)}, bf16[1024,384]{1,0:T(8,128)(2,1)}) custom-call(s32[33]{0:T(128)} %pad_add_fusion.refs_0_, bf16[1024,1152]{1,0:T(8,128)(2,1)} %get-tuple-element.78.refs_1_, bf16[512,384]{1,0:T(8,128)(2,1)} %get-tuple-element.71.refs_1_.refs_2_, ...), custom_call_target="tpu_custom_call" | custom-call | flops 100000000 | bytes 300000 | tf_op jit(solution)/shard_map/attend_back/pallas_call | solution.py:56
  166.3 9.7 %attend_back.5 = (bf16[384,1152]{1,0:T(8,128)(2,1)}, bf16[384,1152]{1,0:T(8,128)(2,1)}, bf16[1024,384]{1,0:T(8,128)(2,1)}) custom-call(s32[33]{0:T(128)} %pad_add_fusion.refs_0_, bf16[1024,1152]{1,0:T(8,128)(2,1)} %get-tuple-element.78.refs_1_, bf16[512,384]{1,0:T(8,128)(2,1)} %get-tuple-element.71.refs_1_.refs_2_, ...), custom_call_target="tpu_custom_call" | custom-call | flops 100000000 | bytes 300000 | tf_op jit(solution)/shard_map/attend_back/pallas_call | solution.py:56
  176.0 2.6 %collective-permute-done.10 = bf16[4,1,48,1536]{3,2,1,0:T(8,128)(2,1)} collective-permute-done((bf16[4,1,48,1536]{3,2,1,0:T(8,128)(2,1)S(1)}, bf16[4,1,48,1536]{3,2,1,0:T(8,128)(2,1)}, u32[]{:S(2)}, u32[]{:S(2)}) %collective-permute-start.10) | collective-permute-done | bytes 589856 | tf_op jit(solution)/shard_map/ppermute | solution.py:412
  178.7 2.5 collective-permute-done.13
  182.2 1.0 add_convert_fusion.10.refs_7_
  183.2 1.3 collective-permute-start.17
  184.5 1.1 add_convert_fusion.7.refs_5_
  185.7 1.2 add_convert_fusion.6.refs_6_
  187.9 6.1 %token_back.1 = (bf16[512,768]{1,0:T(8,128)(2,1)}, f32[512,768]{1,0:T(8,128)}) custom-call(s32[33]{0:T(128)} %pad_add_fusion.refs_0_, bf16[1024,384]{1,0:T(8,128)(2,1)} %get-tuple-element.88.refs_12_.refs_1_, bf16[1024,384]{1,0:T(8,128)(2,1)} %get-tuple-element.100.refs_13_.refs_2_, bf16[1024,384]{1,0:T(8,128)(2,1)} %get-tuple-element.105.refs_3_, ...), custom_call_target="tpu_custom_call" | custom-call | flops 50000000 | bytes 150000 | tf_op jit(solution)/shard_map/token_back/pallas_call | solution.py:56
  194.0 1.9 collective-permute-start.18
  196.8 5.4 %forward_out.2.refs_1_ = f32[512,768]{1,0:T(8,128)} custom-call(s32[33]{0:T(128)} %pad_add_fusion.refs_0_, f32[512,768]{1,0:T(8,128)} %get-tuple-element.76.refs_1_, bf16[512,3072]{1,0:T(8,128)(2,1)} %get-tuple-element.77.refs_2_, bf16[768,6912]{1,0:T(8,128)(2,1)} %all-gather.2.cloned.1.call-done.refs_4_.refs_5_.refs_6_.refs_3_, ...), custom_call_target="tpu_custom_call" | custom-call | flops 30000000 | bytes 90000 | tf_op jit(solution)/shard_map/forward_out/pallas_call | solution.py:56
  202.3 4.0 %collective-permute-done.16 = bf16[4,1,48,768]{3,2,1,0:T(8,128)(2,1)S(1)} collective-permute-done((bf16[4,1,48,768]{3,2,1,0:T(8,128)(2,1)S(1)}, bf16[4,1,48,768]{3,2,1,0:T(8,128)(2,1)S(1)}, u32[]{:S(2)}, u32[]{:S(2)}) %collective-permute-start.16) | collective-permute-done | bytes 294944 | tf_op jit(solution)/shard_map/ppermute | solution.py:412
  206.3 1.1 add_convert_fusion.5
  207.4 1.2 add_convert_fusion.4
  208.6 1.0 add_convert_fusion.9
  210.0 4.3 %collective-permute-start.21 = (bf16[48,1920]{1,0:T(8,128)(2,1)S(1)}, bf16[48,1920]{1,0:T(8,128)(2,1)S(1)}, u32[]{:S(2)}, u32[]{:S(2)}) collective-permute-start(bf16[48,1920]{1,0:T(8,128)(2,1)S(1)} %get-tuple-element.134.refs_4_), channel_id=1, source_target_pairs={{0,4},{1,5},{2,6},{3,7},{4,0},{5,1},{6,2},{7,3},{8,12},{9,13},{10,... | collective-permute-start | bytes 552968 | tf_op jit(solution)/shard_map/ppermute | solution.py:412
  214.3 3.8 %all-to-all-start = ((bf16[4,48,1152]{2,1,0:T(8,128)(2,1)}), bf16[4,48,1152]{2,1,0:T(8,128)(2,1)S(1)}, u32[]{:S(2)}, u32[]{:S(2)}) async-start(bf16[4,48,1152]{2,1,0:T(8,128)(2,1)} %fusion.refs_5_), calls=%async_computation | async-start | bytes 884736 | tf_op jit(solution)/shard_map/all_to_all | solution.py:417
  218.1 4.9 %forward_out.3.refs_6_ = bf16[512,768]{1,0:T(8,128)(2,1)} custom-call(s32[33]{0:T(128)} %pad_add_fusion.refs_0_, f32[512,768]{1,0:T(8,128)} %forward_out.2.refs_1_, bf16[512,3072]{1,0:T(8,128)(2,1)} %get-tuple-element.77.refs_2_, bf16[768,6912]{1,0:T(8,128)(2,1)} %all-gather.2.cloned.1.call-done.refs_4_.refs_5_.refs_6_.refs_3_, bf16[48,1920]{1,0:T(8,128)(2,1)} %copy-done.18, ...), custom_call_target="tpu_custom_call" | custom-call | flops 30000000 | bytes 90000 | tf_op jit(solution)/shard_map/forward_out/pallas_call | solution.py:56
  223.9 4.5 %input_back.1 = f32[512,768]{1,0:T(8,128)} custom-call(s32[33]{0:T(128)} %pad_add_fusion.refs_0_, bf16[512,768]{1,0:T(8,128)(2,1)} %bitcast.65, f32[512,768]{1,0:T(8,128)} %get-tuple-element.112.refs_4_.refs_2_, bf16[512,768]{1,0:T(8,128)(2,1)} %copy-done.17, f32[512,768]{1,0:T(8,128)} %get-tuple-element.118.refs_4_, ...), custom_call_target="tpu_custom_call" | custom-call | flops 40000000 | bytes 120000 | tf_op jit(solution)/shard_map/input_back/pallas_call | solution.py:56
  228.4 5.1 %collective-permute-done.22 = bf16[48,1920]{1,0:T(8,128)(2,1)S(1)} collective-permute-done((bf16[48,1920]{1,0:T(8,128)(2,1)S(1)}, bf16[48,1920]{1,0:T(8,128)(2,1)S(1)}, u32[]{:S(2)}, u32[]{:S(2)}) %collective-permute-start.22) | collective-permute-done | bytes 184352 | tf_op jit(solution)/shard_map/ppermute | solution.py:412
  234.2 3.4 %all-to-all-done = bf16[4,48,1152]{2,1,0:T(8,128)(2,1)S(1)} async-done(((bf16[4,48,1152]{2,1,0:T(8,128)(2,1)}), bf16[4,48,1152]{2,1,0:T(8,128)(2,1)S(1)}, u32[]{:S(2)}, u32[]{:S(2)}) %all-to-all-start) | async-done | bytes 442400 | tf_op jit(solution)/shard_map/all_to_all | solution.py:417
  238.5 4.1 %collective-permute-done.19.refs_2_ = bf16[48,1152]{1,0:T(8,128)(2,1)S(1)} collective-permute-done((bf16[48,1152]{1,0:T(8,128)(2,1)S(1)}, bf16[48,1152]{1,0:T(8,128)(2,1)S(1)}, u32[]{:S(2)}, u32[]{:S(2)}) %collective-permute-start.19) | collective-permute-done | bytes 110624 | tf_op jit(solution)/shard_map/ppermute | solution.py:738
  243.2 2.1 joint_out.1
  246.1 2.8 %feed_out.1 = (f32[48,3072]{1,0:T(8,128)}, f32[192,768]{1,0:T(8,128)}, f32[48,768]{1,0:T(8,128)}, f32[1,48]{1,0:T(1,128)}) custom-call(s32[33]{0:T(128)} %pad_add_fusion.refs_0_, bf16[48,3072]{1,0:T(8,128)(2,1)} %reduce-scatter.2.cloned.1.call-done.refs_1_, bf16[48,3072]{1,0:T(8,128)(2,1)} %copy-done.29, bf16[48,1920]{1,0:T(8,128)(2,1)} %copy-done.21, ...), custom_call_target="tpu_custom_call" | custom-call | flops 40000000 | bytes 120000 | tf_op jit(solution)/shard_map/feed_out/pallas_call | solution.py:56
  (147 shorter events, 16.6 us)
Async XLA Ops:
  7.2 101.7 %all-gather.2.cloned.1.call-start = ((), (), s32[]{:S(2)}) async-start(), calls=%async_computation.2 | async-start | bytes 11280384 | tf_op jit(solution)/shard_map/all_gather | solution.py:485
  12.0 5.0 %copy-start = (bf16[1,512,768]{2,1,0:T(8,128)(2,1)S(1)}, bf16[1,512,768]{2,1,0:T(8,128)(2,1)}, u32[]{:S(2)}) copy-start(bf16[1,512,768]{2,1,0:T(8,128)(2,1)} %param.8) | copy-start | bytes 2359300
  12.0 216.4 %reduce-scatter.2.cloned.1.call-start = ((), (), s32[]{:S(2)}) async-start(), calls=%async_computation.3 | async-start | bytes 5013504 | tf_op jit(solution)/shard_map/reduce_scatter | solution.py:605
  12.9 10.1 %collective-permute-start = (bf16[48,1280]{1,0:T(8,128)(2,1)S(1)}, bf16[48,1280]{1,0:T(8,128)(2,1)S(1)}, u32[]{:S(2)}, u32[]{:S(2)}) collective-permute-start(bf16[48,1280]{1,0:T(8,128)(2,1)S(1)} %pad_maximum_fusion.3), channel_id=1, source_target_pairs={{0,8},{1,9},{2,10},{3,11},{4,12},{5,13},{6,14},{7,15},{8,0},{9,1},... | collective-permute-start | bytes 368648 | tf_op jit(solution)/shard_map/ppermute | solution.py:412
  17.0 23.9 %collective-permute-start.2 = (bf16[512,768]{1,0:T(8,128)(2,1)S(1)}, bf16[512,768]{1,0:T(8,128)(2,1)S(1)}, u32[]{:S(2)}, u32[]{:S(2)}) collective-permute-start(bf16[512,768]{1,0:T(8,128)(2,1)S(1)} %bitcast.66), channel_id=1, source_target_pairs={{0,16},{16,0},{1,17},{17,1},{2,18},{18,2},{3,19},{19,3},{4,20},{20... | collective-permute-start | bytes 2359304 | tf_op jit(solution)/shard_map/ppermute | solution.py:486
  23.0 17.9 %collective-permute-start.1 = (bf16[96,1280]{1,0:T(8,128)(2,1)S(1)}, bf16[96,1280]{1,0:T(8,128)(2,1)S(1)}, u32[]{:S(2)}, u32[]{:S(2)}) collective-permute-start(bf16[96,1280]{1,0:T(8,128)(2,1)S(1)} %pad_maximum_fusion.2), channel_id=1, source_target_pairs={{0,4},{1,5},{2,6},{3,7},{4,0},{5,1},{6,2},{7,3},{8,12},{9,13},{10,... | collective-permute-start | bytes 737288 | tf_op jit(solution)/shard_map/ppermute | solution.py:412
  40.9 9.8 %copy-start.16 = (bf16[512,768]{1,0:T(8,128)(2,1)}, bf16[512,768]{1,0:T(8,128)(2,1)S(1)}, u32[]{:S(2)}) copy-start(bf16[512,768]{1,0:T(8,128)(2,1)S(1)} %collective-permute-done.2.refs_2_) | copy-start | bytes 2359300
  40.9 8.9 %collective-permute-start.3 = (bf16[192,1280]{1,0:T(8,128)(2,1)S(1)}, bf16[192,1280]{1,0:T(8,128)(2,1)S(1)}, u32[]{:S(2)}, u32[]{:S(2)}) collective-permute-start(bf16[192,1280]{1,0:T(8,128)(2,1)S(1)} %pad_maximum_fusion.1), channel_id=1, source_target_pairs={{0,2},{1,3},{2,0},{3,1},{4,6},{5,7},{6,4},{7,5},{8,10},{9,11},{10,... | collective-permute-start | bytes 1474568 | tf_op jit(solution)/shard_map/ppermute | solution.py:412
  49.9 4.9 %copy-start.1 = (bf16[384,1280]{1,0:T(8,128)(2,1)}, bf16[384,1280]{1,0:T(8,128)(2,1)S(1)}, u32[]{:S(2)}) copy-start(bf16[384,1280]{1,0:T(8,128)(2,1)S(1)} %constant_dynamic-update-slice_fusion.refs_2_) | copy-start | bytes 2949124
  49.9 4.9 %collective-permute-start.4 = (bf16[384,1280]{1,0:T(8,128)(2,1)S(1)}, bf16[384,1280]{1,0:T(8,128)(2,1)S(1)}, u32[]{:S(2)}, u32[]{:S(2)}) collective-permute-start(bf16[384,1280]{1,0:T(8,128)(2,1)S(1)} %constant_dynamic-update-slice_fusion.refs_2_), channel_id=1, source_target_pairs={{0,1},{1,0},{2,3},{3,2},{4,5},{5,4},{6,7},{7,6},{8,9},{9,8},{10,11... | collective-permute-start | bytes 2949128 | tf_op jit(solution)/shard_map/ppermute | solution.py:412
  83.5 11.7 %collective-permute-start.5 = (bf16[512,384]{1,0:T(8,128)(2,1)}, bf16[512,384]{1,0:T(8,128)(2,1)S(1)}, u32[]{:S(2)}, u32[]{:S(2)}) collective-permute-start(bf16[512,384]{1,0:T(8,128)(2,1)} %get-tuple-element.72.refs_3_), channel_id=1, source_target_pairs={{0,16},{16,0},{1,17},{17,1},{2,18},{18,2},{3,19},{19,3},{4,20},{20... | collective-permute-start | bytes 1179656 | tf_op jit(solution)/shard_map/ppermute | solution.py:538
  131.7 11.3 %collective-permute-start.6 = (bf16[512,384]{1,0:T(8,128)(2,1)S(1)}, bf16[512,384]{1,0:T(8,128)(2,1)S(1)}, u32[]{:S(2)}, u32[]{:S(2)}) collective-permute-start(bf16[512,384]{1,0:T(8,128)(2,1)S(1)} %copy-done.34), channel_id=1, source_target_pairs={{0,16},{16,0},{1,17},{17,1},{2,18},{18,2},{3,19},{19,3},{4,20},{20... | collective-permute-start | bytes 1179656 | tf_op jit(solution)/shard_map/ppermute | solution.py:585
  143.0 9.4 %collective-permute-start.8 = (bf16[384,1536]{1,0:T(8,128)(2,1)}, bf16[384,1536]{1,0:T(8,128)(2,1)}, u32[]{:S(2)}, u32[]{:S(2)}) collective-permute-start(bf16[384,1536]{1,0:T(8,128)(2,1)} %get-tuple-element.94), channel_id=1, source_target_pairs={{0,1},{1,0},{2,3},{3,2},{4,5},{5,4},{6,7},{7,6},{8,9},{9,8},{10,11... | collective-permute-start | bytes 3538952 | tf_op jit(solution)/shard_map/ppermute | solution.py:412
  143.0 9.4 %collective-permute-start.7 = (bf16[384,1536]{1,0:T(8,128)(2,1)}, bf16[384,1536]{1,0:T(8,128)(2,1)S(1)}, u32[]{:S(2)}, u32[]{:S(2)}) collective-permute-start(bf16[384,1536]{1,0:T(8,128)(2,1)} %get-tuple-element.90), channel_id=1, source_target_pairs={{0,1},{1,0},{2,3},{3,2},{4,5},{5,4},{6,7},{7,6},{8,9},{9,8},{10,11... | collective-permute-start | bytes 3538952 | tf_op jit(solution)/shard_map/ppermute | solution.py:412
  143.5 12.5 %collective-permute-start.9 = (bf16[384,768]{1,0:T(8,128)(2,1)}, bf16[384,768]{1,0:T(8,128)(2,1)}, u32[]{:S(2)}, u32[]{:S(2)}) collective-permute-start(bf16[384,768]{1,0:T(8,128)(2,1)} %get-tuple-element.98), channel_id=1, source_target_pairs={{0,1},{1,0},{2,3},{3,2},{4,5},{5,4},{6,7},{7,6},{8,9},{9,8},{10,11... | collective-permute-start | bytes 1769480 | tf_op jit(solution)/shard_map/ppermute | solution.py:412
  143.8 8.6 %copy-start.11 = (bf16[384,1536]{1,0:T(8,128)(2,1)S(1)}, bf16[384,1536]{1,0:T(8,128)(2,1)}, u32[]{:S(2)}) copy-start(bf16[384,1536]{1,0:T(8,128)(2,1)} %get-tuple-element.92) | copy-start | bytes 3538948
  152.4 2.9 %copy-start.10 = (bf16[384,1536]{1,0:T(8,128)(2,1)S(1)}, bf16[384,1536]{1,0:T(8,128)(2,1)}, u32[]{:S(2)}) copy-start(bf16[384,1536]{1,0:T(8,128)(2,1)} %get-tuple-element.85) | copy-start | bytes 3538948
  153.8 3.4 %copy-start.5 = (bf16[4,2,48,768]{3,2,1,0:T(8,128)(2,1)}, bf16[4,2,48,768]{3,2,1,0:T(8,128)(2,1)S(1)}, u32[]{:S(2)}) copy-start(bf16[4,2,48,768]{3,2,1,0:T(8,128)(2,1)S(1)} %add_convert_fusion.refs_10_) | copy-start | bytes 1769476
  153.8 22.2 %collective-permute-start.11 = (bf16[4,2,48,768]{3,2,1,0:T(8,128)(2,1)S(1)}, bf16[4,2,48,768]{3,2,1,0:T(8,128)(2,1)}, u32[]{:S(2)}, u32[]{:S(2)}) collective-permute-start(bf16[4,2,48,768]{3,2,1,0:T(8,128)(2,1)S(1)} %add_convert_fusion.refs_10_), channel_id=1, source_target_pairs={{0,16},{16,0},{1,17},{17,1},{2,18},{18,2},{3,19},{19,3},{4,20},{20... | collective-permute-start | bytes 1769480 | tf_op jit(solution)/shard_map/ppermute | solution.py:442
  155.4 2.4 copy-start.4
  155.4 23.2 %collective-permute-start.10 = (bf16[4,1,48,1536]{3,2,1,0:T(8,128)(2,1)S(1)}, bf16[4,1,48,1536]{3,2,1,0:T(8,128)(2,1)}, u32[]{:S(2)}, u32[]{:S(2)}) collective-permute-start(bf16[4,1,48,1536]{3,2,1,0:T(8,128)(2,1)S(1)} %add_convert_fusion.1.refs_9_), channel_id=1, source_target_pairs={{0,2},{1,3},{2,0},{3,1},{4,6},{5,7},{6,4},{7,5},{8,10},{9,11},{10,... | collective-permute-start | bytes 1769480 | tf_op jit(solution)/shard_map/ppermute | solution.py:412
  157.2 18.8 %collective-permute-start.12 = (bf16[4,2,48,384]{3,2,1,0:T(8,128)(2,1)S(1)}, bf16[4,2,48,384]{3,2,1,0:T(8,128)(2,1)S(1)}, u32[]{:S(2)}, u32[]{:S(2)}) collective-permute-start(bf16[4,2,48,384]{3,2,1,0:T(8,128)(2,1)S(1)} %add_convert_fusion.8.refs_11_), channel_id=1, source_target_pairs={{0,16},{16,0},{1,17},{17,1},{2,18},{18,2},{3,19},{19,3},{4,20},{20... | collective-permute-start | bytes 884744 | tf_op jit(solution)/shard_map/ppermute | solution.py:442
  176.0 2.6 %copy-start.27 = (bf16[4,2,48,384]{3,2,1,0:T(8,128)(2,1)}, bf16[4,2,48,384]{3,2,1,0:T(8,128)(2,1)S(1)}, u32[]{:S(2)}) copy-start(bf16[4,2,48,384]{3,2,1,0:T(8,128)(2,1)S(1)} %collective-permute-done.12) | copy-start | bytes 884740
  178.6 2.6 %collective-permute-start.13 = (bf16[384,1152]{1,0:T(8,128)(2,1)}, bf16[384,1152]{1,0:T(8,128)(2,1)S(1)}, u32[]{:S(2)}, u32[]{:S(2)}) collective-permute-start(bf16[384,1152]{1,0:T(8,128)(2,1)} %get-tuple-element.111), channel_id=1, source_target_pairs={{0,1},{1,0},{2,3},{3,2},{4,5},{5,4},{6,7},{7,6},{8,9},{9,8},{10,11... | collective-permute-start | bytes 2654216 | tf_op jit(solution)/shard_map/ppermute | solution.py:412
  178.6 2.6 %copy-start.13 = (bf16[384,1152]{1,0:T(8,128)(2,1)S(1)}, bf16[384,1152]{1,0:T(8,128)(2,1)}, u32[]{:S(2)}) copy-start(bf16[384,1152]{1,0:T(8,128)(2,1)} %get-tuple-element.110) | copy-start | bytes 2654212
  178.7 3.6 %copy-start.23 = (bf16[384,768]{1,0:T(8,128)(2,1)S(1)}, bf16[384,768]{1,0:T(8,128)(2,1)}, u32[]{:S(2)}) copy-start(bf16[384,768]{1,0:T(8,128)(2,1)} %get-tuple-element.96) | copy-start | bytes 1769476
  178.7 3.5 %copy-start.28 = (bf16[4,2,48,384]{3,2,1,0:T(8,128)(2,1)S(1)}, bf16[4,2,48,384]{3,2,1,0:T(8,128)(2,1)}, u32[]{:S(2)}) copy-start(bf16[4,2,48,384]{3,2,1,0:T(8,128)(2,1)} %copy-done.27) | copy-start | bytes 884740
  181.4 5.6 %copy-start.6 = (bf16[4,1,48,1152]{3,2,0,1:T(8,128)(2,1)}, bf16[4,1,48,1152]{3,2,0,1:T(8,128)(2,1)S(1)}, u32[]{:S(2)}) copy-start(bf16[4,1,48,1152]{3,2,0,1:T(8,128)(2,1)S(1)} %add_convert_fusion.3) | copy-start | bytes 1327108
  181.4 4.4 %copy-start.12 = (bf16[384,1536]{1,0:T(8,128)(2,1)S(1)}, bf16[384,1536]{1,0:T(8,128)(2,1)}, u32[]{:S(2)}) copy-start(bf16[384,1536]{1,0:T(8,128)(2,1)} %get-tuple-element.92) | copy-start | bytes 3538948
  181.4 14.5 %collective-permute-start.14 = (bf16[4,1,48,1152]{3,2,0,1:T(8,128)(2,1)S(1)}, bf16[4,1,48,1152]{3,2,0,1:T(8,128)(2,1)S(1)}, u32[]{:S(2)}, u32[]{:S(2)}) collective-permute-start(bf16[4,1,48,1152]{3,2,0,1:T(8,128)(2,1)S(1)} %add_convert_fusion.3), channel_id=1, source_target_pairs={{0,2},{1,3},{2,0},{3,1},{4,6},{5,7},{6,4},{7,5},{8,10},{9,11},{10,... | collective-permute-start | bytes 1327112 | tf_op jit(solution)/shard_map/ppermute | solution.py:412
  183.2 3.8 %copy-start.22 = (bf16[4,1,48,384]{3,2,1,0:T(8,128)(2,1)}, bf16[4,1,48,384]{3,2,1,0:T(8,128)(2,1)S(1)}, u32[]{:S(2)}) copy-start(bf16[4,1,48,384]{3,2,1,0:T(8,128)(2,1)S(1)} %add_convert_fusion.10.refs_7_) | copy-start | bytes 442372
  183.2 19.1 %collective-permute-start.17 = (bf16[4,1,48,384]{3,2,1,0:T(8,128)(2,1)S(1)}, bf16[4,1,48,384]{3,2,1,0:T(8,128)(2,1)S(1)}, u32[]{:S(2)}, u32[]{:S(2)}) collective-permute-start(bf16[4,1,48,384]{3,2,1,0:T(8,128)(2,1)S(1)} %add_convert_fusion.10.refs_7_), channel_id=1, source_target_pairs={{0,2},{1,3},{2,0},{3,1},{4,6},{5,7},{6,4},{7,5},{8,10},{9,11},{10,... | collective-permute-start | bytes 442376 | tf_op jit(solution)/shard_map/ppermute | solution.py:412
  185.6 2.3 copy-start.8
  185.6 20.7 %collective-permute-start.15 = (bf16[4,1,48,768]{3,2,1,0:T(8,128)(2,1)S(1)}, bf16[4,1,48,768]{3,2,1,0:T(8,128)(2,1)S(1)}, u32[]{:S(2)}, u32[]{:S(2)}) collective-permute-start(bf16[4,1,48,768]{3,2,1,0:T(8,128)(2,1)S(1)} %add_convert_fusion.7.refs_5_), channel_id=1, source_target_pairs={{0,16},{16,0},{1,17},{17,1},{2,18},{18,2},{3,19},{19,3},{4,20},{20... | collective-permute-start | bytes 884744 | tf_op jit(solution)/shard_map/ppermute | solution.py:442
  187.0 19.3 %collective-permute-start.16 = (bf16[4,1,48,768]{3,2,1,0:T(8,128)(2,1)S(1)}, bf16[4,1,48,768]{3,2,1,0:T(8,128)(2,1)S(1)}, u32[]{:S(2)}, u32[]{:S(2)}) collective-permute-start(bf16[4,1,48,768]{3,2,1,0:T(8,128)(2,1)S(1)} %add_convert_fusion.6.refs_6_), channel_id=1, source_target_pairs={{0,2},{1,3},{2,0},{3,1},{4,6},{5,7},{6,4},{7,5},{8,10},{9,11},{10,... | collective-permute-start | bytes 884744 | tf_op jit(solution)/shard_map/ppermute | solution.py:412
  194.0 29.0 %collective-permute-start.18 = (bf16[512,768]{1,0:T(8,128)(2,1)}, bf16[512,768]{1,0:T(8,128)(2,1)S(1)}, u32[]{:S(2)}, u32[]{:S(2)}) collective-permute-start(bf16[512,768]{1,0:T(8,128)(2,1)} %get-tuple-element.117), channel_id=1, source_target_pairs={{0,16},{16,0},{1,17},{17,1},{2,18},{18,2},{3,19},{19,3},{4,20},{20... | collective-permute-start | bytes 2359304 | tf_op jit(solution)/shard_map/ppermute | solution.py:680
  209.8 8.3 %copy-start.18 = (bf16[48,1920]{1,0:T(8,128)(2,1)}, bf16[48,1920]{1,0:T(8,128)(2,1)S(1)}, u32[]{:S(2)}) copy-start(bf16[48,1920]{1,0:T(8,128)(2,1)S(1)} %get-tuple-element.134.refs_4_) | copy-start | bytes 552964
  209.8 8.3 %copy-start.19 = (bf16[48,1920]{1,0:T(8,128)(2,1)}, bf16[48,1920]{1,0:T(8,128)(2,1)S(1)}, u32[]{:S(2)}) copy-start(bf16[48,1920]{1,0:T(8,128)(2,1)S(1)} %get-tuple-element.133.refs_5_) | copy-start | bytes 552964
  209.8 8.3 %copy-start.20 = (bf16[48,1920]{1,0:T(8,128)(2,1)}, bf16[48,1920]{1,0:T(8,128)(2,1)S(1)}, u32[]{:S(2)}) copy-start(bf16[48,1920]{1,0:T(8,128)(2,1)S(1)} %get-tuple-element.132.refs_6_) | copy-start | bytes 552964
  209.8 18.6 %collective-permute-start.23 = (bf16[48,1920]{1,0:T(8,128)(2,1)S(1)}, bf16[48,1920]{1,0:T(8,128)(2,1)S(1)}, u32[]{:S(2)}, u32[]{:S(2)}) collective-permute-start(bf16[48,1920]{1,0:T(8,128)(2,1)S(1)} %get-tuple-element.132.refs_6_), channel_id=1, source_target_pairs={{0,12},{1,13},{2,14},{3,15},{4,8},{5,9},{6,10},{7,11},{8,4},{9,5},... | collective-permute-start | bytes 552968 | tf_op jit(solution)/shard_map/ppermute | solution.py:412
  209.9 23.7 %collective-permute-start.22 = (bf16[48,1920]{1,0:T(8,128)(2,1)S(1)}, bf16[48,1920]{1,0:T(8,128)(2,1)S(1)}, u32[]{:S(2)}, u32[]{:S(2)}) collective-permute-start(bf16[48,1920]{1,0:T(8,128)(2,1)S(1)} %get-tuple-element.133.refs_5_), channel_id=1, source_target_pairs={{0,8},{1,9},{2,10},{3,11},{4,12},{5,13},{6,14},{7,15},{8,0},{9,1},... | collective-permute-start | bytes 552968 | tf_op jit(solution)/shard_map/ppermute | solution.py:412
  210.0 23.6 %collective-permute-start.21 = (bf16[48,1920]{1,0:T(8,128)(2,1)S(1)}, bf16[48,1920]{1,0:T(8,128)(2,1)S(1)}, u32[]{:S(2)}, u32[]{:S(2)}) collective-permute-start(bf16[48,1920]{1,0:T(8,128)(2,1)S(1)} %get-tuple-element.134.refs_4_), channel_id=1, source_target_pairs={{0,4},{1,5},{2,6},{3,7},{4,0},{5,1},{6,2},{7,3},{8,12},{9,13},{10,... | collective-permute-start | bytes 552968 | tf_op jit(solution)/shard_map/ppermute | solution.py:412
  214.3 23.4 %all-to-all-start = ((bf16[4,48,1152]{2,1,0:T(8,128)(2,1)}), bf16[4,48,1152]{2,1,0:T(8,128)(2,1)S(1)}, u32[]{:S(2)}, u32[]{:S(2)}) async-start(bf16[4,48,1152]{2,1,0:T(8,128)(2,1)} %fusion.refs_5_), calls=%async_computation | async-start | bytes 884736 | tf_op jit(solution)/shard_map/all_to_all | solution.py:417
  228.4 16.9 %collective-permute-start.20 = (bf16[48,3072]{1,0:T(8,128)(2,1)}, bf16[48,3072]{1,0:T(8,128)(2,1)S(1)}, u32[]{:S(2)}, u32[]{:S(2)}) collective-permute-start(bf16[48,3072]{1,0:T(8,128)(2,1)} %reduce-scatter.2.cloned.1.call-done.refs_1_), channel_id=1, source_target_pairs={{0,16},{16,0},{1,17},{17,1},{2,18},{18,2},{3,19},{19,3},{4,20},{20... | collective-permute-start | bytes 884744 | tf_op jit(solution)/shard_map/ppermute | solution.py:738
  233.6 11.7 %copy-start.21 = (bf16[48,1920]{1,0:T(8,128)(2,1)}, bf16[48,1920]{1,0:T(8,128)(2,1)S(1)}, u32[]{:S(2)}) copy-start(bf16[48,1920]{1,0:T(8,128)(2,1)S(1)} %fusion.3.refs_3_) | copy-start | bytes 552964
  233.7 11.6 %collective-permute-start.24 = (bf16[48,1920]{1,0:T(8,128)(2,1)S(1)}, bf16[48,1920]{1,0:T(8,128)(2,1)S(1)}, u32[]{:S(2)}, u32[]{:S(2)}) collective-permute-start(bf16[48,1920]{1,0:T(8,128)(2,1)S(1)} %fusion.3.refs_3_), channel_id=1, source_target_pairs={{0,16},{16,0},{1,17},{17,1},{2,18},{18,2},{3,19},{19,3},{4,20},{20... | collective-permute-start | bytes 552968 | tf_op jit(solution)/shard_map/ppermute | solution.py:738
  237.7 4.8 %copy-start.24 = (bf16[48,1152]{1,0:T(8,128)(2,1)}, bf16[48,1152]{1,0:T(8,128)(2,1)S(1)}, u32[]{:S(2)}) copy-start(bf16[48,1152]{1,0:T(8,128)(2,1)S(1)} %reduce_sum.12.refs_1_) | copy-start | bytes 331780
  237.8 4.8 %collective-permute-start.19 = (bf16[48,1152]{1,0:T(8,128)(2,1)S(1)}, bf16[48,1152]{1,0:T(8,128)(2,1)S(1)}, u32[]{:S(2)}, u32[]{:S(2)}) collective-permute-start(bf16[48,1152]{1,0:T(8,128)(2,1)S(1)} %reduce_sum.12.refs_1_), channel_id=1, source_target_pairs={{0,16},{16,0},{1,17},{17,1},{2,18},{18,2},{3,19},{19,3},{4,20},{20... | collective-permute-start | bytes 331784 | tf_op jit(solution)/shard_map/ppermute | solution.py:738
  (15 other events, 14.8 us)
Sparse Core Ops, SparseCore 0:
  12.1 96.6 all-gather.1
  130.9 90.9 reduce-scatter.1

commit v3 on v2

--- a/solution.py
+++ b/solution.py
@@ -667,7 +667,9 @@
     if direct:
         joint_came = flipped(joint_send, parts, 1)
         joint_red = Reduction([blocks_of(part) for part in (joint_keep, joint_came)], parts, place)
-        marks = [up_red.go("seq"), down_red.go(2), mixed_red.go(2), joint_red.go(2)]
+        marks = [up_red.go("seq"), down_red.go(2), mixed_red.go(2)]
+        joint_red.terms = list(pinned(joint_red.terms, marks))
+        marks.append(joint_red.go(2))
     sent, own_part = call(
         token_back,
         "token_back",
@@ -697,15 +699,10 @@
 
     marks = [own_part]
     if direct:
-        joint_red.take(own_part)
-        joint_sum = rounded_sum(joint_red.terms).reshape(4, rows, -1)
-        marks.append(joint_sum)
-    (out,) = forward_call(0, resid, marks)
-    marks = []
-    if direct:
+        marks = [own_part]
         last_sum = []
         for red in (up_red, down_red, mixed_red):
-            red.take(out)
+            red.take(own_part)
             last_sum.append(rounded_sum(red.terms))
         last_sum = jnp.concatenate(last_sum, axis=-1).reshape(4, rows, -1)
         deep = me // 4
@@ -714,6 +711,12 @@
             away = lax.dynamic_index_in_dim(last_sum, deep ^ far, 0, keepdims=False)
             last_parts.append(flipped(away, parts, 4 * far))
             marks.append(away)
+        joint_red.take(marks)
+        joint_sum = rounded_sum(joint_red.terms).reshape(4, rows, -1)
+        marks.append(joint_sum)
+    (out,) = forward_call(0, resid, marks)
+    marks = []
+    if direct:
         joint_sum = exchanged(joint_sum, parts)
     (out,) = forward_call(1, out, marks)
     marks = [out]
@@ -736,14 +739,6 @@
         joint_sum = scattered(joint_keep, joint_send)
     first_sum = pinned(first_sum, input_grad)
     first_sum, last_sum, joint_sum = ((part, lax.ppermute(part, "seq", SWAP)) for part in (first_sum, last_sum, joint_sum))
-    joint_grad, lead_grad = call(
-        joint_out,
-        "joint_out",
-        (shaped(rows, triple, dtype=F32), shaped(1, rows, dtype=F32)),
-        meta,
-        (*joint_sum, joint_weight, lead_gain[None, :]),
-        took=2,
-    )
     up_grad, down_grad, output_grad, tail_grad = call(
         functools.partial(feed_out, direct),
         "feed_out",
@@ -755,7 +750,16 @@
         ),
         meta,
         (*first_sum, *last_sum, up_weight, tail_gain[None, :]),
-        after=[joint_grad],
+        after=[input_grad],
+    )
+    joint_grad, lead_grad = call(
+        joint_out,
+        "joint_out",
+        (shaped(rows, triple, dtype=F32), shaped(1, rows, dtype=F32)),
+        meta,
+        (*joint_sum, joint_weight, lead_gain[None, :]),
+        took=2,
+        after=[up_grad],
     )
     return (
         out[None],

time: 261 us -> 258 us (0.989)
  waiting for transfers between devices: 69.8 us -> 63.1 us
    ppermute x15, waiting for transfers between devices: 43.4 us -> 37.4 us  [flipped(): lax.ppermute(array, 'fsdp', [(spot, spot ^ bit) for spot in range(parts)])]
    unnamed x80 -> x84, local copies, waits for them, and re-layouts: 7.28 us -> 8.2 us
  transfers between devices with their start and end apart: 28 -> 28, of which waited for: 12 -> 12; matrix products, arithmetic and copies ran while one was open for 5% -> 5% of each run, Pallas kernels for 37% -> 38%
where the time goes in v3:
time: 258 us; the launch traced here: 254 us
  Pallas kernels  120 us (47%)
  waiting for transfers between devices  63.1 us (24%)
  starting transfers between devices  31.3 us (12%)
  between operations  15 us (6%)
  other arithmetic  12.3 us (5%)
  local copies, waits for them, and re-layouts  11.9 us (5%)
    pallas_call x16, Pallas kernels, call(): pl.pallas_call(waiting(kernel, 1 + len(inputs), len(after)), name=name, g...  120 us
    ppermute x15, waiting for transfers between devices, flipped(): lax.ppermute(array, 'fsdp', [(spot, spot ^ bit) for spot in range(parts)])  37.4 us
    ppermute x15, starting transfers between devices, flipped(): lax.ppermute(array, 'fsdp', [(spot, spot ^ bit) for spot in range(parts)])  15 us
    all_gather x1, waiting for transfers between devices, body(): lax.all_gather(jnp.concatenate([output_weight, *hidden], axis=1), 'fsdp',...  10.3 us
    convert_element_type x11, other arithmetic, rounded_sum(): return total.astype(BF16)  9.47 us
    unnamed x84, local copies, waits for them, and re-layouts  8.2 us
    ppermute x1, waiting for transfers between devices, body(): o_came = lax.ppermute(o_other, 'seq', SWAP)  7.04 us
    ppermute x3, waiting for transfers between devices, body(): lax.ppermute(part, 'seq', SWAP)  5.27 us
  transfers between devices with their start and end apart: 28, of which 12 were waited for; matrix products, arithmetic and copies ran while one was open for 5% of the time, Pallas kernels for 38%

profile of v3, /device:TPU:0, one launch (start us, length us, event | category | flops | bytes accessed | tf_op | source)
XLA Modules:
  0.0 253.7 jit_solution(4802896818284237054)
XLA Ops:
  8.1 1.7 reshape.88
  12.9 4.1 %collective-permute-start = (bf16[48,1280]{1,0:T(8,128)(2,1)S(1)}, bf16[48,1280]{1,0:T(8,128)(2,1)S(1)}, u32[]{:S(2)}, u32[]{:S(2)}) collective-permute-start(bf16[48,1280]{1,0:T(8,128)(2,1)S(1)} %pad_maximum_fusion.3), channel_id=1, source_target_pairs={{0,8},{1,9},{2,10},{3,11},{4,12},{5,13},{6,14},{7,15},{8,0},{9,1},... | collective-permute-start | bytes 368648 | tf_op jit(solution)/shard_map/ppermute | solution.py:412
  17.0 1.5 collective-permute-start.2
  18.5 4.4 %collective-permute-done = bf16[48,1280]{1,0:T(8,128)(2,1)S(1)} collective-permute-done((bf16[48,1280]{1,0:T(8,128)(2,1)S(1)}, bf16[48,1280]{1,0:T(8,128)(2,1)S(1)}, u32[]{:S(2)}, u32[]{:S(2)}) %collective-permute-start) | collective-permute-done | bytes 122912 | tf_op jit(solution)/shard_map/ppermute | solution.py:412
  23.8 17.1 %collective-permute-done.1 = bf16[96,1280]{1,0:T(8,128)(2,1)S(1)} collective-permute-done((bf16[96,1280]{1,0:T(8,128)(2,1)S(1)}, bf16[96,1280]{1,0:T(8,128)(2,1)S(1)}, u32[]{:S(2)}, u32[]{:S(2)}) %collective-permute-start.1) | collective-permute-done | bytes 245792 | tf_op jit(solution)/shard_map/ppermute | solution.py:412
  40.9 1.3 collective-permute-start.3
  42.2 7.6 %collective-permute-done.3 = bf16[192,1280]{1,0:T(8,128)(2,1)S(1)} collective-permute-done((bf16[192,1280]{1,0:T(8,128)(2,1)S(1)}, bf16[192,1280]{1,0:T(8,128)(2,1)S(1)}, u32[]{:S(2)}, u32[]{:S(2)}) %collective-permute-start.3) | collective-permute-done | bytes 491552 | tf_op jit(solution)/shard_map/ppermute | solution.py:412
  50.7 4.0 %first_norm.1.refs_1_ = f32[1024,768]{1,0:T(8,128)} custom-call(s32[33]{0:T(128)} %pad_add_fusion.refs_0_, bf16[512,768]{1,0:T(8,128)(2,1)} %bitcast.47, bf16[512,768]{1,0:T(8,128)(2,1)} %copy-done.18), custom_call_target="tpu_custom_call" | custom-call | flops 30000000 | bytes 90000 | tf_op jit(solution)/shard_map/first_norm/pallas_call | solution.py:56
  55.6 3.6 %first_scale.1 = (bf16[1024,768]{1,0:T(8,128)(2,1)}, bf16[16,768]{1,0:T(8,128)(2,1)}) custom-call(s32[33]{0:T(128)} %pad_add_fusion.refs_0_, f32[1024,768]{1,0:T(8,128)} %first_norm.1.refs_1_, bf16[384,1280]{1,0:T(8,128)(2,1)} %copy-done.1, bf16[384,1280]{1,0:T(8,128)(2,1)} %copy-done.2), custom_call_target="tpu_custom_call" | custom-call | flops 20000000 | bytes 60000 | tf_op jit(solution)/shard_map/first_scale/pallas_call | solution.py:56
  59.2 24.5 %attend.1 = (bf16[1024,1152]{1,0:T(8,128)(2,1)}, bf16[512,384]{1,0:T(8,128)(2,1)}, bf16[512,384]{1,0:T(8,128)(2,1)}, f32[3,8,1024]{2,1,0:T(8,128)}, bf16[768,1152]{1,0:T(8,128)(2,1)}) custom-call(s32[33]{0:T(128)} %pad_add_fusion.refs_0_, bf16[1024,768]{1,0:T(8,128)(2,1)} %get-tuple-element.72.refs_1_, bf16[384,1280]{1,0:T(8,128)(2,1)} %copy-done.1, ...), custom_call_target="tpu_custom_call" | custom-call | flops 220000000 | bytes 660000 | tf_op jit(solution)/shard_map/attend/pallas_call | solution.py:56
  83.7 1.4 collective-permute-start.5
  85.1 3.3 %turn.1.refs_3_.refs_7_ = bf16[768,1024]{1,0:T(8,128)(2,1)} custom-call(s32[33]{0:T(128)} %pad_add_fusion.refs_0_, bf16[1024,768]{1,0:T(8,128)(2,1)} %get-tuple-element.72.refs_1_, f32[3,8,1024]{2,1,0:T(8,128)} %get-tuple-element.75.refs_2_.refs_6_), custom_call_target="tpu_custom_call" | custom-call | flops 20000000 | bytes 60000 | tf_op jit(solution)/shard_map/turn/pallas_call | solution.py:56
  88.3 7.0 %collective-permute-done.5.refs_2_ = bf16[512,384]{1,0:T(8,128)(2,1)S(1)} collective-permute-done((bf16[512,384]{1,0:T(8,128)(2,1)}, bf16[512,384]{1,0:T(8,128)(2,1)S(1)}, u32[]{:S(2)}, u32[]{:S(2)}) %collective-permute-start.5) | collective-permute-done | bytes 393248 | tf_op jit(solution)/shard_map/ppermute | solution.py:538
  96.1 2.4 mix.1
  98.5 10.3 %all-gather.2.cloned.1.call-done.refs_4_.refs_5_.refs_6_.refs_3_ = bf16[768,6912]{1,0:T(8,128)(2,1)} async-done(((bf16[48,6912]{1,0:T(8,128)(2,1)}), bf16[768,6912]{1,0:T(8,128)(2,1)}) %all-gather.2.cloned.1.call-update) | async-done | bytes 10616848 | tf_op jit(solution)/shard_map/all_gather | solution.py:485
  108.8 21.9 %feed.1 = (bf16[512,3072]{1,0:T(8,128)(2,1)}, bf16[512,3072]{1,0:T(8,128)(2,1)}, bf16[768,3072]{1,0:T(8,128)(2,1)}, bf16[768,512]{1,0:T(8,128)(2,1)}, f32[512,76...) custom-call(s32[33]{0:T(128)} %pad_add_fusion.refs_0_, ...), custom_call_target="tpu_custom_call" | custom-call | flops 200000000 | bytes 600000 | tf_op jit(solution)/shard_map/feed/pallas_call | solution.py:56
  131.8 1.5 collective-permute-start.6
  133.2 8.2 %hidden_back.1 = (bf16[384,1536]{1,0:T(8,128)(2,1)}, bf16[384,1536]{1,0:T(8,128)(2,1)}, bf16[384,1536]{1,0:T(8,128)(2,1)}, bf16[384,1536]{1,0:T(8,128)(2,1)}, bf...) custom-call(s32[33]{0:T(128)} %pad_add_fusion.refs_0_, bf16[768,512]{1,0:T(8,128)(2,1)} %get-tuple-element.83.refs_1_, ...), custom_call_target="tpu_custom_call" | custom-call | flops 70000000 | bytes 210000 | tf_op jit(solution)/shard_map/hidden_back/pallas_call | solution.py:56
  141.4 1.6 collective-permute-done.6.refs_5_
  143.8 8.6 %attend_back.3 = (bf16[384,384]{1,0:T(8,128)(2,1)}, bf16[384,384]{1,0:T(8,128)(2,1)}, bf16[1024,384]{1,0:T(8,128)(2,1)}) custom-call(s32[33]{0:T(128)} %pad_add_fusion.refs_0_, bf16[1024,1152]{1,0:T(8,128)(2,1)} %get-tuple-element.80.refs_1_, bf16[512,384]{1,0:T(8,128)(2,1)} %get-tuple-element.73.refs_1_.refs_2_, ...), custom_call_target="tpu_custom_call" | custom-call | flops 100000000 | bytes 300000 | tf_op jit(solution)/shard_map/attend_back/pallas_call | solution.py:56
  152.4 1.3 add_convert_fusion.refs_10_
  153.8 1.6 collective-permute-start.11
  156.2 1.1 add_convert_fusion.8.refs_11_
  158.0 8.3 %attend_back.4 = (bf16[384,384]{1,0:T(8,128)(2,1)}, bf16[384,384]{1,0:T(8,128)(2,1)}, bf16[1024,384]{1,0:T(8,128)(2,1)}) custom-call(s32[33]{0:T(128)} %pad_add_fusion.refs_0_, bf16[1024,1152]{1,0:T(8,128)(2,1)} %get-tuple-element.80.refs_1_, bf16[512,384]{1,0:T(8,128)(2,1)} %get-tuple-element.73.refs_1_.refs_2_, ...), custom_call_target="tpu_custom_call" | custom-call | flops 100000000 | bytes 300000 | tf_op jit(solution)/shard_map/attend_back/pallas_call | solution.py:56
  166.3 9.6 %attend_back.5 = (bf16[384,1152]{1,0:T(8,128)(2,1)}, bf16[384,1152]{1,0:T(8,128)(2,1)}, bf16[1024,384]{1,0:T(8,128)(2,1)}) custom-call(s32[33]{0:T(128)} %pad_add_fusion.refs_0_, bf16[1024,1152]{1,0:T(8,128)(2,1)} %get-tuple-element.80.refs_1_, bf16[512,384]{1,0:T(8,128)(2,1)} %get-tuple-element.73.refs_1_.refs_2_, ...), custom_call_target="tpu_custom_call" | custom-call | flops 100000000 | bytes 300000 | tf_op jit(solution)/shard_map/attend_back/pallas_call | solution.py:56
  176.0 2.2 collective-permute-done.10
  181.4 1.1 add_convert_fusion.7.refs_5_
  183.0 1.2 add_convert_fusion.6.refs_6_
  185.1 1.3 collective-permute-start.17
  186.5 6.1 %token_back.1 = (bf16[512,768]{1,0:T(8,128)(2,1)}, f32[512,768]{1,0:T(8,128)}) custom-call(s32[33]{0:T(128)} %pad_add_fusion.refs_0_, bf16[1024,384]{1,0:T(8,128)(2,1)} %get-tuple-element.90.refs_12_.refs_1_, bf16[1024,384]{1,0:T(8,128)(2,1)} %get-tuple-element.102.refs_13_.refs_2_, bf16[1024,384]{1,0:T(8,128)(2,1)} %get-tuple-element.107.refs_3_, ...), custom_call_target="tpu_custom_call" | custom-call | flops 50000000 | bytes 150000 | tf_op jit(solution)/shard_map/token_back/pallas_call | solution.py:56
  192.6 1.5 collective-permute-done.15
  194.1 1.6 collective-permute-start.18
  196.7 1.1 add_convert_fusion.5
  197.9 1.3 add_convert_fusion.4
  200.4 3.4 %collective-permute-start.21 = (bf16[48,1920]{1,0:T(8,128)(2,1)S(1)}, bf16[48,1920]{1,0:T(8,128)(2,1)S(1)}, u32[]{:S(2)}, u32[]{:S(2)}) collective-permute-start(bf16[48,1920]{1,0:T(8,128)(2,1)S(1)} %get-tuple-element.138.refs_5_), channel_id=1, source_target_pairs={{0,4},{1,5},{2,6},{3,7},{4,0},{5,1},{6,2},{7,3},{8,12},{9,13},{10,... | collective-permute-start | bytes 552968 | tf_op jit(solution)/shard_map/ppermute | solution.py:412
  203.8 1.9 collective-permute-done.17
  205.7 1.9 fusion.refs_8_
  207.6 3.7 %all-to-all-start = ((bf16[4,48,1152]{2,1,0:T(8,128)(2,1)}), bf16[4,48,1152]{2,1,0:T(8,128)(2,1)S(1)}, u32[]{:S(2)}, u32[]{:S(2)}) async-start(bf16[4,48,1152]{2,1,0:T(8,128)(2,1)} %fusion.refs_8_), calls=%async_computation | async-start | bytes 884736 | tf_op jit(solution)/shard_map/all_to_all | solution.py:417
  211.4 5.3 %forward_out.2.refs_1_ = f32[512,768]{1,0:T(8,128)} custom-call(s32[33]{0:T(128)} %pad_add_fusion.refs_0_, f32[512,768]{1,0:T(8,128)} %get-tuple-element.78.refs_1_, bf16[512,3072]{1,0:T(8,128)(2,1)} %get-tuple-element.79.refs_2_, bf16[768,6912]{1,0:T(8,128)(2,1)} %all-gather.2.cloned.1.call-done.refs_4_.refs_5_.refs_6_.refs_3_, ...), custom_call_target="tpu_custom_call" | custom-call | flops 30000000 | bytes 90000 | tf_op jit(solution)/shard_map/forward_out/pallas_call | solution.py:56
  216.6 4.9 %forward_out.3.refs_6_ = bf16[512,768]{1,0:T(8,128)(2,1)} custom-call(s32[33]{0:T(128)} %pad_add_fusion.refs_0_, f32[512,768]{1,0:T(8,128)} %forward_out.2.refs_1_, bf16[512,3072]{1,0:T(8,128)(2,1)} %get-tuple-element.79.refs_2_, bf16[768,6912]{1,0:T(8,128)(2,1)} %all-gather.2.cloned.1.call-done.refs_4_.refs_5_.refs_6_.refs_3_), custom_call_target="tpu_custom_call" | custom-call | flops 30000000 | bytes 90000 | tf_op jit(solution)/shard_map/forward_out/pallas_call | solution.py:56
  222.4 4.5 %input_back.1.refs_7_ = f32[512,768]{1,0:T(8,128)} custom-call(s32[33]{0:T(128)} %pad_add_fusion.refs_0_, bf16[512,768]{1,0:T(8,128)(2,1)} %bitcast.49, f32[512,768]{1,0:T(8,128)} %get-tuple-element.116.refs_4_.refs_2_, bf16[512,768]{1,0:T(8,128)(2,1)} %copy-done.19, f32[512,768]{1,0:T(8,128)} %get-tuple-element.122.refs_4_, ...), custom_call_target="tpu_custom_call" | custom-call | flops 40000000 | bytes 120000 | tf_op jit(solution)/shard_map/input_back/pallas_call | solution.py:56
  227.0 1.8 collective-permute-start.20
  228.7 2.7 %collective-permute-done.22 = bf16[48,1920]{1,0:T(8,128)(2,1)S(1)} collective-permute-done((bf16[48,1920]{1,0:T(8,128)(2,1)S(1)}, bf16[48,1920]{1,0:T(8,128)(2,1)S(1)}, u32[]{:S(2)}, u32[]{:S(2)}) %collective-permute-start.22) | collective-permute-done | bytes 184352 | tf_op jit(solution)/shard_map/ppermute | solution.py:412
  232.3 1.4 all-to-all-done
  233.9 1.2 collective-permute-start.19
  235.0 5.3 %collective-permute-done.24.refs_4_ = bf16[48,1920]{1,0:T(8,128)(2,1)S(1)} collective-permute-done((bf16[48,1920]{1,0:T(8,128)(2,1)S(1)}, bf16[48,1920]{1,0:T(8,128)(2,1)S(1)}, u32[]{:S(2)}, u32[]{:S(2)}) %collective-permute-start.24) | collective-permute-done | bytes 184352 | tf_op jit(solution)/shard_map/ppermute | solution.py:741
  241.1 2.8 %feed_out.1 = (f32[48,3072]{1,0:T(8,128)}, f32[192,768]{1,0:T(8,128)}, f32[48,768]{1,0:T(8,128)}, f32[1,48]{1,0:T(1,128)}) custom-call(s32[33]{0:T(128)} %pad_add_fusion.refs_0_, bf16[48,3072]{1,0:T(8,128)(2,1)} %reduce-scatter.2.cloned.1.call-done.refs_1_, bf16[48,3072]{1,0:T(8,128)(2,1)} %copy-done.28, bf16[48,1920]{1,0:T(8,128)(2,1)} %copy-done.23, ...), custom_call_target="tpu_custom_call" | custom-call | flops 40000000 | bytes 120000 | tf_op jit(solution)/shard_map/feed_out/pallas_call | solution.py:56
  244.6 2.1 joint_out.1
  (151 shorter events, 20.4 us)
Async XLA Ops:
  7.2 101.7 %all-gather.2.cloned.1.call-start = ((), (), s32[]{:S(2)}) async-start(), calls=%async_computation.2 | async-start | bytes 11280384 | tf_op jit(solution)/shard_map/all_gather | solution.py:485
  12.0 5.0 %copy-start = (bf16[1,512,768]{2,1,0:T(8,128)(2,1)S(1)}, bf16[1,512,768]{2,1,0:T(8,128)(2,1)}, u32[]{:S(2)}) copy-start(bf16[1,512,768]{2,1,0:T(8,128)(2,1)} %param.8) | copy-start | bytes 2359300
  12.0 214.9 %reduce-scatter.2.cloned.1.call-start = ((), (), s32[]{:S(2)}) async-start(), calls=%async_computation.3 | async-start | bytes 5013504 | tf_op jit(solution)/shard_map/reduce_scatter | solution.py:605
  12.9 10.1 %collective-permute-start = (bf16[48,1280]{1,0:T(8,128)(2,1)S(1)}, bf16[48,1280]{1,0:T(8,128)(2,1)S(1)}, u32[]{:S(2)}, u32[]{:S(2)}) collective-permute-start(bf16[48,1280]{1,0:T(8,128)(2,1)S(1)} %pad_maximum_fusion.3), channel_id=1, source_target_pairs={{0,8},{1,9},{2,10},{3,11},{4,12},{5,13},{6,14},{7,15},{8,0},{9,1},... | collective-permute-start | bytes 368648 | tf_op jit(solution)/shard_map/ppermute | solution.py:412
  17.0 23.9 %collective-permute-start.2 = (bf16[512,768]{1,0:T(8,128)(2,1)S(1)}, bf16[512,768]{1,0:T(8,128)(2,1)S(1)}, u32[]{:S(2)}, u32[]{:S(2)}) collective-permute-start(bf16[512,768]{1,0:T(8,128)(2,1)S(1)} %bitcast.50), channel_id=1, source_target_pairs={{0,16},{16,0},{1,17},{17,1},{2,18},{18,2},{3,19},{19,3},{4,20},{20... | collective-permute-start | bytes 2359304 | tf_op jit(solution)/shard_map/ppermute | solution.py:486
  23.0 17.9 %collective-permute-start.1 = (bf16[96,1280]{1,0:T(8,128)(2,1)S(1)}, bf16[96,1280]{1,0:T(8,128)(2,1)S(1)}, u32[]{:S(2)}, u32[]{:S(2)}) collective-permute-start(bf16[96,1280]{1,0:T(8,128)(2,1)S(1)} %pad_maximum_fusion.2), channel_id=1, source_target_pairs={{0,4},{1,5},{2,6},{3,7},{4,0},{5,1},{6,2},{7,3},{8,12},{9,13},{10,... | collective-permute-start | bytes 737288 | tf_op jit(solution)/shard_map/ppermute | solution.py:412
  40.9 9.8 %copy-start.18 = (bf16[512,768]{1,0:T(8,128)(2,1)}, bf16[512,768]{1,0:T(8,128)(2,1)S(1)}, u32[]{:S(2)}) copy-start(bf16[512,768]{1,0:T(8,128)(2,1)S(1)} %collective-permute-done.2.refs_2_) | copy-start | bytes 2359300
  40.9 8.9 %collective-permute-start.3 = (bf16[192,1280]{1,0:T(8,128)(2,1)S(1)}, bf16[192,1280]{1,0:T(8,128)(2,1)S(1)}, u32[]{:S(2)}, u32[]{:S(2)}) collective-permute-start(bf16[192,1280]{1,0:T(8,128)(2,1)S(1)} %pad_maximum_fusion.1), channel_id=1, source_target_pairs={{0,2},{1,3},{2,0},{3,1},{4,6},{5,7},{6,4},{7,5},{8,10},{9,11},{10,... | collective-permute-start | bytes 1474568 | tf_op jit(solution)/shard_map/ppermute | solution.py:412
  49.9 4.8 %copy-start.1 = (bf16[384,1280]{1,0:T(8,128)(2,1)}, bf16[384,1280]{1,0:T(8,128)(2,1)S(1)}, u32[]{:S(2)}) copy-start(bf16[384,1280]{1,0:T(8,128)(2,1)S(1)} %constant_dynamic-update-slice_fusion.refs_2_) | copy-start | bytes 2949124
  49.9 4.8 %collective-permute-start.4 = (bf16[384,1280]{1,0:T(8,128)(2,1)S(1)}, bf16[384,1280]{1,0:T(8,128)(2,1)S(1)}, u32[]{:S(2)}, u32[]{:S(2)}) collective-permute-start(bf16[384,1280]{1,0:T(8,128)(2,1)S(1)} %constant_dynamic-update-slice_fusion.refs_2_), channel_id=1, source_target_pairs={{0,1},{1,0},{2,3},{3,2},{4,5},{5,4},{6,7},{7,6},{8,9},{9,8},{10,11... | collective-permute-start | bytes 2949128 | tf_op jit(solution)/shard_map/ppermute | solution.py:412
  83.7 11.7 %collective-permute-start.5 = (bf16[512,384]{1,0:T(8,128)(2,1)}, bf16[512,384]{1,0:T(8,128)(2,1)S(1)}, u32[]{:S(2)}, u32[]{:S(2)}) collective-permute-start(bf16[512,384]{1,0:T(8,128)(2,1)} %get-tuple-element.74.refs_3_), channel_id=1, source_target_pairs={{0,16},{16,0},{1,17},{17,1},{2,18},{18,2},{3,19},{19,3},{4,20},{20... | collective-permute-start | bytes 1179656 | tf_op jit(solution)/shard_map/ppermute | solution.py:538
  131.8 11.3 %collective-permute-start.6 = (bf16[512,384]{1,0:T(8,128)(2,1)S(1)}, bf16[512,384]{1,0:T(8,128)(2,1)S(1)}, u32[]{:S(2)}, u32[]{:S(2)}) collective-permute-start(bf16[512,384]{1,0:T(8,128)(2,1)S(1)} %copy-done.36), channel_id=1, source_target_pairs={{0,16},{16,0},{1,17},{17,1},{2,18},{18,2},{3,19},{19,3},{4,20},{20... | collective-permute-start | bytes 1179656 | tf_op jit(solution)/shard_map/ppermute | solution.py:585
  143.1 9.4 %collective-permute-start.8 = (bf16[384,1536]{1,0:T(8,128)(2,1)}, bf16[384,1536]{1,0:T(8,128)(2,1)}, u32[]{:S(2)}, u32[]{:S(2)}) collective-permute-start(bf16[384,1536]{1,0:T(8,128)(2,1)} %get-tuple-element.96), channel_id=1, source_target_pairs={{0,1},{1,0},{2,3},{3,2},{4,5},{5,4},{6,7},{7,6},{8,9},{9,8},{10,11... | collective-permute-start | bytes 3538952 | tf_op jit(solution)/shard_map/ppermute | solution.py:412
  143.1 9.4 %collective-permute-start.7 = (bf16[384,1536]{1,0:T(8,128)(2,1)}, bf16[384,1536]{1,0:T(8,128)(2,1)S(1)}, u32[]{:S(2)}, u32[]{:S(2)}) collective-permute-start(bf16[384,1536]{1,0:T(8,128)(2,1)} %get-tuple-element.92), channel_id=1, source_target_pairs={{0,1},{1,0},{2,3},{3,2},{4,5},{5,4},{6,7},{7,6},{8,9},{9,8},{10,11... | collective-permute-start | bytes 3538952 | tf_op jit(solution)/shard_map/ppermute | solution.py:412
  143.6 12.6 %collective-permute-start.9 = (bf16[384,768]{1,0:T(8,128)(2,1)}, bf16[384,768]{1,0:T(8,128)(2,1)}, u32[]{:S(2)}, u32[]{:S(2)}) collective-permute-start(bf16[384,768]{1,0:T(8,128)(2,1)} %get-tuple-element.100), channel_id=1, source_target_pairs={{0,1},{1,0},{2,3},{3,2},{4,5},{5,4},{6,7},{7,6},{8,9},{9,8},{10,11... | collective-permute-start | bytes 1769480 | tf_op jit(solution)/shard_map/ppermute | solution.py:412
  143.8 8.6 %copy-start.11 = (bf16[384,1536]{1,0:T(8,128)(2,1)S(1)}, bf16[384,1536]{1,0:T(8,128)(2,1)}, u32[]{:S(2)}) copy-start(bf16[384,1536]{1,0:T(8,128)(2,1)} %get-tuple-element.94) | copy-start | bytes 3538948
  152.4 3.0 %copy-start.10 = (bf16[384,1536]{1,0:T(8,128)(2,1)S(1)}, bf16[384,1536]{1,0:T(8,128)(2,1)}, u32[]{:S(2)}) copy-start(bf16[384,1536]{1,0:T(8,128)(2,1)} %get-tuple-element.87) | copy-start | bytes 3538948
  153.7 3.5 %copy-start.5 = (bf16[4,2,48,768]{3,2,1,0:T(8,128)(2,1)}, bf16[4,2,48,768]{3,2,1,0:T(8,128)(2,1)S(1)}, u32[]{:S(2)}) copy-start(bf16[4,2,48,768]{3,2,1,0:T(8,128)(2,1)S(1)} %add_convert_fusion.refs_10_) | copy-start | bytes 1769476
  153.8 22.2 %collective-permute-start.11 = (bf16[4,2,48,768]{3,2,1,0:T(8,128)(2,1)S(1)}, bf16[4,2,48,768]{3,2,1,0:T(8,128)(2,1)}, u32[]{:S(2)}, u32[]{:S(2)}) collective-permute-start(bf16[4,2,48,768]{3,2,1,0:T(8,128)(2,1)S(1)} %add_convert_fusion.refs_10_), channel_id=1, source_target_pairs={{0,16},{16,0},{1,17},{17,1},{2,18},{18,2},{3,19},{19,3},{4,20},{20... | collective-permute-start | bytes 1769480 | tf_op jit(solution)/shard_map/ppermute | solution.py:442
  155.5 2.5 copy-start.4
  155.5 22.7 %collective-permute-start.10 = (bf16[4,1,48,1536]{3,2,1,0:T(8,128)(2,1)S(1)}, bf16[4,1,48,1536]{3,2,1,0:T(8,128)(2,1)}, u32[]{:S(2)}, u32[]{:S(2)}) collective-permute-start(bf16[4,1,48,1536]{3,2,1,0:T(8,128)(2,1)S(1)} %add_convert_fusion.1.refs_9_), channel_id=1, source_target_pairs={{0,2},{1,3},{2,0},{3,1},{4,6},{5,7},{6,4},{7,5},{8,10},{9,11},{10,... | collective-permute-start | bytes 1769480 | tf_op jit(solution)/shard_map/ppermute | solution.py:412
  157.3 18.7 %collective-permute-start.12 = (bf16[4,2,48,384]{3,2,1,0:T(8,128)(2,1)S(1)}, bf16[4,2,48,384]{3,2,1,0:T(8,128)(2,1)S(1)}, u32[]{:S(2)}, u32[]{:S(2)}) collective-permute-start(bf16[4,2,48,384]{3,2,1,0:T(8,128)(2,1)S(1)} %add_convert_fusion.8.refs_11_), channel_id=1, source_target_pairs={{0,16},{16,0},{1,17},{17,1},{2,18},{18,2},{3,19},{19,3},{4,20},{20... | collective-permute-start | bytes 884744 | tf_op jit(solution)/shard_map/ppermute | solution.py:442
  176.0 2.2 copy-start.30
  178.2 6.8 %collective-permute-start.13 = (bf16[384,1152]{1,0:T(8,128)(2,1)}, bf16[384,1152]{1,0:T(8,128)(2,1)S(1)}, u32[]{:S(2)}, u32[]{:S(2)}) collective-permute-start(bf16[384,1152]{1,0:T(8,128)(2,1)} %get-tuple-element.113), channel_id=1, source_target_pairs={{0,1},{1,0},{2,3},{3,2},{4,5},{5,4},{6,7},{7,6},{8,9},{9,8},{10,11... | collective-permute-start | bytes 2654216 | tf_op jit(solution)/shard_map/ppermute | solution.py:412
  179.3 3.6 %copy-start.12 = (bf16[384,1536]{1,0:T(8,128)(2,1)S(1)}, bf16[384,1536]{1,0:T(8,128)(2,1)}, u32[]{:S(2)}) copy-start(bf16[384,1536]{1,0:T(8,128)(2,1)} %get-tuple-element.94) | copy-start | bytes 3538948
  180.4 3.7 %copy-start.24 = (bf16[4,1,48,384]{3,2,1,0:T(8,128)(2,1)}, bf16[4,1,48,384]{3,2,1,0:T(8,128)(2,1)S(1)}, u32[]{:S(2)}) copy-start(bf16[4,1,48,384]{3,2,1,0:T(8,128)(2,1)S(1)} %add_convert_fusion.10.refs_7_) | copy-start | bytes 442372
  180.4 4.6 %copy-start.13 = (bf16[384,1152]{1,0:T(8,128)(2,1)S(1)}, bf16[384,1152]{1,0:T(8,128)(2,1)}, u32[]{:S(2)}) copy-start(bf16[384,1152]{1,0:T(8,128)(2,1)} %get-tuple-element.112) | copy-start | bytes 2654212
  180.4 12.2 %collective-permute-start.16 = (bf16[4,1,48,384]{3,2,1,0:T(8,128)(2,1)S(1)}, bf16[4,1,48,384]{3,2,1,0:T(8,128)(2,1)S(1)}, u32[]{:S(2)}, u32[]{:S(2)}) collective-permute-start(bf16[4,1,48,384]{3,2,1,0:T(8,128)(2,1)S(1)} %add_convert_fusion.10.refs_7_), channel_id=1, source_target_pairs={{0,2},{1,3},{2,0},{3,1},{4,6},{5,7},{6,4},{7,5},{8,10},{9,11},{10,... | collective-permute-start | bytes 442376 | tf_op jit(solution)/shard_map/ppermute | solution.py:412
  182.5 2.6 %copy-start.8 = (bf16[4,1,48,768]{3,2,1,0:T(8,128)(2,1)}, bf16[4,1,48,768]{3,2,1,0:T(8,128)(2,1)S(1)}, u32[]{:S(2)}) copy-start(bf16[4,1,48,768]{3,2,1,0:T(8,128)(2,1)S(1)} %add_convert_fusion.7.refs_5_) | copy-start | bytes 884740
  182.5 11.6 %collective-permute-start.14 = (bf16[4,1,48,768]{3,2,1,0:T(8,128)(2,1)S(1)}, bf16[4,1,48,768]{3,2,1,0:T(8,128)(2,1)S(1)}, u32[]{:S(2)}, u32[]{:S(2)}) collective-permute-start(bf16[4,1,48,768]{3,2,1,0:T(8,128)(2,1)S(1)} %add_convert_fusion.7.refs_5_), channel_id=1, source_target_pairs={{0,16},{16,0},{1,17},{17,1},{2,18},{18,2},{3,19},{19,3},{4,20},{20... | collective-permute-start | bytes 884744 | tf_op jit(solution)/shard_map/ppermute | solution.py:442
  184.2 2.3 copy-start.9
  184.2 9.9 %collective-permute-start.15 = (bf16[4,1,48,768]{3,2,1,0:T(8,128)(2,1)S(1)}, bf16[4,1,48,768]{3,2,1,0:T(8,128)(2,1)S(1)}, u32[]{:S(2)}, u32[]{:S(2)}) collective-permute-start(bf16[4,1,48,768]{3,2,1,0:T(8,128)(2,1)S(1)} %add_convert_fusion.6.refs_6_), channel_id=1, source_target_pairs={{0,2},{1,3},{2,0},{3,1},{4,6},{5,7},{6,4},{7,5},{8,10},{9,11},{10,... | collective-permute-start | bytes 884744 | tf_op jit(solution)/shard_map/ppermute | solution.py:412
  185.0 7.6 %copy-start.14 = (bf16[384,1152]{1,0:T(8,128)(2,1)}, bf16[384,1152]{1,0:T(8,128)(2,1)S(1)}, u32[]{:S(2)}) copy-start(bf16[384,1152]{1,0:T(8,128)(2,1)S(1)} %collective-permute-done.13) | copy-start | bytes 2654212
  185.1 20.5 %collective-permute-start.17 = (bf16[4,1,48,1152]{3,2,0,1:T(8,128)(2,1)S(1)}, bf16[4,1,48,1152]{3,2,0,1:T(8,128)(2,1)}, u32[]{:S(2)}, u32[]{:S(2)}) collective-permute-start(bf16[4,1,48,1152]{3,2,0,1:T(8,128)(2,1)S(1)} %add_convert_fusion.3), channel_id=1, source_target_pairs={{0,2},{1,3},{2,0},{3,1},{4,6},{5,7},{6,4},{7,5},{8,10},{9,11},{10,... | collective-permute-start | bytes 1327112 | tf_op jit(solution)/shard_map/ppermute | solution.py:412
  194.1 27.4 %collective-permute-start.18 = (bf16[512,768]{1,0:T(8,128)(2,1)}, bf16[512,768]{1,0:T(8,128)(2,1)S(1)}, u32[]{:S(2)}, u32[]{:S(2)}) collective-permute-start(bf16[512,768]{1,0:T(8,128)(2,1)} %get-tuple-element.121), channel_id=1, source_target_pairs={{0,16},{16,0},{1,17},{17,1},{2,18},{18,2},{3,19},{19,3},{4,20},{20... | collective-permute-start | bytes 2359304 | tf_op jit(solution)/shard_map/ppermute | solution.py:682
  199.1 6.5 %copy-start.15 = (bf16[384,1152]{1,0:T(8,128)(2,1)S(1)}, bf16[384,1152]{1,0:T(8,128)(2,1)}, u32[]{:S(2)}) copy-start(bf16[384,1152]{1,0:T(8,128)(2,1)} %copy-done.14) | copy-start | bytes 2654212
  199.3 8.3 %copy-start.20 = (bf16[48,1920]{1,0:T(8,128)(2,1)}, bf16[48,1920]{1,0:T(8,128)(2,1)S(1)}, u32[]{:S(2)}) copy-start(bf16[48,1920]{1,0:T(8,128)(2,1)S(1)} %get-tuple-element.138.refs_5_) | copy-start | bytes 552964
  199.3 8.3 %copy-start.21 = (bf16[48,1920]{1,0:T(8,128)(2,1)}, bf16[48,1920]{1,0:T(8,128)(2,1)S(1)}, u32[]{:S(2)}) copy-start(bf16[48,1920]{1,0:T(8,128)(2,1)S(1)} %get-tuple-element.137.refs_6_) | copy-start | bytes 552964
  199.3 8.3 %copy-start.22 = (bf16[48,1920]{1,0:T(8,128)(2,1)}, bf16[48,1920]{1,0:T(8,128)(2,1)S(1)}, u32[]{:S(2)}) copy-start(bf16[48,1920]{1,0:T(8,128)(2,1)S(1)} %get-tuple-element.136.refs_7_) | copy-start | bytes 552964
  199.3 29.4 %collective-permute-start.23 = (bf16[48,1920]{1,0:T(8,128)(2,1)S(1)}, bf16[48,1920]{1,0:T(8,128)(2,1)S(1)}, u32[]{:S(2)}, u32[]{:S(2)}) collective-permute-start(bf16[48,1920]{1,0:T(8,128)(2,1)S(1)} %get-tuple-element.136.refs_7_), channel_id=1, source_target_pairs={{0,12},{1,13},{2,14},{3,15},{4,8},{5,9},{6,10},{7,11},{8,4},{9,5},... | collective-permute-start | bytes 552968 | tf_op jit(solution)/shard_map/ppermute | solution.py:412
  199.8 31.6 %collective-permute-start.22 = (bf16[48,1920]{1,0:T(8,128)(2,1)S(1)}, bf16[48,1920]{1,0:T(8,128)(2,1)S(1)}, u32[]{:S(2)}, u32[]{:S(2)}) collective-permute-start(bf16[48,1920]{1,0:T(8,128)(2,1)S(1)} %get-tuple-element.137.refs_6_), channel_id=1, source_target_pairs={{0,8},{1,9},{2,10},{3,11},{4,12},{5,13},{6,14},{7,15},{8,0},{9,1},... | collective-permute-start | bytes 552968 | tf_op jit(solution)/shard_map/ppermute | solution.py:412
  200.4 31.0 %collective-permute-start.21 = (bf16[48,1920]{1,0:T(8,128)(2,1)S(1)}, bf16[48,1920]{1,0:T(8,128)(2,1)S(1)}, u32[]{:S(2)}, u32[]{:S(2)}) collective-permute-start(bf16[48,1920]{1,0:T(8,128)(2,1)S(1)} %get-tuple-element.138.refs_5_), channel_id=1, source_target_pairs={{0,4},{1,5},{2,6},{3,7},{4,0},{5,1},{6,2},{7,3},{8,12},{9,13},{10,... | collective-permute-start | bytes 552968 | tf_op jit(solution)/shard_map/ppermute | solution.py:412
  207.6 26.2 %all-to-all-start = ((bf16[4,48,1152]{2,1,0:T(8,128)(2,1)}), bf16[4,48,1152]{2,1,0:T(8,128)(2,1)S(1)}, u32[]{:S(2)}, u32[]{:S(2)}) async-start(bf16[4,48,1152]{2,1,0:T(8,128)(2,1)} %fusion.refs_8_), calls=%async_computation | async-start | bytes 884736 | tf_op jit(solution)/shard_map/all_to_all | solution.py:417
  227.0 13.3 %collective-permute-start.20 = (bf16[48,3072]{1,0:T(8,128)(2,1)}, bf16[48,3072]{1,0:T(8,128)(2,1)S(1)}, u32[]{:S(2)}, u32[]{:S(2)}) collective-permute-start(bf16[48,3072]{1,0:T(8,128)(2,1)} %reduce-scatter.2.cloned.1.call-done.refs_1_), channel_id=1, source_target_pairs={{0,16},{16,0},{1,17},{17,1},{2,18},{18,2},{3,19},{19,3},{4,20},{20... | collective-permute-start | bytes 884744 | tf_op jit(solution)/shard_map/ppermute | solution.py:741
  231.5 8.8 %copy-start.23 = (bf16[48,1920]{1,0:T(8,128)(2,1)}, bf16[48,1920]{1,0:T(8,128)(2,1)S(1)}, u32[]{:S(2)}) copy-start(bf16[48,1920]{1,0:T(8,128)(2,1)S(1)} %fusion.3.refs_3_) | copy-start | bytes 552964
  231.5 8.8 %collective-permute-start.24 = (bf16[48,1920]{1,0:T(8,128)(2,1)S(1)}, bf16[48,1920]{1,0:T(8,128)(2,1)S(1)}, u32[]{:S(2)}, u32[]{:S(2)}) collective-permute-start(bf16[48,1920]{1,0:T(8,128)(2,1)S(1)} %fusion.3.refs_3_), channel_id=1, source_target_pairs={{0,16},{16,0},{1,17},{17,1},{2,18},{18,2},{3,19},{19,3},{4,20},{20... | collective-permute-start | bytes 552968 | tf_op jit(solution)/shard_map/ppermute | solution.py:741
  233.8 10.1 %copy-start.26 = (bf16[48,1152]{1,0:T(8,128)(2,1)}, bf16[48,1152]{1,0:T(8,128)(2,1)S(1)}, u32[]{:S(2)}) copy-start(bf16[48,1152]{1,0:T(8,128)(2,1)S(1)} %reduce_sum.12.refs_1_) | copy-start | bytes 331780
  233.9 10.1 %collective-permute-start.19 = (bf16[48,1152]{1,0:T(8,128)(2,1)S(1)}, bf16[48,1152]{1,0:T(8,128)(2,1)S(1)}, u32[]{:S(2)}, u32[]{:S(2)}) collective-permute-start(bf16[48,1152]{1,0:T(8,128)(2,1)S(1)} %reduce_sum.12.refs_1_), channel_id=1, source_target_pairs={{0,16},{16,0},{1,17},{17,1},{2,18},{18,2},{3,19},{19,3},{4,20},{20... | collective-permute-start | bytes 331784 | tf_op jit(solution)/shard_map/ppermute | solution.py:741
  (17 other events, 17.4 us)
Sparse Core Ops, SparseCore 0:
  12.2 96.6 all-gather.1
  130.9 94.9 reduce-scatter.1

commit v4 on v3

--- a/solution.py
+++ b/solution.py
@@ -94,6 +94,17 @@
         source = (near, far)[spot // 8]
         rows = pl.ds(pl.multiple_of(meta[17 + spot] * size, size), size)
         target[rows, :] = source[spot % 8 * size : (spot % 8 + 1) * size, :]
+
+
+def pack(output, up, down, packed):
+    rows, dim = output.shape
+    packed[:, :dim] = output[...]
+    for k in range(4):
+        at = (1 + 2 * k) * dim
+        for owner in range(dim // rows):
+            source = (4 * owner + k) * rows
+            packed[:, at + owner * rows : at + (owner + 1) * rows] = up[:, source : source + rows]
+        packed[:, at + dim : at + 2 * dim] = down[k * rows : (k + 1) * rows, :]
 
 
 def first_norm(meta, own, other, z):
@@ -476,13 +487,17 @@
 
     joint_own = lax.dynamic_index_in_dim(joint_weight.reshape(rows, 3, 2, group), place, 2, keepdims=False)
     joint_own = joint_own.reshape(rows, 3, 3, PAIR).transpose(0, 2, 1, 3).reshape(rows, 3 * group)
-    up_turned = up_weight.reshape(rows, parts, 4, rows).transpose(2, 0, 1, 3).reshape(4, rows, dim)
-    down_turned = down_weight.reshape(4, rows, dim)
-    hidden = [part[k] for k in range(4) for part in (up_turned, down_turned)]
+    packed = pl.pallas_call(
+        pack,
+        name="pack",
+        out_shape=shaped(rows, 9 * dim),
+        compiler_params=pltpu.CompilerParams(vmem_limit_bytes=LIMIT),
+        cost_estimate=cost(2),
+    )(output_weight, up_weight, down_weight)
 
     own = block_input[0]
     upstream = cotangent[0]
-    rest = lax.all_gather(jnp.concatenate([output_weight, *hidden], axis=1), "fsdp", axis=0, tiled=True)
+    rest = lax.all_gather(packed, "fsdp", axis=0, tiled=True)
     other = lax.ppermute(own, "seq", SWAP)
     both_gains = jnp.pad(jnp.stack([lead_gain, tail_gain], axis=1), ((0, 0), (0, PAIR - 2)))
     first = jnp.concatenate([joint_own, both_gains], axis=1)

time: 258 us -> 256 us (level)
  local copies, waits for them, and re-layouts: 11.9 us -> 7.35 us
  Pallas kernels: 120 us -> 123 us
    unnamed x84 -> x72, local copies, waits for them, and re-layouts: 8.2 us -> 6.52 us
where the time goes in v4:
time: 256 us; the launch traced here: 252 us
  Pallas kernels  123 us (48%)
  waiting for transfers between devices  63.8 us (25%)
  starting transfers between devices  31 us (12%)
  between operations  14.9 us (6%)
  other arithmetic  12.3 us (5%)
  local copies, waits for them, and re-layouts  7.35 us (3%)
    pallas_call x16, Pallas kernels, call(): pl.pallas_call(waiting(kernel, 1 + len(inputs), len(after)), name=name, g...  120 us
    ppermute x15, waiting for transfers between devices, flipped(): lax.ppermute(array, 'fsdp', [(spot, spot ^ bit) for spot in range(parts)])  37.5 us
    ppermute x15, starting transfers between devices, flipped(): lax.ppermute(array, 'fsdp', [(spot, spot ^ bit) for spot in range(parts)])  15.1 us
    all_gather x1, waiting for transfers between devices, body(): rest = lax.all_gather(packed, 'fsdp', axis=0, tiled=True)  10.7 us
    convert_element_type x11, other arithmetic, rounded_sum(): return total.astype(BF16)  9.49 us
    ppermute x1, waiting for transfers between devices, body(): o_came = lax.ppermute(o_other, 'seq', SWAP)  6.97 us
    unnamed x72, local copies, waits for them, and re-layouts  6.52 us
    ppermute x3, waiting for transfers between devices, body(): lax.ppermute(part, 'seq', SWAP)  5.41 us
  transfers between devices with their start and end apart: 28, of which 12 were waited for; matrix products, arithmetic and copies ran while one was open for 5% of the time, Pallas kernels for 38%

profile of v4, /device:TPU:0, one launch (start us, length us, event | category | flops | bytes accessed | tf_op | source)
XLA Modules:
  0.0 252.0 jit_solution(18373446319300027273)
XLA Ops:
  7.2 2.4 pack.1
  10.5 4.1 %collective-permute-start = (bf16[48,1280]{1,0:T(8,128)(2,1)S(1)}, bf16[48,1280]{1,0:T(8,128)(2,1)S(1)}, u32[]{:S(2)}, u32[]{:S(2)}) collective-permute-start(bf16[48,1280]{1,0:T(8,128)(2,1)S(1)} %pad_maximum_fusion.3), channel_id=1, source_target_pairs={{0,8},{1,9},{2,10},{3,11},{4,12},{5,13},{6,14},{7,15},{8,0},{9,1},... | collective-permute-start | bytes 368648 | tf_op jit(solution)/shard_map/ppermute | solution.py:423
  14.7 1.5 collective-permute-start.2
  16.2 4.4 %collective-permute-done = bf16[48,1280]{1,0:T(8,128)(2,1)S(1)} collective-permute-done((bf16[48,1280]{1,0:T(8,128)(2,1)S(1)}, bf16[48,1280]{1,0:T(8,128)(2,1)S(1)}, u32[]{:S(2)}, u32[]{:S(2)}) %collective-permute-start) | collective-permute-done | bytes 122912 | tf_op jit(solution)/shard_map/ppermute | solution.py:423
  21.4 17.1 %collective-permute-done.1 = bf16[96,1280]{1,0:T(8,128)(2,1)S(1)} collective-permute-done((bf16[96,1280]{1,0:T(8,128)(2,1)S(1)}, bf16[96,1280]{1,0:T(8,128)(2,1)S(1)}, u32[]{:S(2)}, u32[]{:S(2)}) %collective-permute-start.1) | collective-permute-done | bytes 245792 | tf_op jit(solution)/shard_map/ppermute | solution.py:423
  38.6 1.3 collective-permute-start.3
  39.9 7.6 %collective-permute-done.3 = bf16[192,1280]{1,0:T(8,128)(2,1)S(1)} collective-permute-done((bf16[192,1280]{1,0:T(8,128)(2,1)S(1)}, bf16[192,1280]{1,0:T(8,128)(2,1)S(1)}, u32[]{:S(2)}, u32[]{:S(2)}) %collective-permute-start.3) | collective-permute-done | bytes 491552 | tf_op jit(solution)/shard_map/ppermute | solution.py:423
  48.3 4.0 %first_norm.1.refs_1_ = f32[1024,768]{1,0:T(8,128)} custom-call(s32[33]{0:T(128)} %pad_add_fusion.refs_0_, bf16[512,768]{1,0:T(8,128)(2,1)} %bitcast.36, bf16[512,768]{1,0:T(8,128)(2,1)} %copy-done.17), custom_call_target="tpu_custom_call" | custom-call | flops 30000000 | bytes 90000 | tf_op jit(solution)/shard_map/first_norm/pallas_call | solution.py:56
  53.3 3.6 %first_scale.1 = (bf16[1024,768]{1,0:T(8,128)(2,1)}, bf16[16,768]{1,0:T(8,128)(2,1)}) custom-call(s32[33]{0:T(128)} %pad_add_fusion.refs_0_, f32[1024,768]{1,0:T(8,128)} %first_norm.1.refs_1_, bf16[384,1280]{1,0:T(8,128)(2,1)} %copy-done.1, bf16[384,1280]{1,0:T(8,128)(2,1)} %copy-done.2), custom_call_target="tpu_custom_call" | custom-call | flops 20000000 | bytes 60000 | tf_op jit(solution)/shard_map/first_scale/pallas_call | solution.py:56
  56.9 24.6 %attend.1 = (bf16[1024,1152]{1,0:T(8,128)(2,1)}, bf16[512,384]{1,0:T(8,128)(2,1)}, bf16[512,384]{1,0:T(8,128)(2,1)}, f32[3,8,1024]{2,1,0:T(8,128)}, bf16[768,1152]{1,0:T(8,128)(2,1)}) custom-call(s32[33]{0:T(128)} %pad_add_fusion.refs_0_, bf16[1024,768]{1,0:T(8,128)(2,1)} %get-tuple-element.72.refs_1_, bf16[384,1280]{1,0:T(8,128)(2,1)} %copy-done.1, ...), custom_call_target="tpu_custom_call" | custom-call | flops 220000000 | bytes 660000 | tf_op jit(solution)/shard_map/attend/pallas_call | solution.py:56
  81.5 1.4 collective-permute-start.5
  82.9 3.2 %turn.1.refs_3_.refs_7_ = bf16[768,1024]{1,0:T(8,128)(2,1)} custom-call(s32[33]{0:T(128)} %pad_add_fusion.refs_0_, bf16[1024,768]{1,0:T(8,128)(2,1)} %get-tuple-element.72.refs_1_, f32[3,8,1024]{2,1,0:T(8,128)} %get-tuple-element.75.refs_2_.refs_6_), custom_call_target="tpu_custom_call" | custom-call | flops 20000000 | bytes 60000 | tf_op jit(solution)/shard_map/turn/pallas_call | solution.py:56
  86.1 7.0 %collective-permute-done.5.refs_2_ = bf16[512,384]{1,0:T(8,128)(2,1)S(1)} collective-permute-done((bf16[512,384]{1,0:T(8,128)(2,1)}, bf16[512,384]{1,0:T(8,128)(2,1)S(1)}, u32[]{:S(2)}, u32[]{:S(2)}) %collective-permute-start.5) | collective-permute-done | bytes 393248 | tf_op jit(solution)/shard_map/ppermute | solution.py:553
  93.9 2.4 mix.1
  96.3 10.7 %all-gather.2.cloned.1.call-done.refs_4_.refs_5_.refs_6_.refs_3_ = bf16[768,6912]{1,0:T(8,128)(2,1)} async-done(((bf16[48,6912]{1,0:T(8,128)(2,1)}), bf16[768,6912]{1,0:T(8,128)(2,1)}) %all-gather.2.cloned.1.call-update) | async-done | bytes 10616848 | tf_op jit(solution)/shard_map/all_gather | solution.py:500
  107.0 21.9 %feed.1 = (bf16[512,3072]{1,0:T(8,128)(2,1)}, bf16[512,3072]{1,0:T(8,128)(2,1)}, bf16[768,3072]{1,0:T(8,128)(2,1)}, bf16[768,512]{1,0:T(8,128)(2,1)}, f32[512,76...) custom-call(s32[33]{0:T(128)} %pad_add_fusion.refs_0_, ...), custom_call_target="tpu_custom_call" | custom-call | flops 200000000 | bytes 600000 | tf_op jit(solution)/shard_map/feed/pallas_call | solution.py:56
  129.9 1.5 collective-permute-start.6
  131.4 8.1 %hidden_back.1 = (bf16[384,1536]{1,0:T(8,128)(2,1)}, bf16[384,1536]{1,0:T(8,128)(2,1)}, bf16[384,1536]{1,0:T(8,128)(2,1)}, bf16[384,1536]{1,0:T(8,128)(2,1)}, bf...) custom-call(s32[33]{0:T(128)} %pad_add_fusion.refs_0_, bf16[768,512]{1,0:T(8,128)(2,1)} %get-tuple-element.83.refs_1_, ...), custom_call_target="tpu_custom_call" | custom-call | flops 70000000 | bytes 210000 | tf_op jit(solution)/shard_map/hidden_back/pallas_call | solution.py:56
  139.5 1.7 collective-permute-done.6.refs_5_
  142.0 8.6 %attend_back.3 = (bf16[384,384]{1,0:T(8,128)(2,1)}, bf16[384,384]{1,0:T(8,128)(2,1)}, bf16[1024,384]{1,0:T(8,128)(2,1)}) custom-call(s32[33]{0:T(128)} %pad_add_fusion.refs_0_, bf16[1024,1152]{1,0:T(8,128)(2,1)} %get-tuple-element.80.refs_1_, bf16[512,384]{1,0:T(8,128)(2,1)} %get-tuple-element.73.refs_1_.refs_2_, ...), custom_call_target="tpu_custom_call" | custom-call | flops 100000000 | bytes 300000 | tf_op jit(solution)/shard_map/attend_back/pallas_call | solution.py:56
  150.6 1.4 add_convert_fusion.refs_10_
  152.0 1.5 collective-permute-start.11
  154.4 1.1 add_convert_fusion.8.refs_11_
  156.2 8.3 %attend_back.4 = (bf16[384,384]{1,0:T(8,128)(2,1)}, bf16[384,384]{1,0:T(8,128)(2,1)}, bf16[1024,384]{1,0:T(8,128)(2,1)}) custom-call(s32[33]{0:T(128)} %pad_add_fusion.refs_0_, bf16[1024,1152]{1,0:T(8,128)(2,1)} %get-tuple-element.80.refs_1_, bf16[512,384]{1,0:T(8,128)(2,1)} %get-tuple-element.73.refs_1_.refs_2_, ...), custom_call_target="tpu_custom_call" | custom-call | flops 100000000 | bytes 300000 | tf_op jit(solution)/shard_map/attend_back/pallas_call | solution.py:56
  164.5 9.6 %attend_back.5 = (bf16[384,1152]{1,0:T(8,128)(2,1)}, bf16[384,1152]{1,0:T(8,128)(2,1)}, bf16[1024,384]{1,0:T(8,128)(2,1)}) custom-call(s32[33]{0:T(128)} %pad_add_fusion.refs_0_, bf16[1024,1152]{1,0:T(8,128)(2,1)} %get-tuple-element.80.refs_1_, bf16[512,384]{1,0:T(8,128)(2,1)} %get-tuple-element.73.refs_1_.refs_2_, ...), custom_call_target="tpu_custom_call" | custom-call | flops 100000000 | bytes 300000 | tf_op jit(solution)/shard_map/attend_back/pallas_call | solution.py:56
  174.2 1.9 collective-permute-done.10
  179.4 1.1 add_convert_fusion.7.refs_5_
  181.1 1.2 add_convert_fusion.6.refs_6_
  183.1 1.4 collective-permute-start.17
  184.6 6.2 %token_back.1 = (bf16[512,768]{1,0:T(8,128)(2,1)}, f32[512,768]{1,0:T(8,128)}) custom-call(s32[33]{0:T(128)} %pad_add_fusion.refs_0_, bf16[1024,384]{1,0:T(8,128)(2,1)} %get-tuple-element.90.refs_12_.refs_1_, bf16[1024,384]{1,0:T(8,128)(2,1)} %get-tuple-element.102.refs_13_.refs_2_, bf16[1024,384]{1,0:T(8,128)(2,1)} %get-tuple-element.107.refs_3_, ...), custom_call_target="tpu_custom_call" | custom-call | flops 50000000 | bytes 150000 | tf_op jit(solution)/shard_map/token_back/pallas_call | solution.py:56
  190.7 1.5 collective-permute-done.15
  192.2 1.5 collective-permute-start.18
  194.7 1.1 add_convert_fusion.5
  195.8 1.2 add_convert_fusion.4
  198.4 3.3 %collective-permute-start.21 = (bf16[48,1920]{1,0:T(8,128)(2,1)S(1)}, bf16[48,1920]{1,0:T(8,128)(2,1)S(1)}, u32[]{:S(2)}, u32[]{:S(2)}) collective-permute-start(bf16[48,1920]{1,0:T(8,128)(2,1)S(1)} %get-tuple-element.134.refs_5_), channel_id=1, source_target_pairs={{0,4},{1,5},{2,6},{3,7},{4,0},{5,1},{6,2},{7,3},{8,12},{9,13},{10,... | collective-permute-start | bytes 552968 | tf_op jit(solution)/shard_map/ppermute | solution.py:423
  201.7 1.7 collective-permute-done.17
  203.4 1.9 fusion.refs_8_
  205.4 3.7 %all-to-all-start = ((bf16[4,48,1152]{2,1,0:T(8,128)(2,1)}), bf16[4,48,1152]{2,1,0:T(8,128)(2,1)S(1)}, u32[]{:S(2)}, u32[]{:S(2)}) async-start(bf16[4,48,1152]{2,1,0:T(8,128)(2,1)} %fusion.refs_8_), calls=%async_computation | async-start | bytes 884736 | tf_op jit(solution)/shard_map/all_to_all | solution.py:428
  209.1 5.3 %forward_out.2.refs_1_ = f32[512,768]{1,0:T(8,128)} custom-call(s32[33]{0:T(128)} %pad_add_fusion.refs_0_, f32[512,768]{1,0:T(8,128)} %get-tuple-element.78.refs_1_, bf16[512,3072]{1,0:T(8,128)(2,1)} %get-tuple-element.79.refs_2_, bf16[768,6912]{1,0:T(8,128)(2,1)} %all-gather.2.cloned.1.call-done.refs_4_.refs_5_.refs_6_.refs_3_, ...), custom_call_target="tpu_custom_call" | custom-call | flops 30000000 | bytes 90000 | tf_op jit(solution)/shard_map/forward_out/pallas_call | solution.py:56
  214.4 4.9 %forward_out.3.refs_6_ = bf16[512,768]{1,0:T(8,128)(2,1)} custom-call(s32[33]{0:T(128)} %pad_add_fusion.refs_0_, f32[512,768]{1,0:T(8,128)} %forward_out.2.refs_1_, bf16[512,3072]{1,0:T(8,128)(2,1)} %get-tuple-element.79.refs_2_, bf16[768,6912]{1,0:T(8,128)(2,1)} %all-gather.2.cloned.1.call-done.refs_4_.refs_5_.refs_6_.refs_3_), custom_call_target="tpu_custom_call" | custom-call | flops 30000000 | bytes 90000 | tf_op jit(solution)/shard_map/forward_out/pallas_call | solution.py:56
  220.2 4.6 %input_back.1.refs_7_ = f32[512,768]{1,0:T(8,128)} custom-call(s32[33]{0:T(128)} %pad_add_fusion.refs_0_, bf16[512,768]{1,0:T(8,128)(2,1)} %bitcast.38, f32[512,768]{1,0:T(8,128)} %get-tuple-element.116.refs_4_.refs_2_, bf16[512,768]{1,0:T(8,128)(2,1)} %copy-done.18, f32[512,768]{1,0:T(8,128)} %get-tuple-element.122.refs_4_, ...), custom_call_target="tpu_custom_call" | custom-call | flops 40000000 | bytes 120000 | tf_op jit(solution)/shard_map/input_back/pallas_call | solution.py:56
  224.8 1.5 collective-permute-start.20
  226.3 3.2 %collective-permute-done.22 = bf16[48,1920]{1,0:T(8,128)(2,1)S(1)} collective-permute-done((bf16[48,1920]{1,0:T(8,128)(2,1)S(1)}, bf16[48,1920]{1,0:T(8,128)(2,1)S(1)}, u32[]{:S(2)}, u32[]{:S(2)}) %collective-permute-start.22) | collective-permute-done | bytes 184352 | tf_op jit(solution)/shard_map/ppermute | solution.py:423
  230.4 1.4 all-to-all-done
  232.0 1.2 collective-permute-start.19
  233.2 5.4 %collective-permute-done.24.refs_4_ = bf16[48,1920]{1,0:T(8,128)(2,1)S(1)} collective-permute-done((bf16[48,1920]{1,0:T(8,128)(2,1)S(1)}, bf16[48,1920]{1,0:T(8,128)(2,1)S(1)}, u32[]{:S(2)}, u32[]{:S(2)}) %collective-permute-start.24) | collective-permute-done | bytes 184352 | tf_op jit(solution)/shard_map/ppermute | solution.py:756
  239.3 2.8 %feed_out.1 = (f32[48,3072]{1,0:T(8,128)}, f32[192,768]{1,0:T(8,128)}, f32[48,768]{1,0:T(8,128)}, f32[1,48]{1,0:T(1,128)}) custom-call(s32[33]{0:T(128)} %pad_add_fusion.refs_0_, bf16[48,3072]{1,0:T(8,128)(2,1)} %reduce-scatter.2.cloned.1.call-done.refs_1_, bf16[48,3072]{1,0:T(8,128)(2,1)} %copy-done.27, bf16[48,1920]{1,0:T(8,128)(2,1)} %copy-done.22, ...), custom_call_target="tpu_custom_call" | custom-call | flops 40000000 | bytes 120000 | tf_op jit(solution)/shard_map/feed_out/pallas_call | solution.py:56
  242.8 2.1 joint_out.1
  (132 shorter events, 17.9 us)
Async XLA Ops:
  7.2 2.6 %copy-start.33 = (bf16[48]{0:T(256)(128)(2,1)S(1)}, bf16[48]{0:T(256)(128)(2,1)}, u32[]{:S(2)}) copy-start(bf16[48]{0:T(256)(128)(2,1)} %param.9) | copy-start | bytes 292
  7.2 2.6 %copy-start.32 = (bf16[48]{0:T(256)(128)(2,1)S(1)}, bf16[48]{0:T(256)(128)(2,1)}, u32[]{:S(2)}) copy-start(bf16[48]{0:T(256)(128)(2,1)} %param.12) | copy-start | bytes 292
  7.2 2.7 %copy-start.16 = (bf16[48,2304]{1,0:T(8,128)(2,1)S(1)}, bf16[48,2304]{1,0:T(8,128)(2,1)}, u32[]{:S(2)}) copy-start(bf16[48,2304]{1,0:T(8,128)(2,1)} %refs_3_.1) | copy-start | bytes 663556
  7.2 99.8 %all-gather.2.cloned.1.call-start = ((), (), s32[]{:S(2)}) async-start(), calls=%async_computation.2 | async-start | bytes 11280384 | tf_op jit(solution)/shard_map/all_gather | solution.py:500
  9.7 5.0 %copy-start = (bf16[1,512,768]{2,1,0:T(8,128)(2,1)S(1)}, bf16[1,512,768]{2,1,0:T(8,128)(2,1)}, u32[]{:S(2)}) copy-start(bf16[1,512,768]{2,1,0:T(8,128)(2,1)} %param.8) | copy-start | bytes 2359300
  9.7 215.0 %reduce-scatter.2.cloned.1.call-start = ((), (), s32[]{:S(2)}) async-start(), calls=%async_computation.3 | async-start | bytes 5013504 | tf_op jit(solution)/shard_map/reduce_scatter | solution.py:620
  10.5 10.1 %collective-permute-start = (bf16[48,1280]{1,0:T(8,128)(2,1)S(1)}, bf16[48,1280]{1,0:T(8,128)(2,1)S(1)}, u32[]{:S(2)}, u32[]{:S(2)}) collective-permute-start(bf16[48,1280]{1,0:T(8,128)(2,1)S(1)} %pad_maximum_fusion.3), channel_id=1, source_target_pairs={{0,8},{1,9},{2,10},{3,11},{4,12},{5,13},{6,14},{7,15},{8,0},{9,1},... | collective-permute-start | bytes 368648 | tf_op jit(solution)/shard_map/ppermute | solution.py:423
  14.7 23.9 %collective-permute-start.2 = (bf16[512,768]{1,0:T(8,128)(2,1)S(1)}, bf16[512,768]{1,0:T(8,128)(2,1)S(1)}, u32[]{:S(2)}, u32[]{:S(2)}) collective-permute-start(bf16[512,768]{1,0:T(8,128)(2,1)S(1)} %bitcast.39), channel_id=1, source_target_pairs={{0,16},{16,0},{1,17},{17,1},{2,18},{18,2},{3,19},{19,3},{4,20},{20... | collective-permute-start | bytes 2359304 | tf_op jit(solution)/shard_map/ppermute | solution.py:501
  20.6 17.9 %collective-permute-start.1 = (bf16[96,1280]{1,0:T(8,128)(2,1)S(1)}, bf16[96,1280]{1,0:T(8,128)(2,1)S(1)}, u32[]{:S(2)}, u32[]{:S(2)}) collective-permute-start(bf16[96,1280]{1,0:T(8,128)(2,1)S(1)} %pad_maximum_fusion.2), channel_id=1, source_target_pairs={{0,4},{1,5},{2,6},{3,7},{4,0},{5,1},{6,2},{7,3},{8,12},{9,13},{10,... | collective-permute-start | bytes 737288 | tf_op jit(solution)/shard_map/ppermute | solution.py:423
  38.6 9.8 %copy-start.17 = (bf16[512,768]{1,0:T(8,128)(2,1)}, bf16[512,768]{1,0:T(8,128)(2,1)S(1)}, u32[]{:S(2)}) copy-start(bf16[512,768]{1,0:T(8,128)(2,1)S(1)} %collective-permute-done.2.refs_2_) | copy-start | bytes 2359300
  38.6 8.9 %collective-permute-start.3 = (bf16[192,1280]{1,0:T(8,128)(2,1)S(1)}, bf16[192,1280]{1,0:T(8,128)(2,1)S(1)}, u32[]{:S(2)}, u32[]{:S(2)}) collective-permute-start(bf16[192,1280]{1,0:T(8,128)(2,1)S(1)} %pad_maximum_fusion.1), channel_id=1, source_target_pairs={{0,2},{1,3},{2,0},{3,1},{4,6},{5,7},{6,4},{7,5},{8,10},{9,11},{10,... | collective-permute-start | bytes 1474568 | tf_op jit(solution)/shard_map/ppermute | solution.py:423
  47.5 4.8 %copy-start.1 = (bf16[384,1280]{1,0:T(8,128)(2,1)}, bf16[384,1280]{1,0:T(8,128)(2,1)S(1)}, u32[]{:S(2)}) copy-start(bf16[384,1280]{1,0:T(8,128)(2,1)S(1)} %constant_dynamic-update-slice_fusion.refs_2_) | copy-start | bytes 2949124
  47.5 4.8 %collective-permute-start.4 = (bf16[384,1280]{1,0:T(8,128)(2,1)S(1)}, bf16[384,1280]{1,0:T(8,128)(2,1)S(1)}, u32[]{:S(2)}, u32[]{:S(2)}) collective-permute-start(bf16[384,1280]{1,0:T(8,128)(2,1)S(1)} %constant_dynamic-update-slice_fusion.refs_2_), channel_id=1, source_target_pairs={{0,1},{1,0},{2,3},{3,2},{4,5},{5,4},{6,7},{7,6},{8,9},{9,8},{10,11... | collective-permute-start | bytes 2949128 | tf_op jit(solution)/shard_map/ppermute | solution.py:423
  81.5 11.6 %collective-permute-start.5 = (bf16[512,384]{1,0:T(8,128)(2,1)}, bf16[512,384]{1,0:T(8,128)(2,1)S(1)}, u32[]{:S(2)}, u32[]{:S(2)}) collective-permute-start(bf16[512,384]{1,0:T(8,128)(2,1)} %get-tuple-element.74.refs_3_), channel_id=1, source_target_pairs={{0,16},{16,0},{1,17},{17,1},{2,18},{18,2},{3,19},{19,3},{4,20},{20... | collective-permute-start | bytes 1179656 | tf_op jit(solution)/shard_map/ppermute | solution.py:553
  129.9 11.3 %collective-permute-start.6 = (bf16[512,384]{1,0:T(8,128)(2,1)S(1)}, bf16[512,384]{1,0:T(8,128)(2,1)S(1)}, u32[]{:S(2)}, u32[]{:S(2)}) collective-permute-start(bf16[512,384]{1,0:T(8,128)(2,1)S(1)} %copy-done.34), channel_id=1, source_target_pairs={{0,16},{16,0},{1,17},{17,1},{2,18},{18,2},{3,19},{19,3},{4,20},{20... | collective-permute-start | bytes 1179656 | tf_op jit(solution)/shard_map/ppermute | solution.py:600
  141.2 9.4 %collective-permute-start.8 = (bf16[384,1536]{1,0:T(8,128)(2,1)}, bf16[384,1536]{1,0:T(8,128)(2,1)}, u32[]{:S(2)}, u32[]{:S(2)}) collective-permute-start(bf16[384,1536]{1,0:T(8,128)(2,1)} %get-tuple-element.96), channel_id=1, source_target_pairs={{0,1},{1,0},{2,3},{3,2},{4,5},{5,4},{6,7},{7,6},{8,9},{9,8},{10,11... | collective-permute-start | bytes 3538952 | tf_op jit(solution)/shard_map/ppermute | solution.py:423
  141.2 9.4 %collective-permute-start.7 = (bf16[384,1536]{1,0:T(8,128)(2,1)}, bf16[384,1536]{1,0:T(8,128)(2,1)S(1)}, u32[]{:S(2)}, u32[]{:S(2)}) collective-permute-start(bf16[384,1536]{1,0:T(8,128)(2,1)} %get-tuple-element.92), channel_id=1, source_target_pairs={{0,1},{1,0},{2,3},{3,2},{4,5},{5,4},{6,7},{7,6},{8,9},{9,8},{10,11... | collective-permute-start | bytes 3538952 | tf_op jit(solution)/shard_map/ppermute | solution.py:423
  141.7 12.6 %collective-permute-start.9 = (bf16[384,768]{1,0:T(8,128)(2,1)}, bf16[384,768]{1,0:T(8,128)(2,1)}, u32[]{:S(2)}, u32[]{:S(2)}) collective-permute-start(bf16[384,768]{1,0:T(8,128)(2,1)} %get-tuple-element.100), channel_id=1, source_target_pairs={{0,1},{1,0},{2,3},{3,2},{4,5},{5,4},{6,7},{7,6},{8,9},{9,8},{10,11... | collective-permute-start | bytes 1769480 | tf_op jit(solution)/shard_map/ppermute | solution.py:423
  142.0 8.6 %copy-start.11 = (bf16[384,1536]{1,0:T(8,128)(2,1)S(1)}, bf16[384,1536]{1,0:T(8,128)(2,1)}, u32[]{:S(2)}) copy-start(bf16[384,1536]{1,0:T(8,128)(2,1)} %get-tuple-element.94) | copy-start | bytes 3538948
  150.6 2.9 %copy-start.10 = (bf16[384,1536]{1,0:T(8,128)(2,1)S(1)}, bf16[384,1536]{1,0:T(8,128)(2,1)}, u32[]{:S(2)}) copy-start(bf16[384,1536]{1,0:T(8,128)(2,1)} %get-tuple-element.87) | copy-start | bytes 3538948
  152.0 3.5 %copy-start.5 = (bf16[4,2,48,768]{3,2,1,0:T(8,128)(2,1)}, bf16[4,2,48,768]{3,2,1,0:T(8,128)(2,1)S(1)}, u32[]{:S(2)}) copy-start(bf16[4,2,48,768]{3,2,1,0:T(8,128)(2,1)S(1)} %add_convert_fusion.refs_10_) | copy-start | bytes 1769476
  152.0 22.2 %collective-permute-start.11 = (bf16[4,2,48,768]{3,2,1,0:T(8,128)(2,1)S(1)}, bf16[4,2,48,768]{3,2,1,0:T(8,128)(2,1)}, u32[]{:S(2)}, u32[]{:S(2)}) collective-permute-start(bf16[4,2,48,768]{3,2,1,0:T(8,128)(2,1)S(1)} %add_convert_fusion.refs_10_), channel_id=1, source_target_pairs={{0,16},{16,0},{1,17},{17,1},{2,18},{18,2},{3,19},{19,3},{4,20},{20... | collective-permute-start | bytes 1769480 | tf_op jit(solution)/shard_map/ppermute | solution.py:453
  153.6 22.5 %collective-permute-start.10 = (bf16[4,1,48,1536]{3,2,1,0:T(8,128)(2,1)S(1)}, bf16[4,1,48,1536]{3,2,1,0:T(8,128)(2,1)}, u32[]{:S(2)}, u32[]{:S(2)}) collective-permute-start(bf16[4,1,48,1536]{3,2,1,0:T(8,128)(2,1)S(1)} %add_convert_fusion.1.refs_9_), channel_id=1, source_target_pairs={{0,2},{1,3},{2,0},{3,1},{4,6},{5,7},{6,4},{7,5},{8,10},{9,11},{10,... | collective-permute-start | bytes 1769480 | tf_op jit(solution)/shard_map/ppermute | solution.py:423
  155.5 18.6 %collective-permute-start.12 = (bf16[4,2,48,384]{3,2,1,0:T(8,128)(2,1)S(1)}, bf16[4,2,48,384]{3,2,1,0:T(8,128)(2,1)S(1)}, u32[]{:S(2)}, u32[]{:S(2)}) collective-permute-start(bf16[4,2,48,384]{3,2,1,0:T(8,128)(2,1)S(1)} %add_convert_fusion.8.refs_11_), channel_id=1, source_target_pairs={{0,16},{16,0},{1,17},{17,1},{2,18},{18,2},{3,19},{19,3},{4,20},{20... | collective-permute-start | bytes 884744 | tf_op jit(solution)/shard_map/ppermute | solution.py:453
  176.1 6.9 %collective-permute-start.13 = (bf16[384,1152]{1,0:T(8,128)(2,1)}, bf16[384,1152]{1,0:T(8,128)(2,1)S(1)}, u32[]{:S(2)}, u32[]{:S(2)}) collective-permute-start(bf16[384,1152]{1,0:T(8,128)(2,1)} %get-tuple-element.113), channel_id=1, source_target_pairs={{0,1},{1,0},{2,3},{3,2},{4,5},{5,4},{6,7},{7,6},{8,9},{9,8},{10,11... | collective-permute-start | bytes 2654216 | tf_op jit(solution)/shard_map/ppermute | solution.py:423
  177.2 3.9 %copy-start.12 = (bf16[384,1536]{1,0:T(8,128)(2,1)S(1)}, bf16[384,1536]{1,0:T(8,128)(2,1)}, u32[]{:S(2)}) copy-start(bf16[384,1536]{1,0:T(8,128)(2,1)} %get-tuple-element.94) | copy-start | bytes 3538948
  178.3 3.9 %copy-start.23 = (bf16[4,1,48,384]{3,2,1,0:T(8,128)(2,1)}, bf16[4,1,48,384]{3,2,1,0:T(8,128)(2,1)S(1)}, u32[]{:S(2)}) copy-start(bf16[4,1,48,384]{3,2,1,0:T(8,128)(2,1)S(1)} %add_convert_fusion.10.refs_7_) | copy-start | bytes 442372
  178.3 4.7 %copy-start.13 = (bf16[384,1152]{1,0:T(8,128)(2,1)S(1)}, bf16[384,1152]{1,0:T(8,128)(2,1)}, u32[]{:S(2)}) copy-start(bf16[384,1152]{1,0:T(8,128)(2,1)} %get-tuple-element.112) | copy-start | bytes 2654212
  178.3 12.4 %collective-permute-start.16 = (bf16[4,1,48,384]{3,2,1,0:T(8,128)(2,1)S(1)}, bf16[4,1,48,384]{3,2,1,0:T(8,128)(2,1)S(1)}, u32[]{:S(2)}, u32[]{:S(2)}) collective-permute-start(bf16[4,1,48,384]{3,2,1,0:T(8,128)(2,1)S(1)} %add_convert_fusion.10.refs_7_), channel_id=1, source_target_pairs={{0,2},{1,3},{2,0},{3,1},{4,6},{5,7},{6,4},{7,5},{8,10},{9,11},{10,... | collective-permute-start | bytes 442376 | tf_op jit(solution)/shard_map/ppermute | solution.py:423
  180.4 2.7 %copy-start.8 = (bf16[4,1,48,768]{3,2,1,0:T(8,128)(2,1)}, bf16[4,1,48,768]{3,2,1,0:T(8,128)(2,1)S(1)}, u32[]{:S(2)}) copy-start(bf16[4,1,48,768]{3,2,1,0:T(8,128)(2,1)S(1)} %add_convert_fusion.7.refs_5_) | copy-start | bytes 884740
  180.4 11.8 %collective-permute-start.14 = (bf16[4,1,48,768]{3,2,1,0:T(8,128)(2,1)S(1)}, bf16[4,1,48,768]{3,2,1,0:T(8,128)(2,1)S(1)}, u32[]{:S(2)}, u32[]{:S(2)}) collective-permute-start(bf16[4,1,48,768]{3,2,1,0:T(8,128)(2,1)S(1)} %add_convert_fusion.7.refs_5_), channel_id=1, source_target_pairs={{0,16},{16,0},{1,17},{17,1},{2,18},{18,2},{3,19},{19,3},{4,20},{20... | collective-permute-start | bytes 884744 | tf_op jit(solution)/shard_map/ppermute | solution.py:453
  182.3 9.9 %collective-permute-start.15 = (bf16[4,1,48,768]{3,2,1,0:T(8,128)(2,1)S(1)}, bf16[4,1,48,768]{3,2,1,0:T(8,128)(2,1)S(1)}, u32[]{:S(2)}, u32[]{:S(2)}) collective-permute-start(bf16[4,1,48,768]{3,2,1,0:T(8,128)(2,1)S(1)} %add_convert_fusion.6.refs_6_), channel_id=1, source_target_pairs={{0,2},{1,3},{2,0},{3,1},{4,6},{5,7},{6,4},{7,5},{8,10},{9,11},{10,... | collective-permute-start | bytes 884744 | tf_op jit(solution)/shard_map/ppermute | solution.py:423
  183.0 7.7 %copy-start.14 = (bf16[384,1152]{1,0:T(8,128)(2,1)}, bf16[384,1152]{1,0:T(8,128)(2,1)S(1)}, u32[]{:S(2)}) copy-start(bf16[384,1152]{1,0:T(8,128)(2,1)S(1)} %collective-permute-done.13) | copy-start | bytes 2654212
  183.1 20.3 %collective-permute-start.17 = (bf16[4,1,48,1152]{3,2,0,1:T(8,128)(2,1)S(1)}, bf16[4,1,48,1152]{3,2,0,1:T(8,128)(2,1)}, u32[]{:S(2)}, u32[]{:S(2)}) collective-permute-start(bf16[4,1,48,1152]{3,2,0,1:T(8,128)(2,1)S(1)} %add_convert_fusion.3), channel_id=1, source_target_pairs={{0,2},{1,3},{2,0},{3,1},{4,6},{5,7},{6,4},{7,5},{8,10},{9,11},{10,... | collective-permute-start | bytes 1327112 | tf_op jit(solution)/shard_map/ppermute | solution.py:423
  192.2 27.1 %collective-permute-start.18 = (bf16[512,768]{1,0:T(8,128)(2,1)}, bf16[512,768]{1,0:T(8,128)(2,1)S(1)}, u32[]{:S(2)}, u32[]{:S(2)}) collective-permute-start(bf16[512,768]{1,0:T(8,128)(2,1)} %get-tuple-element.121), channel_id=1, source_target_pairs={{0,16},{16,0},{1,17},{17,1},{2,18},{18,2},{3,19},{19,3},{4,20},{20... | collective-permute-start | bytes 2359304 | tf_op jit(solution)/shard_map/ppermute | solution.py:697
  197.0 6.4 %copy-start.15 = (bf16[384,1152]{1,0:T(8,128)(2,1)S(1)}, bf16[384,1152]{1,0:T(8,128)(2,1)}, u32[]{:S(2)}) copy-start(bf16[384,1152]{1,0:T(8,128)(2,1)} %copy-done.14) | copy-start | bytes 2654212
  197.2 8.2 %copy-start.19 = (bf16[48,1920]{1,0:T(8,128)(2,1)}, bf16[48,1920]{1,0:T(8,128)(2,1)S(1)}, u32[]{:S(2)}) copy-start(bf16[48,1920]{1,0:T(8,128)(2,1)S(1)} %get-tuple-element.134.refs_5_) | copy-start | bytes 552964
  197.2 8.2 %copy-start.20 = (bf16[48,1920]{1,0:T(8,128)(2,1)}, bf16[48,1920]{1,0:T(8,128)(2,1)S(1)}, u32[]{:S(2)}) copy-start(bf16[48,1920]{1,0:T(8,128)(2,1)S(1)} %get-tuple-element.133.refs_6_) | copy-start | bytes 552964
  197.2 8.2 %copy-start.21 = (bf16[48,1920]{1,0:T(8,128)(2,1)}, bf16[48,1920]{1,0:T(8,128)(2,1)S(1)}, u32[]{:S(2)}) copy-start(bf16[48,1920]{1,0:T(8,128)(2,1)S(1)} %get-tuple-element.132.refs_7_) | copy-start | bytes 552964
  197.2 29.0 %collective-permute-start.23 = (bf16[48,1920]{1,0:T(8,128)(2,1)S(1)}, bf16[48,1920]{1,0:T(8,128)(2,1)S(1)}, u32[]{:S(2)}, u32[]{:S(2)}) collective-permute-start(bf16[48,1920]{1,0:T(8,128)(2,1)S(1)} %get-tuple-element.132.refs_7_), channel_id=1, source_target_pairs={{0,12},{1,13},{2,14},{3,15},{4,8},{5,9},{6,10},{7,11},{8,4},{9,5},... | collective-permute-start | bytes 552968 | tf_op jit(solution)/shard_map/ppermute | solution.py:423
  197.9 31.6 %collective-permute-start.22 = (bf16[48,1920]{1,0:T(8,128)(2,1)S(1)}, bf16[48,1920]{1,0:T(8,128)(2,1)S(1)}, u32[]{:S(2)}, u32[]{:S(2)}) collective-permute-start(bf16[48,1920]{1,0:T(8,128)(2,1)S(1)} %get-tuple-element.133.refs_6_), channel_id=1, source_target_pairs={{0,8},{1,9},{2,10},{3,11},{4,12},{5,13},{6,14},{7,15},{8,0},{9,1},... | collective-permute-start | bytes 552968 | tf_op jit(solution)/shard_map/ppermute | solution.py:423
  198.4 31.1 %collective-permute-start.21 = (bf16[48,1920]{1,0:T(8,128)(2,1)S(1)}, bf16[48,1920]{1,0:T(8,128)(2,1)S(1)}, u32[]{:S(2)}, u32[]{:S(2)}) collective-permute-start(bf16[48,1920]{1,0:T(8,128)(2,1)S(1)} %get-tuple-element.134.refs_5_), channel_id=1, source_target_pairs={{0,4},{1,5},{2,6},{3,7},{4,0},{5,1},{6,2},{7,3},{8,12},{9,13},{10,... | collective-permute-start | bytes 552968 | tf_op jit(solution)/shard_map/ppermute | solution.py:423
  205.4 26.5 %all-to-all-start = ((bf16[4,48,1152]{2,1,0:T(8,128)(2,1)}), bf16[4,48,1152]{2,1,0:T(8,128)(2,1)S(1)}, u32[]{:S(2)}, u32[]{:S(2)}) async-start(bf16[4,48,1152]{2,1,0:T(8,128)(2,1)} %fusion.refs_8_), calls=%async_computation | async-start | bytes 884736 | tf_op jit(solution)/shard_map/all_to_all | solution.py:428
  224.8 13.8 %collective-permute-start.20 = (bf16[48,3072]{1,0:T(8,128)(2,1)}, bf16[48,3072]{1,0:T(8,128)(2,1)S(1)}, u32[]{:S(2)}, u32[]{:S(2)}) collective-permute-start(bf16[48,3072]{1,0:T(8,128)(2,1)} %reduce-scatter.2.cloned.1.call-done.refs_1_), channel_id=1, source_target_pairs={{0,16},{16,0},{1,17},{17,1},{2,18},{18,2},{3,19},{19,3},{4,20},{20... | collective-permute-start | bytes 884744 | tf_op jit(solution)/shard_map/ppermute | solution.py:756
  229.6 9.0 %copy-start.22 = (bf16[48,1920]{1,0:T(8,128)(2,1)}, bf16[48,1920]{1,0:T(8,128)(2,1)S(1)}, u32[]{:S(2)}) copy-start(bf16[48,1920]{1,0:T(8,128)(2,1)S(1)} %fusion.3.refs_3_) | copy-start | bytes 552964
  229.6 8.9 %collective-permute-start.24 = (bf16[48,1920]{1,0:T(8,128)(2,1)S(1)}, bf16[48,1920]{1,0:T(8,128)(2,1)S(1)}, u32[]{:S(2)}, u32[]{:S(2)}) collective-permute-start(bf16[48,1920]{1,0:T(8,128)(2,1)S(1)} %fusion.3.refs_3_), channel_id=1, source_target_pairs={{0,16},{16,0},{1,17},{17,1},{2,18},{18,2},{3,19},{19,3},{4,20},{20... | collective-permute-start | bytes 552968 | tf_op jit(solution)/shard_map/ppermute | solution.py:756
  231.9 10.2 %copy-start.25 = (bf16[48,1152]{1,0:T(8,128)(2,1)}, bf16[48,1152]{1,0:T(8,128)(2,1)S(1)}, u32[]{:S(2)}) copy-start(bf16[48,1152]{1,0:T(8,128)(2,1)S(1)} %reduce_sum.12.refs_1_) | copy-start | bytes 331780
  232.0 10.2 %collective-permute-start.19 = (bf16[48,1152]{1,0:T(8,128)(2,1)S(1)}, bf16[48,1152]{1,0:T(8,128)(2,1)S(1)}, u32[]{:S(2)}, u32[]{:S(2)}) collective-permute-start(bf16[48,1152]{1,0:T(8,128)(2,1)S(1)} %reduce_sum.12.refs_1_), channel_id=1, source_target_pairs={{0,16},{16,0},{1,17},{17,1},{2,18},{18,2},{3,19},{19,3},{4,20},{20... | collective-permute-start | bytes 331784 | tf_op jit(solution)/shard_map/ppermute | solution.py:756
  (15 other events, 17.5 us)
Sparse Core Ops, SparseCore 0:
  10.3 96.6 all-gather.1
  129.1 95.0 reduce-scatter.1

commit v5 on v4

--- a/solution.py
+++ b/solution.py
@@ -696,19 +696,18 @@
     )
     other_part = lax.ppermute(sent, "seq", SWAP)
 
-    def forward_call(late, before, after):
-        at = 2 * late
+    def forward_call(before, after):
         return call(
             forward_out,
             "forward_out",
-            (shaped(half, dim) if late else total_f32,),
+            (shaped(half, dim),),
             meta,
             (before, active, rest),
             [pltpu.VMEM((half, dim), F32)],
             took=3,
             after=after,
-            grid=(2,),
-            specs=[tokens, column(half, dim, lambda k: at + k), column(dim, dim, lambda k: 2 + 2 * (at + k))],
+            grid=(4,),
+            specs=[tokens, column(half, dim), column(dim, dim, lambda k: 2 + 2 * k)],
             out_specs=[tokens],
         )
 
@@ -729,11 +728,10 @@
         joint_red.take(marks)
         joint_sum = rounded_sum(joint_red.terms).reshape(4, rows, -1)
         marks.append(joint_sum)
-    (out,) = forward_call(0, resid, marks)
+    (out,) = forward_call(resid, marks)
     marks = []
     if direct:
         joint_sum = exchanged(joint_sum, parts)
-    (out,) = forward_call(1, out, marks)
     marks = [out]
     (input_grad,) = call(
         input_back, "input_back", (total_f32,), meta, (own, own_part, other_part, dresid, gains), after=marks

time: 256 us -> 255 us (level)
  waiting for transfers between devices: 63.8 us -> 67.1 us
  Pallas kernels: 123 us -> 120 us
    pallas_call x16 -> x15, Pallas kernels: 120 us -> 118 us  [call(): pl.pallas_call(waiting(kernel, 1 + len(inputs), len(after)), name=name, g...]
  transfers between devices with their start and end apart: 28 -> 28, of which waited for: 12 -> 13; matrix products, arithmetic and copies ran while one was open for 5% -> 5% of each run, Pallas kernels for 38% -> 37%
where the time goes in v5:
time: 255 us; the launch traced here: 252 us
  Pallas kernels  120 us (47%)
  waiting for transfers between devices  67.1 us (26%)
  starting transfers between devices  29.7 us (12%)
  between operations  15 us (6%)
  other arithmetic  12.4 us (5%)
  local copies, waits for them, and re-layouts  7.32 us (3%)
    pallas_call x15, Pallas kernels, call(): pl.pallas_call(waiting(kernel, 1 + len(inputs), len(after)), name=name, g...  118 us
    ppermute x15, waiting for transfers between devices, flipped(): lax.ppermute(array, 'fsdp', [(spot, spot ^ bit) for spot in range(parts)])  39.4 us
    ppermute x15, starting transfers between devices, flipped(): lax.ppermute(array, 'fsdp', [(spot, spot ^ bit) for spot in range(parts)])  15 us
    all_gather x1, waiting for transfers between devices, body(): rest = lax.all_gather(packed, 'fsdp', axis=0, tiled=True)  10.7 us
    convert_element_type x11, other arithmetic, rounded_sum(): return total.astype(BF16)  9.53 us
    ppermute x1, waiting for transfers between devices, body(): o_came = lax.ppermute(o_other, 'seq', SWAP)  6.97 us
    unnamed x72, local copies, waits for them, and re-layouts  6.48 us
  transfers between devices with their start and end apart: 28, of which 13 were waited for; matrix products, arithmetic and copies ran while one was open for 5% of the time, Pallas kernels for 37%

profile of v5, /device:TPU:0, one launch (start us, length us, event | category | flops | bytes accessed | tf_op | source)
XLA Modules:
  0.0 251.8 jit_solution(7990493226461274671)
XLA Ops:
  7.2 2.4 pack.1
  10.5 4.1 %collective-permute-start = (bf16[48,1280]{1,0:T(8,128)(2,1)S(1)}, bf16[48,1280]{1,0:T(8,128)(2,1)S(1)}, u32[]{:S(2)}, u32[]{:S(2)}) collective-permute-start(bf16[48,1280]{1,0:T(8,128)(2,1)S(1)} %pad_maximum_fusion.3), channel_id=1, source_target_pairs={{0,8},{1,9},{2,10},{3,11},{4,12},{5,13},{6,14},{7,15},{8,0},{9,1},... | collective-permute-start | bytes 368648 | tf_op jit(solution)/shard_map/ppermute | solution.py:423
  14.7 1.5 collective-permute-start.2
  16.2 4.4 %collective-permute-done = bf16[48,1280]{1,0:T(8,128)(2,1)S(1)} collective-permute-done((bf16[48,1280]{1,0:T(8,128)(2,1)S(1)}, bf16[48,1280]{1,0:T(8,128)(2,1)S(1)}, u32[]{:S(2)}, u32[]{:S(2)}) %collective-permute-start) | collective-permute-done | bytes 122912 | tf_op jit(solution)/shard_map/ppermute | solution.py:423
  21.4 17.1 %collective-permute-done.1 = bf16[96,1280]{1,0:T(8,128)(2,1)S(1)} collective-permute-done((bf16[96,1280]{1,0:T(8,128)(2,1)S(1)}, bf16[96,1280]{1,0:T(8,128)(2,1)S(1)}, u32[]{:S(2)}, u32[]{:S(2)}) %collective-permute-start.1) | collective-permute-done | bytes 245792 | tf_op jit(solution)/shard_map/ppermute | solution.py:423
  38.6 1.3 collective-permute-start.3
  39.9 7.6 %collective-permute-done.3 = bf16[192,1280]{1,0:T(8,128)(2,1)S(1)} collective-permute-done((bf16[192,1280]{1,0:T(8,128)(2,1)S(1)}, bf16[192,1280]{1,0:T(8,128)(2,1)S(1)}, u32[]{:S(2)}, u32[]{:S(2)}) %collective-permute-start.3) | collective-permute-done | bytes 491552 | tf_op jit(solution)/shard_map/ppermute | solution.py:423
  48.3 4.0 %first_norm.1.refs_1_ = f32[1024,768]{1,0:T(8,128)} custom-call(s32[33]{0:T(128)} %pad_add_fusion.refs_0_, bf16[512,768]{1,0:T(8,128)(2,1)} %bitcast.36, bf16[512,768]{1,0:T(8,128)(2,1)} %copy-done.17), custom_call_target="tpu_custom_call" | custom-call | flops 30000000 | bytes 90000 | tf_op jit(solution)/shard_map/first_norm/pallas_call | solution.py:56
  53.3 3.6 %first_scale.1 = (bf16[1024,768]{1,0:T(8,128)(2,1)}, bf16[16,768]{1,0:T(8,128)(2,1)}) custom-call(s32[33]{0:T(128)} %pad_add_fusion.refs_0_, f32[1024,768]{1,0:T(8,128)} %first_norm.1.refs_1_, bf16[384,1280]{1,0:T(8,128)(2,1)} %copy-done.1, bf16[384,1280]{1,0:T(8,128)(2,1)} %copy-done.2), custom_call_target="tpu_custom_call" | custom-call | flops 20000000 | bytes 60000 | tf_op jit(solution)/shard_map/first_scale/pallas_call | solution.py:56
  56.9 24.6 %attend.1 = (bf16[1024,1152]{1,0:T(8,128)(2,1)}, bf16[512,384]{1,0:T(8,128)(2,1)}, bf16[512,384]{1,0:T(8,128)(2,1)}, f32[3,8,1024]{2,1,0:T(8,128)}, bf16[768,1152]{1,0:T(8,128)(2,1)}) custom-call(s32[33]{0:T(128)} %pad_add_fusion.refs_0_, bf16[1024,768]{1,0:T(8,128)(2,1)} %get-tuple-element.72.refs_1_, bf16[384,1280]{1,0:T(8,128)(2,1)} %copy-done.1, ...), custom_call_target="tpu_custom_call" | custom-call | flops 220000000 | bytes 660000 | tf_op jit(solution)/shard_map/attend/pallas_call | solution.py:56
  81.5 1.4 collective-permute-start.5
  82.9 3.2 %turn.1.refs_3_.refs_7_ = bf16[768,1024]{1,0:T(8,128)(2,1)} custom-call(s32[33]{0:T(128)} %pad_add_fusion.refs_0_, bf16[1024,768]{1,0:T(8,128)(2,1)} %get-tuple-element.72.refs_1_, f32[3,8,1024]{2,1,0:T(8,128)} %get-tuple-element.75.refs_2_.refs_6_), custom_call_target="tpu_custom_call" | custom-call | flops 20000000 | bytes 60000 | tf_op jit(solution)/shard_map/turn/pallas_call | solution.py:56
  86.1 7.0 %collective-permute-done.5.refs_2_ = bf16[512,384]{1,0:T(8,128)(2,1)S(1)} collective-permute-done((bf16[512,384]{1,0:T(8,128)(2,1)}, bf16[512,384]{1,0:T(8,128)(2,1)S(1)}, u32[]{:S(2)}, u32[]{:S(2)}) %collective-permute-start.5) | collective-permute-done | bytes 393248 | tf_op jit(solution)/shard_map/ppermute | solution.py:553
  93.8 2.5 mix.1
  96.3 10.7 %all-gather.2.cloned.1.call-done.refs_4_.refs_5_.refs_6_.refs_3_ = bf16[768,6912]{1,0:T(8,128)(2,1)} async-done(((bf16[48,6912]{1,0:T(8,128)(2,1)}), bf16[768,6912]{1,0:T(8,128)(2,1)}) %all-gather.2.cloned.1.call-update) | async-done | bytes 10616848 | tf_op jit(solution)/shard_map/all_gather | solution.py:500
  107.0 21.9 %feed.1 = (bf16[512,3072]{1,0:T(8,128)(2,1)}, bf16[512,3072]{1,0:T(8,128)(2,1)}, bf16[768,3072]{1,0:T(8,128)(2,1)}, bf16[768,512]{1,0:T(8,128)(2,1)}, f32[512,76...) custom-call(s32[33]{0:T(128)} %pad_add_fusion.refs_0_, ...), custom_call_target="tpu_custom_call" | custom-call | flops 200000000 | bytes 600000 | tf_op jit(solution)/shard_map/feed/pallas_call | solution.py:56
  129.9 1.5 collective-permute-start.6
  131.4 8.2 %hidden_back.1 = (bf16[384,1536]{1,0:T(8,128)(2,1)}, bf16[384,1536]{1,0:T(8,128)(2,1)}, bf16[384,1536]{1,0:T(8,128)(2,1)}, bf16[384,1536]{1,0:T(8,128)(2,1)}, bf...) custom-call(s32[33]{0:T(128)} %pad_add_fusion.refs_0_, bf16[768,512]{1,0:T(8,128)(2,1)} %get-tuple-element.83.refs_1_, ...), custom_call_target="tpu_custom_call" | custom-call | flops 70000000 | bytes 210000 | tf_op jit(solution)/shard_map/hidden_back/pallas_call | solution.py:56
  139.6 1.6 collective-permute-done.6.refs_5_
  142.0 8.6 %attend_back.3 = (bf16[384,384]{1,0:T(8,128)(2,1)}, bf16[384,384]{1,0:T(8,128)(2,1)}, bf16[1024,384]{1,0:T(8,128)(2,1)}) custom-call(s32[33]{0:T(128)} %pad_add_fusion.refs_0_, bf16[1024,1152]{1,0:T(8,128)(2,1)} %get-tuple-element.80.refs_1_, bf16[512,384]{1,0:T(8,128)(2,1)} %get-tuple-element.73.refs_1_.refs_2_, ...), custom_call_target="tpu_custom_call" | custom-call | flops 100000000 | bytes 300000 | tf_op jit(solution)/shard_map/attend_back/pallas_call | solution.py:56
  150.6 1.3 add_convert_fusion.refs_10_
  152.0 1.5 collective-permute-start.11
  154.3 1.1 add_convert_fusion.8.refs_11_
  156.2 8.3 %attend_back.4 = (bf16[384,384]{1,0:T(8,128)(2,1)}, bf16[384,384]{1,0:T(8,128)(2,1)}, bf16[1024,384]{1,0:T(8,128)(2,1)}) custom-call(s32[33]{0:T(128)} %pad_add_fusion.refs_0_, bf16[1024,1152]{1,0:T(8,128)(2,1)} %get-tuple-element.80.refs_1_, bf16[512,384]{1,0:T(8,128)(2,1)} %get-tuple-element.73.refs_1_.refs_2_, ...), custom_call_target="tpu_custom_call" | custom-call | flops 100000000 | bytes 300000 | tf_op jit(solution)/shard_map/attend_back/pallas_call | solution.py:56
  164.5 9.6 %attend_back.5 = (bf16[384,1152]{1,0:T(8,128)(2,1)}, bf16[384,1152]{1,0:T(8,128)(2,1)}, bf16[1024,384]{1,0:T(8,128)(2,1)}) custom-call(s32[33]{0:T(128)} %pad_add_fusion.refs_0_, bf16[1024,1152]{1,0:T(8,128)(2,1)} %get-tuple-element.80.refs_1_, bf16[512,384]{1,0:T(8,128)(2,1)} %get-tuple-element.73.refs_1_.refs_2_, ...), custom_call_target="tpu_custom_call" | custom-call | flops 100000000 | bytes 300000 | tf_op jit(solution)/shard_map/attend_back/pallas_call | solution.py:56
  174.2 2.2 collective-permute-done.10
  177.5 1.1 add_convert_fusion.10.refs_7_
  179.5 1.1 add_convert_fusion.7.refs_5_
  181.2 1.2 add_convert_fusion.6.refs_6_
  183.3 1.4 collective-permute-start.17
  184.6 6.2 %token_back.1 = (bf16[512,768]{1,0:T(8,128)(2,1)}, f32[512,768]{1,0:T(8,128)}) custom-call(s32[33]{0:T(128)} %pad_add_fusion.refs_0_, bf16[1024,384]{1,0:T(8,128)(2,1)} %get-tuple-element.90.refs_12_.refs_1_, bf16[1024,384]{1,0:T(8,128)(2,1)} %get-tuple-element.102.refs_13_.refs_2_, bf16[1024,384]{1,0:T(8,128)(2,1)} %get-tuple-element.107.refs_3_, ...), custom_call_target="tpu_custom_call" | custom-call | flops 50000000 | bytes 150000 | tf_op jit(solution)/shard_map/token_back/pallas_call | solution.py:56
  190.8 1.5 collective-permute-done.15
  192.3 1.6 collective-permute-start.18
  194.9 1.1 add_convert_fusion.5
  196.0 1.3 add_convert_fusion.4
  198.4 3.5 %collective-permute-start.21 = (bf16[48,1920]{1,0:T(8,128)(2,1)S(1)}, bf16[48,1920]{1,0:T(8,128)(2,1)S(1)}, u32[]{:S(2)}, u32[]{:S(2)}) collective-permute-start(bf16[48,1920]{1,0:T(8,128)(2,1)S(1)} %get-tuple-element.134.refs_5_), channel_id=1, source_target_pairs={{0,4},{1,5},{2,6},{3,7},{4,0},{5,1},{6,2},{7,3},{8,12},{9,13},{10,... | collective-permute-start | bytes 552968 | tf_op jit(solution)/shard_map/ppermute | solution.py:423
  201.9 1.8 collective-permute-done.17
  203.7 1.9 fusion.refs_8_
  205.7 3.5 %all-to-all-start = ((bf16[4,48,1152]{2,1,0:T(8,128)(2,1)}), bf16[4,48,1152]{2,1,0:T(8,128)(2,1)S(1)}, u32[]{:S(2)}, u32[]{:S(2)}) async-start(bf16[4,48,1152]{2,1,0:T(8,128)(2,1)} %fusion.refs_8_), calls=%async_computation | async-start | bytes 884736 | tf_op jit(solution)/shard_map/all_to_all | solution.py:428
  209.2 7.5 %forward_out.1.refs_6_ = bf16[512,768]{1,0:T(8,128)(2,1)} custom-call(s32[33]{0:T(128)} %pad_add_fusion.refs_0_, f32[512,768]{1,0:T(8,128)} %get-tuple-element.78.refs_1_, bf16[512,3072]{1,0:T(8,128)(2,1)} %get-tuple-element.79.refs_2_, bf16[768,6912]{1,0:T(8,128)(2,1)} %all-gather.2.cloned.1.call-done.refs_4_.refs_5_.refs_6_.refs_3_, ...), custom_call_target="tpu_custom_call" | custom-call | flops 30000000 | bytes 90000 | tf_op jit(solution)/shard_map/forward_out/pallas_call | solution.py:56
  217.6 4.5 %input_back.1.refs_7_ = f32[512,768]{1,0:T(8,128)} custom-call(s32[33]{0:T(128)} %pad_add_fusion.refs_0_, bf16[512,768]{1,0:T(8,128)(2,1)} %bitcast.38, f32[512,768]{1,0:T(8,128)} %get-tuple-element.116.refs_4_.refs_2_, bf16[512,768]{1,0:T(8,128)(2,1)} %copy-done.18, f32[512,768]{1,0:T(8,128)} %get-tuple-element.122.refs_4_, ...), custom_call_target="tpu_custom_call" | custom-call | flops 40000000 | bytes 120000 | tf_op jit(solution)/shard_map/input_back/pallas_call | solution.py:56
  222.1 2.0 reduce-scatter.2.cloned.1.call-done.refs_1_
  224.7 4.8 %collective-permute-done.22 = bf16[48,1920]{1,0:T(8,128)(2,1)S(1)} collective-permute-done((bf16[48,1920]{1,0:T(8,128)(2,1)S(1)}, bf16[48,1920]{1,0:T(8,128)(2,1)S(1)}, u32[]{:S(2)}, u32[]{:S(2)}) %collective-permute-start.22) | collective-permute-done | bytes 184352 | tf_op jit(solution)/shard_map/ppermute | solution.py:423
  230.5 1.4 all-to-all-done
  232.0 1.2 collective-permute-start.19
  233.2 5.0 %collective-permute-done.24.refs_4_ = bf16[48,1920]{1,0:T(8,128)(2,1)S(1)} collective-permute-done((bf16[48,1920]{1,0:T(8,128)(2,1)S(1)}, bf16[48,1920]{1,0:T(8,128)(2,1)S(1)}, u32[]{:S(2)}, u32[]{:S(2)}) %collective-permute-start.24) | collective-permute-done | bytes 184352 | tf_op jit(solution)/shard_map/ppermute | solution.py:754
  239.0 2.8 %feed_out.1 = (f32[48,3072]{1,0:T(8,128)}, f32[192,768]{1,0:T(8,128)}, f32[48,768]{1,0:T(8,128)}, f32[1,48]{1,0:T(1,128)}) custom-call(s32[33]{0:T(128)} %pad_add_fusion.refs_0_, bf16[48,3072]{1,0:T(8,128)(2,1)} %reduce-scatter.2.cloned.1.call-done.refs_1_, bf16[48,3072]{1,0:T(8,128)(2,1)} %copy-done.27, bf16[48,1920]{1,0:T(8,128)(2,1)} %copy-done.22, ...), custom_call_target="tpu_custom_call" | custom-call | flops 40000000 | bytes 120000 | tf_op jit(solution)/shard_map/feed_out/pallas_call | solution.py:56
  242.5 2.1 joint_out.1
  (131 shorter events, 17.0 us)
Async XLA Ops:
  7.2 2.6 %copy-start.33 = (bf16[48]{0:T(256)(128)(2,1)S(1)}, bf16[48]{0:T(256)(128)(2,1)}, u32[]{:S(2)}) copy-start(bf16[48]{0:T(256)(128)(2,1)} %param.9) | copy-start | bytes 292
  7.2 2.6 %copy-start.32 = (bf16[48]{0:T(256)(128)(2,1)S(1)}, bf16[48]{0:T(256)(128)(2,1)}, u32[]{:S(2)}) copy-start(bf16[48]{0:T(256)(128)(2,1)} %param.12) | copy-start | bytes 292
  7.2 2.7 %copy-start.16 = (bf16[48,2304]{1,0:T(8,128)(2,1)S(1)}, bf16[48,2304]{1,0:T(8,128)(2,1)}, u32[]{:S(2)}) copy-start(bf16[48,2304]{1,0:T(8,128)(2,1)} %refs_3_.1) | copy-start | bytes 663556
  7.2 99.8 %all-gather.2.cloned.1.call-start = ((), (), s32[]{:S(2)}) async-start(), calls=%async_computation.2 | async-start | bytes 11280384 | tf_op jit(solution)/shard_map/all_gather | solution.py:500
  9.7 5.0 %copy-start = (bf16[1,512,768]{2,1,0:T(8,128)(2,1)S(1)}, bf16[1,512,768]{2,1,0:T(8,128)(2,1)}, u32[]{:S(2)}) copy-start(bf16[1,512,768]{2,1,0:T(8,128)(2,1)} %param.8) | copy-start | bytes 2359300
  9.7 214.5 %reduce-scatter.2.cloned.1.call-start = ((), (), s32[]{:S(2)}) async-start(), calls=%async_computation.3 | async-start | bytes 5013504 | tf_op jit(solution)/shard_map/reduce_scatter | solution.py:620
  10.5 10.1 %collective-permute-start = (bf16[48,1280]{1,0:T(8,128)(2,1)S(1)}, bf16[48,1280]{1,0:T(8,128)(2,1)S(1)}, u32[]{:S(2)}, u32[]{:S(2)}) collective-permute-start(bf16[48,1280]{1,0:T(8,128)(2,1)S(1)} %pad_maximum_fusion.3), channel_id=1, source_target_pairs={{0,8},{1,9},{2,10},{3,11},{4,12},{5,13},{6,14},{7,15},{8,0},{9,1},... | collective-permute-start | bytes 368648 | tf_op jit(solution)/shard_map/ppermute | solution.py:423
  14.7 23.9 %collective-permute-start.2 = (bf16[512,768]{1,0:T(8,128)(2,1)S(1)}, bf16[512,768]{1,0:T(8,128)(2,1)S(1)}, u32[]{:S(2)}, u32[]{:S(2)}) collective-permute-start(bf16[512,768]{1,0:T(8,128)(2,1)S(1)} %bitcast.39), channel_id=1, source_target_pairs={{0,16},{16,0},{1,17},{17,1},{2,18},{18,2},{3,19},{19,3},{4,20},{20... | collective-permute-start | bytes 2359304 | tf_op jit(solution)/shard_map/ppermute | solution.py:501
  20.6 17.9 %collective-permute-start.1 = (bf16[96,1280]{1,0:T(8,128)(2,1)S(1)}, bf16[96,1280]{1,0:T(8,128)(2,1)S(1)}, u32[]{:S(2)}, u32[]{:S(2)}) collective-permute-start(bf16[96,1280]{1,0:T(8,128)(2,1)S(1)} %pad_maximum_fusion.2), channel_id=1, source_target_pairs={{0,4},{1,5},{2,6},{3,7},{4,0},{5,1},{6,2},{7,3},{8,12},{9,13},{10,... | collective-permute-start | bytes 737288 | tf_op jit(solution)/shard_map/ppermute | solution.py:423
  38.6 9.8 %copy-start.17 = (bf16[512,768]{1,0:T(8,128)(2,1)}, bf16[512,768]{1,0:T(8,128)(2,1)S(1)}, u32[]{:S(2)}) copy-start(bf16[512,768]{1,0:T(8,128)(2,1)S(1)} %collective-permute-done.2.refs_2_) | copy-start | bytes 2359300
  38.6 8.9 %collective-permute-start.3 = (bf16[192,1280]{1,0:T(8,128)(2,1)S(1)}, bf16[192,1280]{1,0:T(8,128)(2,1)S(1)}, u32[]{:S(2)}, u32[]{:S(2)}) collective-permute-start(bf16[192,1280]{1,0:T(8,128)(2,1)S(1)} %pad_maximum_fusion.1), channel_id=1, source_target_pairs={{0,2},{1,3},{2,0},{3,1},{4,6},{5,7},{6,4},{7,5},{8,10},{9,11},{10,... | collective-permute-start | bytes 1474568 | tf_op jit(solution)/shard_map/ppermute | solution.py:423
  47.5 4.8 %copy-start.1 = (bf16[384,1280]{1,0:T(8,128)(2,1)}, bf16[384,1280]{1,0:T(8,128)(2,1)S(1)}, u32[]{:S(2)}) copy-start(bf16[384,1280]{1,0:T(8,128)(2,1)S(1)} %constant_dynamic-update-slice_fusion.refs_2_) | copy-start | bytes 2949124
  47.5 4.8 %collective-permute-start.4 = (bf16[384,1280]{1,0:T(8,128)(2,1)S(1)}, bf16[384,1280]{1,0:T(8,128)(2,1)S(1)}, u32[]{:S(2)}, u32[]{:S(2)}) collective-permute-start(bf16[384,1280]{1,0:T(8,128)(2,1)S(1)} %constant_dynamic-update-slice_fusion.refs_2_), channel_id=1, source_target_pairs={{0,1},{1,0},{2,3},{3,2},{4,5},{5,4},{6,7},{7,6},{8,9},{9,8},{10,11... | collective-permute-start | bytes 2949128 | tf_op jit(solution)/shard_map/ppermute | solution.py:423
  81.5 11.6 %collective-permute-start.5 = (bf16[512,384]{1,0:T(8,128)(2,1)}, bf16[512,384]{1,0:T(8,128)(2,1)S(1)}, u32[]{:S(2)}, u32[]{:S(2)}) collective-permute-start(bf16[512,384]{1,0:T(8,128)(2,1)} %get-tuple-element.74.refs_3_), channel_id=1, source_target_pairs={{0,16},{16,0},{1,17},{17,1},{2,18},{18,2},{3,19},{19,3},{4,20},{20... | collective-permute-start | bytes 1179656 | tf_op jit(solution)/shard_map/ppermute | solution.py:553
  129.9 11.3 %collective-permute-start.6 = (bf16[512,384]{1,0:T(8,128)(2,1)S(1)}, bf16[512,384]{1,0:T(8,128)(2,1)S(1)}, u32[]{:S(2)}, u32[]{:S(2)}) collective-permute-start(bf16[512,384]{1,0:T(8,128)(2,1)S(1)} %copy-done.34), channel_id=1, source_target_pairs={{0,16},{16,0},{1,17},{17,1},{2,18},{18,2},{3,19},{19,3},{4,20},{20... | collective-permute-start | bytes 1179656 | tf_op jit(solution)/shard_map/ppermute | solution.py:600
  141.2 9.4 %collective-permute-start.8 = (bf16[384,1536]{1,0:T(8,128)(2,1)}, bf16[384,1536]{1,0:T(8,128)(2,1)}, u32[]{:S(2)}, u32[]{:S(2)}) collective-permute-start(bf16[384,1536]{1,0:T(8,128)(2,1)} %get-tuple-element.96), channel_id=1, source_target_pairs={{0,1},{1,0},{2,3},{3,2},{4,5},{5,4},{6,7},{7,6},{8,9},{9,8},{10,11... | collective-permute-start | bytes 3538952 | tf_op jit(solution)/shard_map/ppermute | solution.py:423
  141.2 9.4 %collective-permute-start.7 = (bf16[384,1536]{1,0:T(8,128)(2,1)}, bf16[384,1536]{1,0:T(8,128)(2,1)S(1)}, u32[]{:S(2)}, u32[]{:S(2)}) collective-permute-start(bf16[384,1536]{1,0:T(8,128)(2,1)} %get-tuple-element.92), channel_id=1, source_target_pairs={{0,1},{1,0},{2,3},{3,2},{4,5},{5,4},{6,7},{7,6},{8,9},{9,8},{10,11... | collective-permute-start | bytes 3538952 | tf_op jit(solution)/shard_map/ppermute | solution.py:423
  141.7 12.6 %collective-permute-start.9 = (bf16[384,768]{1,0:T(8,128)(2,1)}, bf16[384,768]{1,0:T(8,128)(2,1)}, u32[]{:S(2)}, u32[]{:S(2)}) collective-permute-start(bf16[384,768]{1,0:T(8,128)(2,1)} %get-tuple-element.100), channel_id=1, source_target_pairs={{0,1},{1,0},{2,3},{3,2},{4,5},{5,4},{6,7},{7,6},{8,9},{9,8},{10,11... | collective-permute-start | bytes 1769480 | tf_op jit(solution)/shard_map/ppermute | solution.py:423
  142.0 8.6 %copy-start.11 = (bf16[384,1536]{1,0:T(8,128)(2,1)S(1)}, bf16[384,1536]{1,0:T(8,128)(2,1)}, u32[]{:S(2)}) copy-start(bf16[384,1536]{1,0:T(8,128)(2,1)} %get-tuple-element.94) | copy-start | bytes 3538948
  150.6 2.9 %copy-start.10 = (bf16[384,1536]{1,0:T(8,128)(2,1)S(1)}, bf16[384,1536]{1,0:T(8,128)(2,1)}, u32[]{:S(2)}) copy-start(bf16[384,1536]{1,0:T(8,128)(2,1)} %get-tuple-element.87) | copy-start | bytes 3538948
  152.0 3.5 %copy-start.5 = (bf16[4,2,48,768]{3,2,1,0:T(8,128)(2,1)}, bf16[4,2,48,768]{3,2,1,0:T(8,128)(2,1)S(1)}, u32[]{:S(2)}) copy-start(bf16[4,2,48,768]{3,2,1,0:T(8,128)(2,1)S(1)} %add_convert_fusion.refs_10_) | copy-start | bytes 1769476
  152.0 22.2 %collective-permute-start.11 = (bf16[4,2,48,768]{3,2,1,0:T(8,128)(2,1)S(1)}, bf16[4,2,48,768]{3,2,1,0:T(8,128)(2,1)}, u32[]{:S(2)}, u32[]{:S(2)}) collective-permute-start(bf16[4,2,48,768]{3,2,1,0:T(8,128)(2,1)S(1)} %add_convert_fusion.refs_10_), channel_id=1, source_target_pairs={{0,16},{16,0},{1,17},{17,1},{2,18},{18,2},{3,19},{19,3},{4,20},{20... | collective-permute-start | bytes 1769480 | tf_op jit(solution)/shard_map/ppermute | solution.py:453
  153.6 22.7 %collective-permute-start.10 = (bf16[4,1,48,1536]{3,2,1,0:T(8,128)(2,1)S(1)}, bf16[4,1,48,1536]{3,2,1,0:T(8,128)(2,1)}, u32[]{:S(2)}, u32[]{:S(2)}) collective-permute-start(bf16[4,1,48,1536]{3,2,1,0:T(8,128)(2,1)S(1)} %add_convert_fusion.1.refs_9_), channel_id=1, source_target_pairs={{0,2},{1,3},{2,0},{3,1},{4,6},{5,7},{6,4},{7,5},{8,10},{9,11},{10,... | collective-permute-start | bytes 1769480 | tf_op jit(solution)/shard_map/ppermute | solution.py:423
  155.5 18.7 %collective-permute-start.12 = (bf16[4,2,48,384]{3,2,1,0:T(8,128)(2,1)S(1)}, bf16[4,2,48,384]{3,2,1,0:T(8,128)(2,1)S(1)}, u32[]{:S(2)}, u32[]{:S(2)}) collective-permute-start(bf16[4,2,48,384]{3,2,1,0:T(8,128)(2,1)S(1)} %add_convert_fusion.8.refs_11_), channel_id=1, source_target_pairs={{0,16},{16,0},{1,17},{17,1},{2,18},{18,2},{3,19},{19,3},{4,20},{20... | collective-permute-start | bytes 884744 | tf_op jit(solution)/shard_map/ppermute | solution.py:453
  176.3 6.8 %collective-permute-start.13 = (bf16[384,1152]{1,0:T(8,128)(2,1)}, bf16[384,1152]{1,0:T(8,128)(2,1)S(1)}, u32[]{:S(2)}, u32[]{:S(2)}) collective-permute-start(bf16[384,1152]{1,0:T(8,128)(2,1)} %get-tuple-element.113), channel_id=1, source_target_pairs={{0,1},{1,0},{2,3},{3,2},{4,5},{5,4},{6,7},{7,6},{8,9},{9,8},{10,11... | collective-permute-start | bytes 2654216 | tf_op jit(solution)/shard_map/ppermute | solution.py:423
  177.5 3.7 %copy-start.12 = (bf16[384,1536]{1,0:T(8,128)(2,1)S(1)}, bf16[384,1536]{1,0:T(8,128)(2,1)}, u32[]{:S(2)}) copy-start(bf16[384,1536]{1,0:T(8,128)(2,1)} %get-tuple-element.94) | copy-start | bytes 3538948
  178.6 3.8 %copy-start.23 = (bf16[4,1,48,384]{3,2,1,0:T(8,128)(2,1)}, bf16[4,1,48,384]{3,2,1,0:T(8,128)(2,1)S(1)}, u32[]{:S(2)}) copy-start(bf16[4,1,48,384]{3,2,1,0:T(8,128)(2,1)S(1)} %add_convert_fusion.10.refs_7_) | copy-start | bytes 442372
  178.6 4.6 %copy-start.13 = (bf16[384,1152]{1,0:T(8,128)(2,1)S(1)}, bf16[384,1152]{1,0:T(8,128)(2,1)}, u32[]{:S(2)}) copy-start(bf16[384,1152]{1,0:T(8,128)(2,1)} %get-tuple-element.112) | copy-start | bytes 2654212
  178.6 12.2 %collective-permute-start.16 = (bf16[4,1,48,384]{3,2,1,0:T(8,128)(2,1)S(1)}, bf16[4,1,48,384]{3,2,1,0:T(8,128)(2,1)S(1)}, u32[]{:S(2)}, u32[]{:S(2)}) collective-permute-start(bf16[4,1,48,384]{3,2,1,0:T(8,128)(2,1)S(1)} %add_convert_fusion.10.refs_7_), channel_id=1, source_target_pairs={{0,2},{1,3},{2,0},{3,1},{4,6},{5,7},{6,4},{7,5},{8,10},{9,11},{10,... | collective-permute-start | bytes 442376 | tf_op jit(solution)/shard_map/ppermute | solution.py:423
  180.6 2.6 %copy-start.8 = (bf16[4,1,48,768]{3,2,1,0:T(8,128)(2,1)}, bf16[4,1,48,768]{3,2,1,0:T(8,128)(2,1)S(1)}, u32[]{:S(2)}) copy-start(bf16[4,1,48,768]{3,2,1,0:T(8,128)(2,1)S(1)} %add_convert_fusion.7.refs_5_) | copy-start | bytes 884740
  180.6 11.7 %collective-permute-start.14 = (bf16[4,1,48,768]{3,2,1,0:T(8,128)(2,1)S(1)}, bf16[4,1,48,768]{3,2,1,0:T(8,128)(2,1)S(1)}, u32[]{:S(2)}, u32[]{:S(2)}) collective-permute-start(bf16[4,1,48,768]{3,2,1,0:T(8,128)(2,1)S(1)} %add_convert_fusion.7.refs_5_), channel_id=1, source_target_pairs={{0,16},{16,0},{1,17},{17,1},{2,18},{18,2},{3,19},{19,3},{4,20},{20... | collective-permute-start | bytes 884744 | tf_op jit(solution)/shard_map/ppermute | solution.py:453
  182.3 9.9 %collective-permute-start.15 = (bf16[4,1,48,768]{3,2,1,0:T(8,128)(2,1)S(1)}, bf16[4,1,48,768]{3,2,1,0:T(8,128)(2,1)S(1)}, u32[]{:S(2)}, u32[]{:S(2)}) collective-permute-start(bf16[4,1,48,768]{3,2,1,0:T(8,128)(2,1)S(1)} %add_convert_fusion.6.refs_6_), channel_id=1, source_target_pairs={{0,2},{1,3},{2,0},{3,1},{4,6},{5,7},{6,4},{7,5},{8,10},{9,11},{10,... | collective-permute-start | bytes 884744 | tf_op jit(solution)/shard_map/ppermute | solution.py:423
  183.1 7.7 %copy-start.14 = (bf16[384,1152]{1,0:T(8,128)(2,1)}, bf16[384,1152]{1,0:T(8,128)(2,1)S(1)}, u32[]{:S(2)}) copy-start(bf16[384,1152]{1,0:T(8,128)(2,1)S(1)} %collective-permute-done.13) | copy-start | bytes 2654212
  183.3 20.5 %collective-permute-start.17 = (bf16[4,1,48,1152]{3,2,0,1:T(8,128)(2,1)S(1)}, bf16[4,1,48,1152]{3,2,0,1:T(8,128)(2,1)}, u32[]{:S(2)}, u32[]{:S(2)}) collective-permute-start(bf16[4,1,48,1152]{3,2,0,1:T(8,128)(2,1)S(1)} %add_convert_fusion.3), channel_id=1, source_target_pairs={{0,2},{1,3},{2,0},{3,1},{4,6},{5,7},{6,4},{7,5},{8,10},{9,11},{10,... | collective-permute-start | bytes 1327112 | tf_op jit(solution)/shard_map/ppermute | solution.py:423
  192.3 24.4 %collective-permute-start.18 = (bf16[512,768]{1,0:T(8,128)(2,1)}, bf16[512,768]{1,0:T(8,128)(2,1)S(1)}, u32[]{:S(2)}, u32[]{:S(2)}) collective-permute-start(bf16[512,768]{1,0:T(8,128)(2,1)} %get-tuple-element.121), channel_id=1, source_target_pairs={{0,16},{16,0},{1,17},{17,1},{2,18},{18,2},{3,19},{19,3},{4,20},{20... | collective-permute-start | bytes 2359304 | tf_op jit(solution)/shard_map/ppermute | solution.py:697
  197.3 6.4 %copy-start.15 = (bf16[384,1152]{1,0:T(8,128)(2,1)S(1)}, bf16[384,1152]{1,0:T(8,128)(2,1)}, u32[]{:S(2)}) copy-start(bf16[384,1152]{1,0:T(8,128)(2,1)} %copy-done.14) | copy-start | bytes 2654212
  197.4 8.2 %copy-start.19 = (bf16[48,1920]{1,0:T(8,128)(2,1)}, bf16[48,1920]{1,0:T(8,128)(2,1)S(1)}, u32[]{:S(2)}) copy-start(bf16[48,1920]{1,0:T(8,128)(2,1)S(1)} %get-tuple-element.134.refs_5_) | copy-start | bytes 552964
  197.5 8.2 %copy-start.20 = (bf16[48,1920]{1,0:T(8,128)(2,1)}, bf16[48,1920]{1,0:T(8,128)(2,1)S(1)}, u32[]{:S(2)}) copy-start(bf16[48,1920]{1,0:T(8,128)(2,1)S(1)} %get-tuple-element.133.refs_6_) | copy-start | bytes 552964
  197.5 8.2 %copy-start.21 = (bf16[48,1920]{1,0:T(8,128)(2,1)}, bf16[48,1920]{1,0:T(8,128)(2,1)S(1)}, u32[]{:S(2)}) copy-start(bf16[48,1920]{1,0:T(8,128)(2,1)S(1)} %get-tuple-element.132.refs_7_) | copy-start | bytes 552964
  197.5 27.2 %collective-permute-start.23 = (bf16[48,1920]{1,0:T(8,128)(2,1)S(1)}, bf16[48,1920]{1,0:T(8,128)(2,1)S(1)}, u32[]{:S(2)}, u32[]{:S(2)}) collective-permute-start(bf16[48,1920]{1,0:T(8,128)(2,1)S(1)} %get-tuple-element.132.refs_7_), channel_id=1, source_target_pairs={{0,12},{1,13},{2,14},{3,15},{4,8},{5,9},{6,10},{7,11},{8,4},{9,5},... | collective-permute-start | bytes 552968 | tf_op jit(solution)/shard_map/ppermute | solution.py:423
  198.0 31.6 %collective-permute-start.22 = (bf16[48,1920]{1,0:T(8,128)(2,1)S(1)}, bf16[48,1920]{1,0:T(8,128)(2,1)S(1)}, u32[]{:S(2)}, u32[]{:S(2)}) collective-permute-start(bf16[48,1920]{1,0:T(8,128)(2,1)S(1)} %get-tuple-element.133.refs_6_), channel_id=1, source_target_pairs={{0,8},{1,9},{2,10},{3,11},{4,12},{5,13},{6,14},{7,15},{8,0},{9,1},... | collective-permute-start | bytes 552968 | tf_op jit(solution)/shard_map/ppermute | solution.py:423
  198.4 31.1 %collective-permute-start.21 = (bf16[48,1920]{1,0:T(8,128)(2,1)S(1)}, bf16[48,1920]{1,0:T(8,128)(2,1)S(1)}, u32[]{:S(2)}, u32[]{:S(2)}) collective-permute-start(bf16[48,1920]{1,0:T(8,128)(2,1)S(1)} %get-tuple-element.134.refs_5_), channel_id=1, source_target_pairs={{0,4},{1,5},{2,6},{3,7},{4,0},{5,1},{6,2},{7,3},{8,12},{9,13},{10,... | collective-permute-start | bytes 552968 | tf_op jit(solution)/shard_map/ppermute | solution.py:423
  205.7 26.2 %all-to-all-start = ((bf16[4,48,1152]{2,1,0:T(8,128)(2,1)}), bf16[4,48,1152]{2,1,0:T(8,128)(2,1)S(1)}, u32[]{:S(2)}, u32[]{:S(2)}) async-start(bf16[4,48,1152]{2,1,0:T(8,128)(2,1)} %fusion.refs_8_), calls=%async_computation | async-start | bytes 884736 | tf_op jit(solution)/shard_map/all_to_all | solution.py:428
  224.2 14.0 %collective-permute-start.20 = (bf16[48,3072]{1,0:T(8,128)(2,1)}, bf16[48,3072]{1,0:T(8,128)(2,1)S(1)}, u32[]{:S(2)}, u32[]{:S(2)}) collective-permute-start(bf16[48,3072]{1,0:T(8,128)(2,1)} %reduce-scatter.2.cloned.1.call-done.refs_1_), channel_id=1, source_target_pairs={{0,16},{16,0},{1,17},{17,1},{2,18},{18,2},{3,19},{19,3},{4,20},{20... | collective-permute-start | bytes 884744 | tf_op jit(solution)/shard_map/ppermute | solution.py:754
  229.7 8.6 %copy-start.22 = (bf16[48,1920]{1,0:T(8,128)(2,1)}, bf16[48,1920]{1,0:T(8,128)(2,1)S(1)}, u32[]{:S(2)}) copy-start(bf16[48,1920]{1,0:T(8,128)(2,1)S(1)} %fusion.3.refs_3_) | copy-start | bytes 552964
  229.7 8.5 %collective-permute-start.24 = (bf16[48,1920]{1,0:T(8,128)(2,1)S(1)}, bf16[48,1920]{1,0:T(8,128)(2,1)S(1)}, u32[]{:S(2)}, u32[]{:S(2)}) collective-permute-start(bf16[48,1920]{1,0:T(8,128)(2,1)S(1)} %fusion.3.refs_3_), channel_id=1, source_target_pairs={{0,16},{16,0},{1,17},{17,1},{2,18},{18,2},{3,19},{19,3},{4,20},{20... | collective-permute-start | bytes 552968 | tf_op jit(solution)/shard_map/ppermute | solution.py:754
  232.0 9.8 %copy-start.25 = (bf16[48,1152]{1,0:T(8,128)(2,1)}, bf16[48,1152]{1,0:T(8,128)(2,1)S(1)}, u32[]{:S(2)}) copy-start(bf16[48,1152]{1,0:T(8,128)(2,1)S(1)} %reduce_sum.12.refs_1_) | copy-start | bytes 331780
  232.0 9.8 %collective-permute-start.19 = (bf16[48,1152]{1,0:T(8,128)(2,1)S(1)}, bf16[48,1152]{1,0:T(8,128)(2,1)S(1)}, u32[]{:S(2)}, u32[]{:S(2)}) collective-permute-start(bf16[48,1152]{1,0:T(8,128)(2,1)S(1)} %reduce_sum.12.refs_1_), channel_id=1, source_target_pairs={{0,16},{16,0},{1,17},{17,1},{2,18},{18,2},{3,19},{19,3},{4,20},{20... | collective-permute-start | bytes 331784 | tf_op jit(solution)/shard_map/ppermute | solution.py:754
  (15 other events, 17.7 us)
Sparse Core Ops, SparseCore 0:
  10.3 96.6 all-gather.1
  129.1 95.0 reduce-scatter.1
